TPU v7x, 32 devices: a whole 2x2x4 slice. The times are simulated.
32 devices in a mesh: dp: 4 (over x, core), seq: 8 (over z, y).
Axes of the slice: x: 2, y: 2, z: 4, core: 2. Of those that a mesh axis runs over, the one named last changes fastest.
Arguments:
- hidden: bfloat16 [4, 1024, 1024], P('dp', 'seq'), may hold values from -6 to 6
- group_ids: int32 [4, 1024], P('dp'), may hold values from 0 to 4, as said below
- norm1_gain: bfloat16 [1024], replicated, may hold values from 0.25 to 1.75
- query_weight: bfloat16 [1024, 1024], replicated, may hold values from -0.09375 to 0.09375
- key_weight: bfloat16 [1024, 1024], replicated, may hold values from -0.09375 to 0.09375
- value_weight: bfloat16 [1024, 1024], replicated, may hold values from -0.1875 to 0.1875
- out_weight: bfloat16 [1024, 1024], replicated, may hold values from -0.75 to 0.75
- relative_bias: bfloat16 [32, 16], replicated, may hold values from -4 to 4
- norm2_gain: bfloat16 [1024], replicated, may hold values from 0.25 to 1.75
- gate_weight: bfloat16 [1024, 2816], replicated, may hold values from -0.1875 to 0.1875
- up_weight: bfloat16 [1024, 2816], replicated, may hold values from -0.1875 to 0.1875
- down_projection_weight: bfloat16 [2816, 1024], replicated, may hold values from -0.109375 to 0.109375
- out_grad: bfloat16 [4, 1024, 1024], P('dp', 'seq'), may hold values from -6 to 6
Outputs:
- block_out: bfloat16 [4, 1024, 1024], P('dp', 'seq')
- hidden_grad: float32 [4, 1024, 1024], P('dp', 'seq')
- norm1_gain_grad: float32 [1024], replicated
- query_weight_grad: float32 [1024, 1024], replicated
- key_weight_grad: float32 [1024, 1024], replicated
- value_weight_grad: float32 [1024, 1024], replicated
- out_weight_grad: float32 [1024, 1024], replicated
- relative_bias_grad: float32 [32, 16], replicated
- norm2_gain_grad: float32 [1024], replicated
- gate_weight_grad: float32 [1024, 2816], replicated
- up_weight_grad: float32 [1024, 2816], replicated
- down_weight_grad: float32 [2816, 1024], replicated
Inputs may be any that keep to these rules, and one draw needn't show every extreme that they name: `group_ids`: along each row the ids never fall and each of the values 0 to 4 forms one run; the run of id 2 begins within the row's first 128 positions and ends within its last 128 positions.
All inputs are finite; a program needn't handle non-finite values.
Results may differ from a plain program's by a relative error of at most 0.018.
Values may be sent and summed in bfloat16 or wider, within the bound.
A program may use at most 384 MiB of HBM per device.

v0:
```python
import jax
import jax.numpy as jnp
from jax import lax
from jax.sharding import PartitionSpec as P

EPSILON = 1e-06
MASKED = -1e30
THRESHOLDS = (12, 16, 23, 32, 46, 64, 91)


def bucket_of(relative):
    distance = jnp.abs(relative)
    bucket_level = jnp.full(relative.shape, 8, jnp.int32)
    for boundary in THRESHOLDS:
        bucket_level = bucket_level + (distance >= boundary).astype(jnp.int32)
    near_bucket = jnp.where(distance < 8, distance, bucket_level)
    return near_bucket + 16 * (relative > 0).astype(jnp.int32)


def rms_norm(vector, norm_gain):
    return (
        vector * lax.rsqrt(jnp.mean(vector * vector, axis=-1, keepdims=True) + EPSILON) * norm_gain
    )


def dot_rows(left_mat, right_mat):
    return lax.dot_general(
        left_mat, right_mat, (((0,), (0,)), ((), ())), preferred_element_type=jnp.float32
    )


def dot_cols(left_mat, right_mat):
    return lax.dot_general(
        left_mat, right_mat, (((1,), (1,)), ((), ())), preferred_element_type=jnp.float32
    )


def activate(gate_proj, up_proj):
    return jax.nn.gelu(gate_proj, approximate=True) * up_proj


def scores_of(
    query_part, key_part, query_places, key_places, query_groups, key_groups, bias_lookup
):
    bucket = bucket_of(key_places[None, :] - query_places[:, None])
    levels = jnp.arange(bias_lookup.shape[0], dtype=jnp.int32)
    one_hot_mask = (bucket[None] == levels[:, None, None]).astype(jnp.bfloat16)
    bias_patch_block = jnp.einsum(
        "ctf,cx->xtf", one_hot_mask, bias_lookup, preferred_element_type=jnp.float32
    )
    raw_scores = (
        jnp.einsum("qhd,khd->hqk", query_part, key_part, preferred_element_type=jnp.float32)
        + bias_patch_block
    )
    same_group = query_groups[:, None] == key_groups[None, :]
    return (one_hot_mask, jnp.where(same_group[None], raw_scores, MASKED))


def shards(
    hidden,
    group_ids,
    norm1_gain,
    query_weight,
    key_weight,
    value_weight,
    out_weight,
    relative_bias,
    norm2_gain,
    gate_weight,
    up_weight,
    down_projection_weight,
    out_grad,
):
    tok_rows = hidden.shape[1]
    head_count = relative_bias.shape[1]
    inner_width = query_weight.shape[1]
    head_depth = inner_width // head_count
    row_length = group_ids.shape[1]
    row_start = lax.axis_index("seq") * tok_rows
    key_block = min(1024, row_length)
    block_count = row_length // key_block
    row_groups = group_ids[0]
    own_groups = lax.dynamic_slice_in_dim(row_groups, row_start, tok_rows)
    own_places = row_start + jnp.arange(tok_rows, dtype=jnp.int32)
    all_places = jnp.arange(row_length, dtype=jnp.int32)

    def key_blocks(key_rows, value_rows):
        return (
            key_rows.reshape(block_count, key_block, head_count, head_depth),
            value_rows.reshape(block_count, key_block, head_count, head_depth),
            row_groups.reshape(block_count, key_block),
            all_places.reshape(block_count, key_block),
        )

    inputs = hidden[0].astype(jnp.float32)
    normed, norm_pull = jax.vjp(rms_norm, inputs, norm1_gain.astype(jnp.float32))
    normed_low = normed.astype(jnp.bfloat16)
    query_low = jnp.dot(normed_low, query_weight, preferred_element_type=jnp.float32).astype(
        jnp.bfloat16
    )
    key_low = jnp.dot(normed_low, key_weight, preferred_element_type=jnp.float32).astype(
        jnp.bfloat16
    )
    value_low = jnp.dot(normed_low, value_weight, preferred_element_type=jnp.float32).astype(
        jnp.bfloat16
    )
    key_all, value_all = (
        lax.all_gather(key_low, "seq", axis=0, tiled=True),
        lax.all_gather(value_low, "seq", axis=0, tiled=True),
    )
    query_heads = query_low.reshape(tok_rows, head_count, head_depth)

    def gather_stats(carry_state, scanned):
        running_max, running_sum = carry_state
        key_part, value_part, key_groups, key_places = scanned
        one_hot_mask, scores = scores_of(
            query_heads, key_part, own_places, key_places, own_groups, key_groups, relative_bias
        )
        new_max = jnp.maximum(running_max, jnp.max(scores, axis=-1))
        running_sum = running_sum * jnp.exp(running_max - new_max) + jnp.sum(
            jnp.exp(scores - new_max[..., None]), axis=-1
        )
        return ((new_max, running_sum), None)

    stats_init = (
        jnp.full((head_count, tok_rows), MASKED, jnp.float32),
        jnp.zeros((head_count, tok_rows), jnp.float32),
    )
    (running_max, running_sum), _ = lax.scan(
        gather_stats, stats_init, key_blocks(key_all, value_all)
    )
    log_total = running_max + jnp.log(running_sum)

    def gather_values(summed, scanned):
        key_part, value_part, key_groups, key_places = scanned
        one_hot_mask, scores = scores_of(
            query_heads, key_part, own_places, key_places, own_groups, key_groups, relative_bias
        )
        attention_low = jnp.exp(scores - log_total[..., None]).astype(jnp.bfloat16)
        return (
            summed
            + jnp.einsum(
                "hqk,khd->qhd", attention_low, value_part, preferred_element_type=jnp.float32
            ),
            None,
        )

    mixed, _ = lax.scan(
        gather_values,
        jnp.zeros((tok_rows, head_count, head_depth), jnp.float32),
        key_blocks(key_all, value_all),
    )
    mixed_low = mixed.reshape(tok_rows, inner_width).astype(jnp.bfloat16)
    middle = inputs + jnp.dot(mixed_low, out_weight, preferred_element_type=jnp.float32)
    normed_two, norm_two_pull = jax.vjp(rms_norm, middle, norm2_gain.astype(jnp.float32))
    normed_two_low = normed_two.astype(jnp.bfloat16)
    gate_proj = jnp.dot(normed_two_low, gate_weight, preferred_element_type=jnp.float32)
    up_proj = jnp.dot(normed_two_low, up_weight, preferred_element_type=jnp.float32)
    activated, act_pull = jax.vjp(activate, gate_proj, up_proj)
    activated_low = activated.astype(jnp.bfloat16)
    result = middle + jnp.dot(
        activated_low, down_projection_weight, preferred_element_type=jnp.float32
    )
    block_out = result.astype(jnp.bfloat16)[None]
    cotangent_low = out_grad[0]
    grad_down = dot_rows(activated_low, cotangent_low)
    act_grad = dot_cols(cotangent_low, down_projection_weight)
    gate_grad, up_grad = act_pull(act_grad)
    gate_grad_low = gate_grad.astype(jnp.bfloat16)
    up_grad_low = up_grad.astype(jnp.bfloat16)
    grad_gate = dot_rows(normed_two_low, gate_grad_low)
    grad_up = dot_rows(normed_two_low, up_grad_low)
    normed_two_grad = dot_cols(gate_grad_low, gate_weight) + dot_cols(up_grad_low, up_weight)
    middle_norm_grad, grad_gain_two = norm_two_pull(normed_two_grad)
    middle_grad = cotangent_low.astype(jnp.float32) + middle_norm_grad
    branch_grad_low = middle_grad.astype(jnp.bfloat16)
    grad_out = dot_rows(mixed_low, branch_grad_low)
    mixed_grad_low = (
        dot_cols(branch_grad_low, out_weight)
        .astype(jnp.bfloat16)
        .reshape(tok_rows, head_count, head_depth)
    )
    row_dots = jnp.einsum("qhd,qhd->hq", mixed_grad_low.astype(jnp.float32), mixed)
    key_back, value_back = (
        lax.all_gather(key_low, "seq", axis=0, tiled=True),
        lax.all_gather(value_low, "seq", axis=0, tiled=True),
    )
    grads_init = (
        jnp.zeros((tok_rows, head_count, head_depth), jnp.float32),
        jnp.zeros(relative_bias.shape, jnp.float32),
    )

    def backward_block(carry_state, scanned):
        query_grad, table_grad = carry_state
        key_part, value_part, key_groups, key_places = scanned
        one_hot_mask, scores = scores_of(
            query_heads, key_part, own_places, key_places, own_groups, key_groups, relative_bias
        )
        attention = jnp.exp(scores - log_total[..., None])
        grad_weights = jnp.einsum(
            "qhd,khd->hqk", mixed_grad_low, value_part, preferred_element_type=jnp.float32
        )
        score_gradients = (attention * (grad_weights - row_dots[..., None])).astype(jnp.bfloat16)
        query_grad = query_grad + jnp.einsum(
            "hqk,khd->qhd", score_gradients, key_part, preferred_element_type=jnp.float32
        )
        table_grad = table_grad + jnp.einsum(
            "oei,cei->oc", one_hot_mask, score_gradients, preferred_element_type=jnp.float32
        )
        key_grad = jnp.einsum(
            "hqk,qhd->khd", score_gradients, query_heads, preferred_element_type=jnp.float32
        )
        value_grad = jnp.einsum(
            "hqk,qhd->khd",
            attention.astype(jnp.bfloat16),
            mixed_grad_low,
            preferred_element_type=jnp.float32,
        )
        return ((query_grad, table_grad), (key_grad, value_grad))

    (query_grad, table_grad), (key_terms, value_terms) = lax.scan(
        backward_block, grads_init, key_blocks(key_back, value_back)
    )
    key_grad, value_grad = (
        lax.psum_scatter(
            key_terms.reshape(row_length, inner_width), "seq", scatter_dimension=0, tiled=True
        ),
        lax.psum_scatter(
            value_terms.reshape(row_length, inner_width), "seq", scatter_dimension=0, tiled=True
        ),
    )
    query_grad_low = query_grad.reshape(tok_rows, inner_width).astype(jnp.bfloat16)
    key_grad_low = key_grad.astype(jnp.bfloat16)
    value_grad_low = value_grad.astype(jnp.bfloat16)
    grad_query = dot_rows(normed_low, query_grad_low)
    grad_key = dot_rows(normed_low, key_grad_low)
    grad_value = dot_rows(normed_low, value_grad_low)
    normed_grad = (
        dot_cols(query_grad_low, query_weight)
        + dot_cols(key_grad_low, key_weight)
        + dot_cols(value_grad_low, value_weight)
    )
    input_norm_grad, grad_gain_one = norm_pull(normed_grad)
    hidden_grad = (middle_grad + input_norm_grad)[None]
    local_grads = (
        grad_gain_one,
        grad_query,
        grad_key,
        grad_value,
        grad_out,
        table_grad.reshape(-1),
        grad_gain_two,
        grad_gate,
        grad_up,
        grad_down,
    )
    shared = (
        lax.psum_scatter(local_grads[0], "seq", scatter_dimension=0, tiled=True),
        lax.psum_scatter(local_grads[1], "seq", scatter_dimension=0, tiled=True),
        lax.psum_scatter(local_grads[2], "seq", scatter_dimension=0, tiled=True),
        lax.psum_scatter(local_grads[3], "seq", scatter_dimension=0, tiled=True),
        lax.psum_scatter(local_grads[4], "seq", scatter_dimension=0, tiled=True),
        lax.psum_scatter(local_grads[5], "seq", scatter_dimension=0, tiled=True),
        lax.psum_scatter(local_grads[6], "seq", scatter_dimension=0, tiled=True),
        lax.psum_scatter(local_grads[7], "seq", scatter_dimension=0, tiled=True),
        lax.psum_scatter(local_grads[8], "seq", scatter_dimension=0, tiled=True),
        lax.psum_scatter(local_grads[9], "seq", scatter_dimension=0, tiled=True),
    )
    shared = (
        lax.psum(shared[0].astype(jnp.bfloat16), "dp").astype(jnp.float32),
        lax.psum(shared[1].astype(jnp.bfloat16), "dp").astype(jnp.float32),
        lax.psum(shared[2].astype(jnp.bfloat16), "dp").astype(jnp.float32),
        lax.psum(shared[3].astype(jnp.bfloat16), "dp").astype(jnp.float32),
        lax.psum(shared[4].astype(jnp.bfloat16), "dp").astype(jnp.float32),
        lax.psum(shared[5].astype(jnp.bfloat16), "dp").astype(jnp.float32),
        lax.psum(shared[6].astype(jnp.bfloat16), "dp").astype(jnp.float32),
        lax.psum(shared[7].astype(jnp.bfloat16), "dp").astype(jnp.float32),
        lax.psum(shared[8].astype(jnp.bfloat16), "dp").astype(jnp.float32),
        lax.psum(shared[9].astype(jnp.bfloat16), "dp").astype(jnp.float32),
    )
    summed = (
        lax.all_gather(shared[0].astype(jnp.bfloat16), "seq", axis=0, tiled=True).astype(
            jnp.float32
        ),
        lax.all_gather(shared[1].astype(jnp.bfloat16), "seq", axis=0, tiled=True).astype(
            jnp.float32
        ),
        lax.all_gather(shared[2].astype(jnp.bfloat16), "seq", axis=0, tiled=True).astype(
            jnp.float32
        ),
        lax.all_gather(shared[3].astype(jnp.bfloat16), "seq", axis=0, tiled=True).astype(
            jnp.float32
        ),
        lax.all_gather(shared[4].astype(jnp.bfloat16), "seq", axis=0, tiled=True).astype(
            jnp.float32
        ),
        lax.all_gather(shared[5].astype(jnp.bfloat16), "seq", axis=0, tiled=True).astype(
            jnp.float32
        ),
        lax.all_gather(shared[6].astype(jnp.bfloat16), "seq", axis=0, tiled=True).astype(
            jnp.float32
        ),
        lax.all_gather(shared[7].astype(jnp.bfloat16), "seq", axis=0, tiled=True).astype(
            jnp.float32
        ),
        lax.all_gather(shared[8].astype(jnp.bfloat16), "seq", axis=0, tiled=True).astype(
            jnp.float32
        ),
        lax.all_gather(shared[9].astype(jnp.bfloat16), "seq", axis=0, tiled=True).astype(
            jnp.float32
        ),
    )
    return (
        block_out,
        hidden_grad,
        summed[0],
        summed[1],
        summed[2],
        summed[3],
        summed[4],
        summed[5].reshape(relative_bias.shape),
        summed[6],
        summed[7],
        summed[8],
        summed[9],
    )


def solution(mesh):
    placed = (
        P("dp", "seq", None),
        P("dp", None),
        P(),
        P(),
        P(),
        P(),
        P(),
        P(),
        P(),
        P(),
        P(),
        P(),
        P("dp", "seq", None),
    )
    return jax.shard_map(
        shards,
        mesh=mesh,
        in_specs=placed,
        out_specs=(
            P("dp", "seq", None),
            P("dp", "seq", None),
            P(),
            P(),
            P(),
            P(),
            P(),
            P(),
            P(),
            P(),
            P(),
            P(),
        ),
        check_vma=False,
    )
```

profile of v0, /device:TPU:0, one launch (start us, length us, event | category | flops | bytes accessed | tf_op | source)
XLA Modules:
  0.0 1855.8 jit_solution(14557225213163011262)
XLA Ops:
  9.2 2.9 convolution_convert_fusion.2
  12.2 2.2 convolution_convert_fusion.4
  14.5 2.1 convolution_convert_fusion.3
  18.3 6.0 fusion.1
  24.3 40.0 %all-gather.14.cloned.1.call-done = bf16[1024,1024]{1,0:T(8,128)(2,1)} async-done(((bf16[128,1024]{1,0:T(8,128)(2,1)}), bf16[1024,1024]{1,0:T(8,128)(2,1)}) %all-gather.14.cloned.1.call-update) | async-done | bytes 2097168 | tf_op jit(solution)/shard_map/all_gather | solution.py:108
  64.3 3.9 copy.45
  68.2 10.3 fusion.76
  78.5 1.9 exponential_reduce_fusion
  80.5 1.4 copy-done.1
  81.9 32.8 %all-gather.12.cloned.1.call-done = bf16[1024,1024]{1,0:T(8,128)(2,1)} async-done(((bf16[128,1024]{1,0:T(8,128)(2,1)}), bf16[1024,1024]{1,0:T(8,128)(2,1)}) %all-gather.12.cloned.1.call-update) | async-done | bytes 2097168 | tf_op jit(solution)/shard_map/all_gather | solution.py:109
  114.8 4.4 copy.43
  119.2 6.6 bitcast_convert_fusion
  130.5 3.7 multiply_convert_fusion.1
  134.2 2.0 fusion.79
  136.2 2.1 multiply_reduce_fusion
  139.3 1.5 convolution_convert_fusion.1
  142.0 7.0 fusion.19
  150.4 6.3 multiply_convert_fusion
  156.8 3.1 fusion.81
  161.0 3.7 fusion.64
  164.8 4.4 convolution_convert_fusion
  169.2 2.8 fusion.50
  172.1 64.0 %reduce-scatter.12.cloned.1.call-done = f32[128,1024]{0,1:T(8,128)} async-done(((f32[1024,1024]{0,1:T(8,128)}), f32[128,1024]{0,1:T(8,128)}) %reduce-scatter.12.cloned.1.call-update) | async-done | bytes 524304 | tf_op jit(solution)/shard_map/reduce_scatter | solution.py:228
  236.1 3.9 fusion.58
  240.1 88.6 %reduce-scatter.10.cloned.1.call-done = f32[128,1024]{0,1:T(8,128)} async-done(((f32[1024,1024]{0,1:T(8,128)}), f32[128,1024]{0,1:T(8,128)}) %reduce-scatter.10.cloned.1.call-update) | async-done | bytes 524304 | tf_op jit(solution)/shard_map/reduce_scatter | solution.py:225
  328.7 3.9 fusion.61
  332.7 7.2 fusion.83
  340.0 7.2 fusion.82
  348.2 7.2 fusion.52
  355.7 64.2 %reduce-scatter.20.cloned.1.call-done = f32[128,1024]{1,0:T(8,128)} async-done(((f32[1024,1024]{1,0:T(8,128)}), f32[128,1024]{1,0:T(8,128)}) %reduce-scatter.20.cloned.1.call-update) | async-done | bytes 524304 | tf_op jit(solution)/shard_map/reduce_scatter | solution.py:262
  419.9 1.8 convert_element_type.307
  421.7 90.6 %reduce-scatter.14.cloned.1.call-done = f32[128,1024]{1,0:T(8,128)} async-done(((f32[1024,1024]{1,0:T(8,128)}), f32[128,1024]{1,0:T(8,128)}) %reduce-scatter.14.cloned.1.call-update) | async-done | bytes 524304 | tf_op jit(solution)/shard_map/reduce_scatter | solution.py:259
  512.2 1.8 convert_element_type.301
  514.0 90.3 %reduce-scatter.18.cloned.1.call-done = f32[128,1024]{1,0:T(8,128)} async-done(((f32[1024,1024]{1,0:T(8,128)}), f32[128,1024]{1,0:T(8,128)}) %reduce-scatter.18.cloned.1.call-update) | async-done | bytes 524304 | tf_op jit(solution)/shard_map/reduce_scatter | solution.py:261
  604.3 1.8 convert_element_type.305
  606.1 90.5 %reduce-scatter.16.cloned.1.call-done = f32[128,1024]{1,0:T(8,128)} async-done(((f32[1024,1024]{1,0:T(8,128)}), f32[128,1024]{1,0:T(8,128)}) %reduce-scatter.16.cloned.1.call-update) | async-done | bytes 524304 | tf_op jit(solution)/shard_map/reduce_scatter | solution.py:260
  696.6 1.8 convert_element_type.303
  698.4 194.9 %reduce-scatter.24.cloned.1.call-done = f32[128,2816]{1,0:T(8,128)} async-done(((f32[1024,2816]{1,0:T(8,128)}), f32[128,2816]{1,0:T(8,128)}) %reduce-scatter.24.cloned.1.call-update) | async-done | bytes 1441808 | tf_op jit(solution)/shard_map/reduce_scatter | solution.py:266
  893.3 2.3 convert_element_type.314
  895.6 193.5 %reduce-scatter.22.cloned.1.call-done = f32[128,2816]{1,0:T(8,128)} async-done(((f32[1024,2816]{1,0:T(8,128)}), f32[128,2816]{1,0:T(8,128)}) %reduce-scatter.22.cloned.1.call-update) | async-done | bytes 1441808 | tf_op jit(solution)/shard_map/reduce_scatter | solution.py:265
  1089.1 2.3 convert_element_type.312
  1091.4 193.7 %reduce-scatter.26.cloned.1.call-done = f32[352,1024]{1,0:T(8,128)} async-done(((f32[2816,1024]{1,0:T(8,128)}), f32[352,1024]{1,0:T(8,128)}) %reduce-scatter.26.cloned.1.call-update) | async-done | bytes 1441808 | tf_op jit(solution)/shard_map/reduce_scatter | solution.py:267
  1285.1 2.3 convert_element_type.316
  1287.5 70.6 %all-reduce.9.cloned.1.call-done = (bf16[128,1024]{1,0:T(8,128)(2,1)}, bf16[128,1024]{1,0:T(8,128)(2,1)}, bf16[128,1024]{1,0:T(8,128)(2,1)}, bf16[128,1024]{1,0:...) async-done(((bf16[128,1024]{1,0:T(8,128)(2,1)}, bf16[128,1024]{1,0:T(8,128)(2,1)}, bf16[128,1024]{1,0:T(8,128)(2,1)}, ...) | async-done | bytes 3211280 | tf_op jit(solution)/shard_map/psum | solution.py:271
  1364.4 8.0 fusion.16
  1372.5 2.4 fusion.80
  1374.9 4.6 fusion.15
  1381.4 37.6 %all-reduce.4 = (bf16[512]{0:T(512)(128)(2,1)S(1)}, bf16[1024]{0:T(1024)(128)(2,1)S(1)}, bf16[1024]{0:T(1024)(128)(2,1)S(1)}) all-reduce(f32[512]{0:T(512)S(1)} %reshape.217, f32[1024]{0:T(1024)S(1)} %get-tuple-element.149, f32[1024]{0:T(1024)S(1)} %get-tuple-element.131), channel_id=9, replica_groups=mesh['dp'=4,'seq'=8] {'seq'}, use_global_device_ids=true, to_apply=%region_19.20.clone | all-reduce | flops 2560 | bytes 15360
  1419.3 6.0 all-reduce.5
  1425.3 16.2 all-gather
  1442.1 18.4 all-gather.1
  1461.3 17.5 all-reduce
  1480.6 4.1 convert_element_type.308
  1484.6 4.1 convert_element_type.306
  1488.7 22.4 %all-gather.18.cloned.1.call-done = bf16[1024,1024]{1,0:T(8,128)(2,1)} async-done(((bf16[128,1024]{1,0:T(8,128)(2,1)}), bf16[1024,1024]{1,0:T(8,128)(2,1)}) %all-gather.18.cloned.1.call-update) | async-done | bytes 2097168 | tf_op jit(solution)/shard_map/all_gather | solution.py:288
  1511.1 4.1 convert_element_type.304
  1515.1 45.9 %all-gather.16.cloned.1.call-done = bf16[1024,1024]{1,0:T(8,128)(2,1)} async-done(((bf16[128,1024]{1,0:T(8,128)(2,1)}), bf16[1024,1024]{1,0:T(8,128)(2,1)}) %all-gather.16.cloned.1.call-update) | async-done | bytes 2097168 | tf_op jit(solution)/shard_map/all_gather | solution.py:285
  1561.1 4.1 convert_element_type.302
  1565.2 89.4 %all-gather.28.cloned.1.call-done = bf16[2816,1024]{1,0:T(8,128)(2,1)} async-done(((bf16[352,1024]{1,0:T(8,128)(2,1)}), bf16[2816,1024]{1,0:T(8,128)(2,1)}) %all-gather.28.cloned.1.call-update) | async-done | bytes 5767184 | tf_op jit(solution)/shard_map/all_gather | solution.py:309
  1654.5 8.5 convert_element_type.317
  1663.0 84.7 %all-gather.26.cloned.1.call-done = bf16[1024,2816]{1,0:T(8,128)(2,1)} async-done(((bf16[128,2816]{1,0:T(8,128)(2,1)}), bf16[1024,2816]{1,0:T(8,128)(2,1)}) %all-gather.26.cloned.1.call-update) | async-done | bytes 5767184 | tf_op jit(solution)/shard_map/all_gather | solution.py:306
  1747.6 7.9 convert_element_type.315
  1755.6 85.3 %all-gather.24.cloned.1.call-done = bf16[1024,2816]{1,0:T(8,128)(2,1)} async-done(((bf16[128,2816]{1,0:T(8,128)(2,1)}), bf16[1024,2816]{1,0:T(8,128)(2,1)}) %all-gather.24.cloned.1.call-update) | async-done | bytes 5767184 | tf_op jit(solution)/shard_map/all_gather | solution.py:303
  1840.9 7.9 convert_element_type.313
  (135 shorter events, 24.0 us)
Async XLA Ops:
  7.2 5.0 copy-start
  7.2 7.3 copy-start.3
  7.2 7.2 copy-start.21
  7.2 57.1 %all-gather.14.cloned.1.call-start = ((), (), s32[]{:S(2)}) async-start(), calls=%async_computation.10 | async-start | bytes 2359296 | tf_op jit(solution)/shard_map/all_gather | solution.py:108
  9.2 7.5 copy-start.20
  9.2 9.1 copy-start.19
  12.1 102.6 %all-gather.12.cloned.1.call-start = ((), (), s32[]{:S(2)}) async-start(), calls=%async_computation.9 | async-start | bytes 2359296 | tf_op jit(solution)/shard_map/all_gather | solution.py:109
  14.4 221.8 %reduce-scatter.12.cloned.1.call-start = ((), (), s32[]{:S(2)}) async-start(), calls=%async_computation.12 | async-start | bytes 4718592 | tf_op jit(solution)/shard_map/reduce_scatter | solution.py:228
  16.7 51.5 %copy-start.10 = (bf16[128,1024]{0,1:T(8,128)(2,1)}, bf16[128,1024]{0,1:T(8,128)(2,1)S(1)}, u32[]{:S(2)}) copy-start(bf16[128,1024]{0,1:T(8,128)(2,1)S(1)} %copy.44) | copy-start | bytes 786436
  17.5 0.8 copy-start.16
  78.5 3.4 copy-start.1
  119.2 7.5 slice-start.2
  119.2 6.7 copy-start.7
  119.2 7.5 slice-start.3
  125.8 0.7 copy-start.12
  125.8 2.3 slice-start
  126.7 2.1 slice-start.1
  126.7 3.4 slice-start.4
  128.8 1.7 slice-start.5
  128.8 1.7 copy-start.17
  134.2 4.1 copy-start.8
  134.2 4.1 copy-start.9
  138.5 0.8 copy-start.4
  149.1 179.6 %reduce-scatter.10.cloned.1.call-start = ((), (), s32[]{:S(2)}) async-start(), calls=%async_computation.11 | async-start | bytes 4718592 | tf_op jit(solution)/shard_map/reduce_scatter | solution.py:225
  150.4 6.4 copy-start.11
  156.8 3.3 copy-start.2
  160.1 1.0 copy-start.13
  160.1 259.8 %reduce-scatter.20.cloned.1.call-start = ((), (), s32[]{:S(2)}) async-start(), calls=%async_computation.19 | async-start | bytes 4718592 | tf_op jit(solution)/shard_map/reduce_scatter | solution.py:262
  164.7 347.5 %reduce-scatter.14.cloned.1.call-start = ((), (), s32[]{:S(2)}) async-start(), calls=%async_computation.13 | async-start | bytes 4718592 | tf_op jit(solution)/shard_map/reduce_scatter | solution.py:259
  172.1 432.2 %reduce-scatter.18.cloned.1.call-start = ((), (), s32[]{:S(2)}) async-start(), calls=%async_computation.17 | async-start | bytes 4718592 | tf_op jit(solution)/shard_map/reduce_scatter | solution.py:261
  240.0 456.6 %reduce-scatter.16.cloned.1.call-start = ((), (), s32[]{:S(2)}) async-start(), calls=%async_computation.15 | async-start | bytes 4718592 | tf_op jit(solution)/shard_map/reduce_scatter | solution.py:260
  332.6 560.7 %reduce-scatter.24.cloned.1.call-start = ((), (), s32[]{:S(2)}) async-start(), calls=%async_computation.23 | async-start | bytes 12976128 | tf_op jit(solution)/shard_map/reduce_scatter | solution.py:266
  339.9 749.2 %reduce-scatter.22.cloned.1.call-start = ((), (), s32[]{:S(2)}) async-start(), calls=%async_computation.21 | async-start | bytes 12976128 | tf_op jit(solution)/shard_map/reduce_scatter | solution.py:265
  347.2 1.0 copy-start.18
  347.2 937.9 %reduce-scatter.26.cloned.1.call-start = ((), (), s32[]{:S(2)}) async-start(), calls=%async_computation.25 | async-start | bytes 12976128 | tf_op jit(solution)/shard_map/reduce_scatter | solution.py:267
  355.4 1002.8 %all-reduce.9.cloned.1.call-start = ((), (), s32[]{:S(2)}) async-start(), calls=%async_computation.27 | async-start | bytes 6422528 | tf_op jit(solution)/shard_map/psum | solution.py:271
  1091.4 270.4 %copy-start.22 = (u32[32]{0:T(128)S(1)}, u32[32]{0:T(128)}, u32[]{:S(2)}) copy-start(u32[32]{0:T(128)} %constant.145) | copy-start | bytes 388
  1287.5 193.1 %all-gather.22.cloned.1.call-start = ((), (), s32[]{:S(2)}) async-start(), calls=%async_computation.20 | async-start | bytes 2359296 | tf_op jit(solution)/shard_map/all_gather | solution.py:294
  1358.2 126.4 %all-gather.20.cloned.1.call-start = ((), (), s32[]{:S(2)}) async-start(), calls=%async_computation.18 | async-start | bytes 2359296 | tf_op jit(solution)/shard_map/all_gather | solution.py:291
  1358.8 152.3 %all-gather.18.cloned.1.call-start = ((), (), s32[]{:S(2)}) async-start(), calls=%async_computation.16 | async-start | bytes 2359296 | tf_op jit(solution)/shard_map/all_gather | solution.py:288
  1359.3 201.7 %all-gather.16.cloned.1.call-start = ((), (), s32[]{:S(2)}) async-start(), calls=%async_computation.14 | async-start | bytes 2359296 | tf_op jit(solution)/shard_map/all_gather | solution.py:285
  1359.9 294.6 %all-gather.28.cloned.1.call-start = ((), (), s32[]{:S(2)}) async-start(), calls=%async_computation.26 | async-start | bytes 6488064 | tf_op jit(solution)/shard_map/all_gather | solution.py:309
  1360.5 387.1 %all-gather.26.cloned.1.call-start = ((), (), s32[]{:S(2)}) async-start(), calls=%async_computation.24 | async-start | bytes 6488064 | tf_op jit(solution)/shard_map/all_gather | solution.py:306
  1361.1 479.8 %all-gather.24.cloned.1.call-start = ((), (), s32[]{:S(2)}) async-start(), calls=%async_computation.22 | async-start | bytes 6488064 | tf_op jit(solution)/shard_map/all_gather | solution.py:303
  1374.9 4.7 copy-start.6
  1374.9 4.7 copy-start.15
  1374.9 5.5 copy-start.14
  1379.6 100.0 %copy-start.5 = (f32[128,1024]{1,0:T(8,128)S(1)}, f32[128,1024]{1,0:T(8,128)}, u32[]{:S(2)}) copy-start(f32[128,1024]{1,0:T(8,128)} %copy-done.4) | copy-start | bytes 1572868
Sparse Core Ops, SparseCore 0:
  12.3 51.9 all-gather.13
  67.0 47.7 all-gather.11
  149.2 86.9 reduce-scatter.11
  240.6 88.0 reduce-scatter.9
  332.2 87.6 reduce-scatter.19
  424.4 87.8 reduce-scatter.13
  516.4 87.8 reduce-scatter.17
  609.0 87.6 reduce-scatter.15
  700.8 192.4 reduce-scatter.23
  897.3 191.7 reduce-scatter.21
  1093.3 191.7 reduce-scatter.25
  1288.4 69.7 all-reduce.8
  1360.5 49.5 all-gather.21
  1412.3 48.6 all-gather.19
  1463.2 47.8 all-gather.17
  1513.3 47.7 all-gather.15
  1563.3 91.1 all-gather.27
  1656.8 90.8 all-gather.25
  1750.1 90.8 all-gather.23
where the time goes:
time: 1870 us; the launch traced here: 1860 us
  waiting for transfers between devices  1550 us (83%)
  matrix products  116 us (6%)
  blocking collectives  95.8 us (5%)
  other arithmetic  62.8 us (3%)
    reduce_scatter x1, waiting for transfers between devices, shards(): lax.psum_scatter(local_grads[8], 'seq', scatter_dimension=0, tiled=True)  195 us
    reduce_scatter x1, waiting for transfers between devices, shards(): lax.psum_scatter(local_grads[9], 'seq', scatter_dimension=0, tiled=True)  194 us
    reduce_scatter x1, waiting for transfers between devices, shards(): lax.psum_scatter(local_grads[7], 'seq', scatter_dimension=0, tiled=True)  194 us
    reduce_scatter x1, waiting for transfers between devices, shards(): lax.psum_scatter(local_grads[1], 'seq', scatter_dimension=0, tiled=True)  90.6 us
    reduce_scatter x1, waiting for transfers between devices, shards(): lax.psum_scatter(local_grads[2], 'seq', scatter_dimension=0, tiled=True)  90.5 us
    reduce_scatter x1, waiting for transfers between devices, shards(): lax.psum_scatter(local_grads[3], 'seq', scatter_dimension=0, tiled=True)  90.3 us
    all_gather x1, waiting for transfers between devices, shards(): lax.all_gather(shared[9].astype(jnp.bfloat16), 'seq', axis=0, tiled=True)  89.4 us
    reduce_scatter x1, waiting for transfers between devices, shards(): lax.psum_scatter(key_terms.reshape(row_length, inner_width), 'seq', scatt...  88.6 us
  transfers between devices with their start and end apart: 19, of which 17 were waited for; matrix products, arithmetic and copies ran while one was open for 8% of the time, Pallas kernels for 0%

commit v1 on v0

--- a/solution.py
+++ b/solution.py
@@ -1,11 +1,22 @@
+import functools
+
 import jax
 import jax.numpy as jnp
 from jax import lax
+from jax.experimental import pallas as pl
+from jax.experimental.pallas import tpu as pltpu
 from jax.sharding import PartitionSpec as P
 
 EPSILON = 1e-06
 MASKED = -1e30
 THRESHOLDS = (12, 16, 23, 32, 46, 64, 91)
+MESH = pl.DeviceIdType.MESH
+BF = jnp.bfloat16
+F32 = jnp.float32
+LANES = 128
+ANY = pl.BlockSpec(memory_space=pl.ANY)
+VMEM = pl.BlockSpec(memory_space=pltpu.VMEM)
+SMEM = pl.BlockSpec(memory_space=pltpu.SMEM)
 
 
 def bucket_of(relative):
@@ -17,21 +28,964 @@
     return near_bucket + 16 * (relative > 0).astype(jnp.int32)
 
 
+def dot(left_mat, right_mat):
+    return jnp.dot(left_mat, right_mat, preferred_element_type=F32)
+
+
+def dot_rows(left_mat, right_mat):
+    return lax.dot_general(
+        left_mat, right_mat, (((0,), (0,)), ((), ())), preferred_element_type=F32
+    )
+
+
+def dot_cols(left_mat, right_mat):
+    return lax.dot_general(
+        left_mat, right_mat, (((1,), (1,)), ((), ())), preferred_element_type=F32
+    )
+
+
+def ring_place(index, count):
+    odd = index % 2
+    return (1 - odd) * (index // 2) + odd * ((2 * count - 1 - index) // 2)
+
+
+def ring_index(place, count):
+    late = place // (count // 2)
+    return (1 - late) * 2 * place + late * (2 * count - 1 - 2 * place)
+
+
+def greet(targets):
+    barrier = pltpu.get_barrier_semaphore()
+    for target in targets:
+        pl.semaphore_signal(barrier, inc=1, device_id=target, device_id_type=MESH)
+    pl.semaphore_wait(barrier, len(targets))
+
+
+def comm_params(collective_id, vmem=None):
+    return pltpu.CompilerParams(
+        collective_id=collective_id, has_side_effects=True, vmem_limit_bytes=vmem
+    )
+
+
+class Spot:
+    def __init__(self, count):
+        self.count = count
+        self.half = count // 2
+        self.me = lax.axis_index("seq")
+        self.dp = lax.axis_index("dp")
+        self.place = ring_place(self.me, count)
+        self.nexts = tuple((self.dp, self.at(step)) for step in (1, -1))
+        self.far_dp = (self.dp + 2) % 4
+        self.twin_dp = self.dp + 1 - 2 * (self.dp % 2)
+        self.far = (self.far_dp, self.me)
+        self.twin = (self.twin_dp, self.me)
+        self.others = tuple((self.dp, (self.me + step) % count) for step in range(1, count))
+
+    def at(self, step):
+        return ring_index((self.place + (step + self.count) % self.count) % self.count, self.count)
+
+    def back(self, way, hop):
+        return self.at(-hop if way == 0 else hop)
+
+
+def push(source, target, send_sem, recv_sem, device):
+    copy = pltpu.make_async_remote_copy(
+        src_ref=source,
+        dst_ref=target,
+        send_sem=send_sem,
+        recv_sem=recv_sem,
+        device_id=device,
+        device_id_type=MESH,
+    )
+    copy.start()
+    return copy
+
+
+class RingGather:
+    def __init__(self, spot, own, into, send_sems, recv_sems):
+        self.spot, self.own, self.into = spot, own, into
+        self.send_sems, self.recv_sems = send_sems, recv_sems
+        self.copies = {}
+
+    def pieces(self, way, hop):
+        return (0, 1) if hop < self.spot.half - 1 else (way,)
+
+    def forward(self, hop, way, piece):
+        spot = self.spot
+        if hop >= spot.half or piece not in self.pieces(way, hop):
+            return
+        origin = spot.back(way, hop)
+        target = self.into(origin, piece)
+        self.copies[hop, way, piece] = push(
+            self.own(piece) if hop == 0 else target,
+            target,
+            self.send_sems.at[way, hop, piece],
+            self.recv_sems.at[way, hop, piece],
+            spot.nexts[way],
+        )
+
+    def begin(self):
+        for piece in range(2):
+            for way in range(2):
+                self.forward(0, way, piece)
+
+    def step(self, hop):
+        for piece in range(2):
+            for way in range(2):
+                if (hop, way, piece) in self.copies:
+                    self.copies[hop, way, piece].wait_recv()
+                    self.forward(hop + 1, way, piece)
+
+    def finish(self):
+        for copy in self.copies.values():
+            copy.wait_send()
+
+
+def ring_sems(count):
+    return [pltpu.SemaphoreType.DMA((2, count // 2, 2))] * 2
+
+
+class RingSum:
+    def __init__(self, spot, term, bufs, send_sems, recv_sems):
+        self.spot, self.term, self.bufs = spot, term, bufs
+        self.send_sems, self.recv_sems = send_sems, recv_sems
+        self.copies = {}
+
+    def send(self, hop, way, piece, sources):
+        for kind, source in enumerate(sources):
+            self.copies[hop, way, piece, kind] = push(
+                source,
+                self.bufs[kind].at[way, hop, piece],
+                self.send_sems.at[way, hop, piece, kind],
+                self.recv_sems.at[way, hop, piece, kind],
+                self.spot.nexts[way],
+            )
+
+    def block(self, way, hop):
+        step = self.spot.half - hop
+        return self.spot.at(step if way == 0 else -step)
+
+    def begin(self):
+        for way in range(2):
+            self.send(0, way, way, self.term(self.block(way, 0), way))
+        for way in range(2):
+            self.send(1, way, 1 - way, self.term(self.block(way, 1), 1 - way))
+
+    def step(self, hop):
+        for piece in range(2):
+            for way in range(2):
+                if (hop, way, piece, 0) not in self.copies or hop + 1 >= self.spot.half:
+                    continue
+                terms = self.term(self.block(way, hop + 1), piece)
+                for kind, term in enumerate(terms):
+                    self.copies[hop, way, piece, kind].wait_recv()
+                    buf = self.bufs[kind]
+                    buf[way, hop, piece] = (
+                        buf[way, hop, piece].astype(F32) + term[...].astype(F32)
+                    ).astype(BF)
+                self.send(
+                    hop + 1, way, piece, [buf.at[way, hop, piece] for buf in self.bufs]
+                )
+
+    def total(self, piece, kind):
+        last = self.spot.half - 1
+        value = self.term(self.spot.me, piece)[kind][...].astype(F32)
+        for way in range(2):
+            self.copies[last, way, piece, kind].wait_recv()
+            value = value + self.bufs[kind][way, last, piece].astype(F32)
+        return value
+
+    def finish(self):
+        for copy in self.copies.values():
+            copy.wait_send()
+
+
+class MeshGather:
+    def __init__(self, spot, x_ref, o_ref, share, sems):
+        self.spot, self.x_ref, self.o_ref = spot, x_ref, o_ref
+        self.ring_s, self.ring_r, self.x_s, self.x_r, self.core_s, self.core_r = sems
+        rows = x_ref.shape[0]
+        first = rows * share // 100 // 32 * 32
+        cuts = (0, first // 2, first, first + (rows - first) // 2 // 16 * 16, rows)
+        self.windows = [
+            [pl.ds(cuts[2 * part + piece], cuts[2 * part + piece + 1] - cuts[2 * part + piece]) for piece in range(2)]
+            for part in range(2)
+        ]
+        self.ring, self.x, self.core = {}, {}, {}
+
+    def into(self, dp, origin, part, piece):
+        return self.o_ref.at[dp, origin, self.windows[part][piece]]
+
+    def pieces(self, way, hop):
+        return (0, 1) if hop < self.spot.half - 1 else (way,)
+
+    def pass_on(self, part, lane, hop, way, piece, source):
+        spot = self.spot
+        dp = spot.far_dp if lane else spot.dp
+        origin = spot.me if way is None else spot.back(way, hop)
+        target = self.into(dp, origin, part, piece)
+        source = target if source is None else source
+        slot = 0 if way is None else 2 * hop - 1 + way
+        for onward in (0, 1) if way is None else (way,):
+            if hop < spot.half and piece in self.pieces(onward, hop):
+                index = (2 * part if lane == 0 else 4) + onward
+                self.ring[part, lane, hop, onward, piece] = push(
+                    source, target,
+                    self.ring_s.at[index, hop, piece], self.ring_r.at[index, hop, piece],
+                    spot.nexts[onward],
+                )
+        if part == 0 and lane == 0:
+            self.x[part, slot, piece] = push(
+                source, target,
+                self.x_s.at[part, slot, piece], self.x_r.at[part, slot, piece], spot.far,
+            )
+        index = 2 * part + lane
+        self.core[part, lane, slot, piece] = push(
+            source, target,
+            self.core_s.at[index, slot, piece], self.core_r.at[index, slot, piece], spot.twin,
+        )
+
+    def begin(self):
+        spot = self.spot
+        for piece in range(2):
+            self.x[1, 0, piece] = push(
+                self.x_ref.at[self.windows[1][piece]],
+                self.into(spot.dp, spot.me, 1, piece),
+                self.x_s.at[1, 0, piece], self.x_r.at[1, 0, piece], spot.far,
+            )
+        for part in range(2):
+            for piece in range(2):
+                self.pass_on(part, 0, 0, None, piece, self.x_ref.at[self.windows[part][piece]])
+
+    def begin_far(self):
+        for piece in range(2):
+            self.x[1, 0, piece].wait_recv()
+            self.pass_on(1, 1, 0, None, piece, None)
+
+    def step(self, hop):
+        for piece in range(2):
+            for part, lane in ((0, 0), (1, 0), (1, 1)):
+                for way in range(2):
+                    key = (part, lane, hop, way, piece)
+                    if key in self.ring:
+                        self.ring[key].wait_recv()
+                        self.pass_on(part, lane, hop + 1, way, piece, None)
+
+    def step_far(self, hop):
+        spot = self.spot
+        for piece in range(2):
+            for way in (None,) if hop == 0 else range(2):
+                slot = 0 if way is None else 2 * hop - 1 + way
+                if (0, slot, piece) in self.x:
+                    self.x[0, slot, piece].wait_recv()
+                    origin = spot.me if way is None else spot.back(way, hop)
+                    target = self.into(spot.far_dp, origin, 0, piece)
+                    self.core[0, 1, slot, piece] = push(
+                        target, target,
+                        self.core_s.at[1, slot, piece], self.core_r.at[1, slot, piece], spot.twin,
+                    )
+
+    def finish(self):
+        for copy in self.core.values():
+            copy.wait_recv()
+        for copies in (self.ring, self.x, self.core):
+            for copy in copies.values():
+                copy.wait_send()
+
+
+def mesh_sems(count):
+    half = count // 2
+    return [
+        pltpu.SemaphoreType.DMA(shape)
+        for shape in ((6, half, 2), (2, 2 * half + 1, 2), (4, 2 * half + 1, 2))
+        for _ in range(2)
+    ]
+
+
+def ring_gather_body(count, x_ref, o_ref, own_sem, send_sems, recv_sems):
+    spot = Spot(count)
+    greet(spot.nexts)
+    rows = x_ref.shape[0] // 2
+    own = pltpu.make_async_copy(x_ref, o_ref.at[spot.me], own_sem)
+    own.start()
+    ring = RingGather(
+        spot,
+        lambda piece: x_ref.at[pl.ds(piece * rows, rows)],
+        lambda origin, piece: o_ref.at[origin, pl.ds(piece * rows, rows)],
+        send_sems,
+        recv_sems,
+    )
+    ring.begin()
+    for hop in range(spot.half):
+        ring.step(hop)
+    own.wait()
+    ring.finish()
+
+
+def ring_gather(block, count, collective_id, name):
+    return pl.pallas_call(
+        functools.partial(ring_gather_body, count),
+        name=name,
+        out_shape=jax.ShapeDtypeStruct((count,) + block.shape, block.dtype),
+        in_specs=[ANY],
+        out_specs=ANY,
+        scratch_shapes=[pltpu.SemaphoreType.DMA(())] + ring_sems(count),
+        compiler_params=comm_params(collective_id),
+    )(block)
+
+
+def exchange_body(count, parts, x_ref, o_ref, own_sems, send_sems, recv_sems):
+    me = lax.axis_index("seq")
+    dp = lax.axis_index("dp")
+    greet([(dp, (me + step) % count) for step in range(1, count)])
+    rows = x_ref.shape[0] // count
+    copies = []
+    columns = pl.ds(pl.multiple_of(me * LANES, LANES), LANES)
+    for step in range(1, count):
+        target = (me + step) % count
+        for part in range(parts):
+            copy = pltpu.make_async_remote_copy(
+                src_ref=x_ref.at[pl.ds(target * rows, rows), pl.ds(part * LANES, LANES)],
+                dst_ref=o_ref.at[part, :, columns],
+                send_sem=send_sems.at[step - 1, part],
+                recv_sem=recv_sems.at[step - 1, part],
+                device_id=(dp, target),
+                device_id_type=MESH,
+            )
+            copy.start()
+            copies.append(copy)
+    for part in range(parts):
+        copy = pltpu.make_async_copy(
+            x_ref.at[pl.ds(me * rows, rows), pl.ds(part * LANES, LANES)],
+            o_ref.at[part, :, columns],
+            own_sems.at[part],
+        )
+        copy.start()
+        copies.append(copy)
+    for copy in copies:
+        copy.wait()
+
+
+def exchange(block, count, collective_id, name):
+    parts = block.shape[1] // LANES
+    rows = block.shape[0] // count
+    return pl.pallas_call(
+        functools.partial(exchange_body, count, parts),
+        name=name,
+        out_shape=jax.ShapeDtypeStruct((parts, rows, count * LANES), block.dtype),
+        in_specs=[ANY],
+        out_specs=ANY,
+        scratch_shapes=[
+            pltpu.SemaphoreType.DMA((parts,)),
+            pltpu.SemaphoreType.DMA((count - 1, parts)),
+            pltpu.SemaphoreType.DMA((count - 1, parts)),
+        ],
+        compiler_params=comm_params(collective_id),
+    )(block)
+
+
+def near_buckets(rows):
+    shape = (rows, rows + 2 * LANES)
+    column = lax.broadcasted_iota(jnp.int32, shape, 1) - LANES
+    return bucket_of(column - lax.broadcasted_iota(jnp.int32, shape, 0))
+
+
+def strip_window(step, rows, length):
+    return pl.ds(pl.multiple_of(length - rows - step * rows, LANES), length)
+
+
+def attend_body(heads, depth, table_ref, qkv_ref, column_ids, row_ids, p_ref, mixed_ref, strip):
+    step = pl.program_id(0)
+    rows = column_ids.shape[0]
+    length = qkv_ref.shape[0]
+    low = length - rows - LANES
+
+    @pl.when(step == 0)
+    def _():
+        bucket = near_buckets(rows)
+        for head in range(heads):
+            value = jnp.zeros(bucket.shape, F32)
+            for level in range(table_ref.shape[1]):
+                value = jnp.where(bucket == level, table_ref[head, level], value)
+            before = jnp.full((rows, low), table_ref[head, 15], F32)
+            after = jnp.full((rows, strip.shape[2] - low - bucket.shape[1]), table_ref[head, 31], F32)
+            strip[head, :, :low] = before
+            strip[head, :, low : low + bucket.shape[1]] = value
+            strip[head, :, low + bucket.shape[1] :] = after
+
+    same = column_ids[...] == row_ids[...]
+    mine = pl.ds(step * rows, rows)
+    inner = heads * depth
+    window = strip_window(step, rows, length)
+    for head in range(heads):
+        columns = slice(head * depth, (head + 1) * depth)
+        query = qkv_ref[mine, columns]
+        key = qkv_ref[:, inner + head * depth : inner + (head + 1) * depth]
+        value = qkv_ref[:, 2 * inner + head * depth : 2 * inner + (head + 1) * depth]
+        scores = dot_cols(query, key) + strip[head, :, window]
+        scores = jnp.where(same, scores, MASKED)
+        top = jnp.max(scores, axis=1, keepdims=True)
+        weight = jnp.exp(scores - top)
+        weight = weight * (1.0 / jnp.sum(weight, axis=1, keepdims=True))
+        weight = weight.astype(BF)
+        p_ref[head] = weight
+        mixed_ref[:, columns] = dot(weight, value).astype(BF)
+
+
+def attend(qkv, groups, table, heads, depth):
+    length = qkv.shape[0]
+    rows = 256
+    inner = heads * depth
+    return pl.pallas_call(
+        functools.partial(attend_body, heads, depth),
+        name="attend",
+        grid=(length // rows,),
+        out_shape=(
+            jax.ShapeDtypeStruct((heads, length, length), BF),
+            jax.ShapeDtypeStruct((length, inner), BF),
+        ),
+        in_specs=[
+            SMEM,
+            pl.BlockSpec((length, 3 * inner), lambda i: (0, 0)),
+            pl.BlockSpec((rows, 1), lambda i: (i, 0)),
+            pl.BlockSpec((1, length), lambda i: (0, 0)),
+        ],
+        out_specs=(
+            pl.BlockSpec((heads, rows, length), lambda i: (0, i, 0)),
+            pl.BlockSpec((rows, inner), lambda i: (i, 0)),
+        ),
+        scratch_shapes=[pltpu.VMEM((heads, rows, 2 * length - rows), F32)],
+        compiler_params=pltpu.CompilerParams(vmem_limit_bytes=48 << 20),
+    )(table, qkv, groups[:, None], groups[None, :])
+
+
+def tail_body(
+    count,
+    heads,
+    depth,
+    levels,
+    branch_ref,
+    wide_ref,
+    tall_ref,
+    own_out_ref,
+    qkv_ref,
+    p_ref,
+    normed_ref,
+    mixed_ref,
+    feed_ref,
+    proj_ref,
+    own_dqkv_ref,
+    table_ref,
+    branch,
+    dqkv,
+    strip,
+    keys,
+    values,
+    wide_buf,
+    tall_buf,
+    feed_block,
+    packed,
+    near_out,
+    near_in,
+    far_out,
+    far_in,
+    proj_block,
+    ring_s,
+    ring_r,
+    sum_s,
+    sum_r,
+    trade_own,
+    trade_s,
+    trade_r,
+    pair_s,
+    pair_r,
+    copy_sems,
+    *gather_sems,
+):
+    spot = Spot(count)
+    rows, width = branch_ref.shape
+    length = qkv_ref.shape[0]
+    inner = heads * depth
+    greet(spot.others + (spot.far, spot.twin))
+
+    half_rows = rows // 2
+    ring = RingGather(
+        spot,
+        lambda piece: branch_ref.at[pl.ds(piece * half_rows, half_rows)],
+        lambda origin, piece: branch.at[origin, pl.ds(piece * half_rows, half_rows)],
+        ring_s,
+        ring_r,
+    )
+    ring.begin()
+    wide_rows, tall_rows = wide_ref.shape[1] // 2, tall_ref.shape[0] // 2
+    total = RingSum(
+        spot,
+        lambda block, piece: (
+            wide_ref.at[block, pl.ds(piece * wide_rows, wide_rows)],
+            tall_ref.at[
+                pl.ds(piece * tall_rows, tall_rows),
+                pl.ds(pl.multiple_of(block * LANES, LANES), LANES),
+            ],
+        ),
+        (wide_buf, tall_buf),
+        sum_s,
+        sum_r,
+    )
+    total.begin()
+    branch[spot.me] = branch_ref[...]
+    strip[...] = jnp.zeros_like(strip)
+    keys[...] = jnp.zeros_like(keys)
+    values[...] = jnp.zeros_like(values)
+
+    def attend_block(origin):
+        mine = pl.ds(pl.multiple_of(origin * rows, rows), rows)
+        window = strip_window(origin, rows, length)
+        grads = dot_cols(branch[origin], own_out_ref[...]).astype(BF)
+        for head in range(heads):
+            columns = slice(head * depth, (head + 1) * depth)
+            query = qkv_ref[mine, columns]
+            key = qkv_ref[:, inner + head * depth : inner + (head + 1) * depth]
+            value = qkv_ref[:, 2 * inner + head * depth : 2 * inner + (head + 1) * depth]
+            grad = grads[:, columns]
+            weight_low = p_ref[head, mine]
+            weight = weight_low.astype(F32)
+            scaled = weight * dot_cols(grad, value)
+            score_grad = scaled - weight * jnp.sum(scaled, axis=1, keepdims=True)
+            strip[head, :, window] += score_grad
+            score_low = score_grad.astype(BF)
+            dqkv[mine, columns] = dot(score_low, key).astype(BF)
+            keys[:, columns] += dot_rows(score_low, query)
+            values[:, columns] += dot_rows(weight_low, grad)
+
+    attend_block(spot.me)
+    for hop in range(spot.half):
+        ring.step(hop)
+        total.step(hop)
+        if hop < spot.half - 1:
+
+            def both(side, carry, hop=hop):
+                attend_block(spot.at((1 - 2 * side) * (hop + 1)))
+                return carry
+
+            lax.fori_loop(0, 2, both, 0)
+        else:
+            attend_block(spot.at(spot.half))
+
+    tiles = wide_ref.shape[2] // LANES
+    for piece in range(2):
+        value = total.total(piece, 0).astype(BF)
+        for tile in range(tiles):
+            feed_block[pl.ds((2 * tile + piece) * wide_rows, wide_rows)] = value[
+                :, tile * LANES : (tile + 1) * LANES
+            ]
+        feed_block[pl.ds(2 * tiles * wide_rows + piece * tall_rows, tall_rows)] = total.total(
+            piece, 1
+        ).astype(BF)
+    half_sems = len(gather_sems) // 2
+    feed = MeshGather(spot, feed_block, feed_ref, 62, gather_sems[:half_sems])
+    feed.begin()
+    feed_copy = pltpu.make_async_copy(feed_block, feed_ref.at[spot.dp, spot.me], copy_sems.at[0])
+    feed_copy.start()
+
+    dqkv[:, inner : 2 * inner] = keys[...].astype(BF)
+    dqkv[:, 2 * inner :] = values[...].astype(BF)
+    trades = []
+    columns = pl.ds(pl.multiple_of(spot.me * LANES, LANES), LANES)
+    for index, device in enumerate(spot.others):
+        for part in range(3):
+            trades.append(
+                push(
+                    dqkv.at[pl.ds(device[1] * rows, rows), pl.ds(part * LANES, LANES)],
+                    own_dqkv_ref.at[part, :, columns],
+                    trade_s.at[index, part],
+                    trade_r.at[index, part],
+                    device,
+                )
+            )
+    for part in range(3):
+        copy = pltpu.make_async_copy(
+            dqkv.at[pl.ds(spot.me * rows, rows), pl.ds(part * LANES, LANES)],
+            own_dqkv_ref.at[part, :, columns],
+            trade_own.at[part],
+        )
+        copy.start()
+        trades.append(copy)
+
+    feed.begin_far()
+
+    quarter = width // 4
+
+    @pl.loop(0, 4)
+    def _(index):
+        block = dot_rows(
+            normed_ref[:, pl.ds(pl.multiple_of(index * quarter, quarter), quarter)], dqkv[...]
+        )
+        for part in range(3):
+            packed[index, part * quarter : (part + 1) * quarter] = block[
+                :, part * LANES : (part + 1) * LANES
+            ]
+
+    slim = inner // 4
+    for tile in range(width // LANES):
+        terms = jnp.zeros((inner, LANES), F32)
+        for source in range(count):
+            terms = terms + dot_rows(
+                mixed_ref[pl.ds(source * rows, rows)],
+                branch[source, :, tile * LANES : (tile + 1) * LANES],
+            )
+        for index in range(4):
+            base = 3 * quarter + tile * slim
+            packed[index, base : base + slim] = terms[index * slim : (index + 1) * slim]
+    core, side = spot.dp % 2, spot.dp // 2
+    for index in range(2):
+        near_out[index] = packed[2 * index + 1 - core].astype(BF)
+    near = push(near_out, near_in, pair_s.at[0], pair_r.at[0], spot.twin)
+    near.wait_recv()
+    far_out[...] = (packed[2 * (1 - side) + core] + near_in[1 - side].astype(F32)).astype(BF)
+    far = push(far_out, far_in, pair_s.at[1], pair_r.at[1], spot.far)
+    feed.step(0)
+    feed.step_far(0)
+    far.wait_recv()
+    proj_block[...] = (
+        packed[2 * side + core] + near_in[side].astype(F32) + far_in[...].astype(F32)
+    ).astype(BF)
+    proj = MeshGather(spot, proj_block, proj_ref, 57, gather_sems[half_sems:])
+    proj.begin()
+    proj_copy = pltpu.make_async_copy(proj_block, proj_ref.at[spot.dp, spot.me], copy_sems.at[1])
+    proj_copy.start()
+
+    bucket = near_buckets(rows)
+    span = bucket.shape[1]
+    low = length - rows - LANES
+    for head in range(heads):
+        middle = strip[head, :, low : low + span]
+        before = jnp.sum(strip[head, :, :low], axis=0, keepdims=True)
+        after = jnp.sum(strip[head, :, low + span :], axis=0, keepdims=True)
+        for level in range(levels):
+            part = jnp.sum(jnp.where(bucket == level, middle, 0.0), axis=0, keepdims=True)
+            row = part[:, :LANES]
+            for tile in range(1, span // LANES):
+                row = row + part[:, tile * LANES : (tile + 1) * LANES]
+            edge = before if level == 15 else after if level == 31 else None
+            if edge is not None:
+                for tile in range(edge.shape[1] // LANES):
+                    row = row + edge[:, tile * LANES : (tile + 1) * LANES]
+            table_ref[head, level : level + 1, :] = row
+
+    for hop in range(1, spot.half):
+        feed.step(hop)
+        if hop == 1:
+            proj.begin_far()
+        feed.step_far(hop)
+    feed.step_far(spot.half)
+    for hop in range(spot.half):
+        proj.step(hop)
+        proj.step_far(hop)
+    proj.step_far(spot.half)
+    feed_copy.wait()
+    proj_copy.wait()
+    near.wait_send()
+    far.wait_send()
+    for copy in trades:
+        copy.wait()
+    ring.finish()
+    total.finish()
+    feed.finish()
+    proj.finish()
+
+
+def tail(branch, wide, tall, own_out, qkv, weights, normed, mixed, count, heads, depth, levels):
+    rows, width = branch.shape
+    length = qkv.shape[0]
+    inner = heads * depth
+    half = count // 2
+    wide_rows, span = wide.shape[1:]
+    tall_rows = tall.shape[0]
+    feed_rows = wide_rows * (span // LANES) + tall_rows
+    proj_rows = 3 * (width // 4) + inner // 4 * (width // LANES)
+    dma = pltpu.SemaphoreType.DMA
+    return pl.pallas_call(
+        functools.partial(tail_body, count, heads, depth, levels),
+        name="tail",
+        out_shape=(
+            jax.ShapeDtypeStruct((4, count, feed_rows, LANES), BF),
+            jax.ShapeDtypeStruct((4, count, proj_rows, LANES), BF),
+            jax.ShapeDtypeStruct((3, rows, width), BF),
+            jax.ShapeDtypeStruct((heads, levels, LANES), F32),
+        ),
+        in_specs=[VMEM] * 8,
+        out_specs=(ANY, ANY, ANY, VMEM),
+        scratch_shapes=[
+            pltpu.VMEM((count, rows, width), BF),
+            pltpu.VMEM((length, 3 * inner), BF),
+            pltpu.VMEM((heads, rows, 2 * length - rows), F32),
+            pltpu.VMEM((length, inner), F32),
+            pltpu.VMEM((length, inner), F32),
+            pltpu.VMEM((2, half, 2, wide_rows // 2, span), BF),
+            pltpu.VMEM((2, half, 2, tall_rows // 2, LANES), BF),
+            pltpu.VMEM((feed_rows, LANES), BF),
+            pltpu.VMEM((4, proj_rows, LANES), F32),
+            pltpu.VMEM((2, proj_rows, LANES), BF),
+            pltpu.VMEM((2, proj_rows, LANES), BF),
+            pltpu.VMEM((proj_rows, LANES), BF),
+            pltpu.VMEM((proj_rows, LANES), BF),
+            pltpu.VMEM((proj_rows, LANES), BF),
+            *ring_sems(count),
+            dma((2, half, 2, 2)),
+            dma((2, half, 2, 2)),
+            dma((3,)),
+            dma((count - 1, 3)),
+            dma((count - 1, 3)),
+            dma((2,)),
+            dma((2,)),
+            dma((2,)),
+            *mesh_sems(count),
+            *mesh_sems(count),
+        ],
+        compiler_params=comm_params(3, 56 << 20),
+    )(branch, wide, tall, own_out, qkv, weights, normed, mixed)
+
+
+def widen_pair_body(part, x_ref, gate_ref, up_ref):
+    outs = (gate_ref, up_ref)
+    for dp in range(x_ref.shape[0]):
+        for tile in range(x_ref.shape[2] // LANES):
+            block = x_ref[dp, 0, tile * LANES : (tile + 1) * LANES].astype(F32)
+            start = tile * LANES
+            while start < (tile + 1) * LANES:
+                which = start // part
+                stop = min((tile + 1) * LANES, (which + 1) * part)
+                base = dp * part + start - which * part
+                outs[which][:, base : base + stop - start] = block[
+                    :, start - tile * LANES : stop - tile * LANES
+                ]
+                start = stop
+
+
+def widen_pair(gathered, rows, part):
+    dps, count = gathered.shape[:2]
+    size = rows * 2 * part // LANES
+    shape = jax.ShapeDtypeStruct((count * rows, dps * part), F32)
+    spec = pl.BlockSpec((rows, dps * part), lambda i: (i, 0))
+    return pl.pallas_call(
+        functools.partial(widen_pair_body, part),
+        name="widen_pair",
+        grid=(count,),
+        out_shape=(shape, shape),
+        in_specs=[pl.BlockSpec((dps, 1, size, LANES), lambda i: (0, i, 0, 0))],
+        out_specs=(spec, spec),
+        compiler_params=pltpu.CompilerParams(vmem_limit_bytes=48 << 20),
+    )(gathered)
+
+
+def widen_columns_body(x_ref, *o_refs):
+    rows = o_refs[0].shape[0]
+    for index, o_ref in enumerate(o_refs):
+        for source in range(x_ref.shape[1]):
+            o_ref[:, source * LANES : (source + 1) * LANES] = x_ref[
+                0, source, index * rows : (index + 1) * rows
+            ].astype(F32)
+
+
+def widen_columns(gathered, first, rows, outs, pieces):
+    dps, count = gathered.shape[:2]
+    size = rows // pieces
+    shape = jax.ShapeDtypeStruct((dps * rows, count * LANES), F32)
+    spec = pl.BlockSpec((size, count * LANES), lambda i, k: (i * pieces + k, 0))
+    base = first // (size * outs)
+    return pl.pallas_call(
+        widen_columns_body,
+        name="widen_columns",
+        grid=(dps, pieces),
+        out_shape=(shape,) * outs,
+        in_specs=[
+            pl.BlockSpec((1, count, size * outs, LANES), lambda i, k: (i, 0, base + k, 0))
+        ],
+        out_specs=(spec,) * outs,
+        compiler_params=pltpu.CompilerParams(vmem_limit_bytes=48 << 20),
+    )(gathered)
+
+
+def widen_rows_body(x_ref, o_ref):
+    dps, _, size, _ = x_ref.shape
+    tiles = o_ref.shape[1] // LANES
+    rows = size // tiles
+    for dp in range(dps):
+        for tile in range(tiles):
+            o_ref[dp * rows : (dp + 1) * rows, tile * LANES : (tile + 1) * LANES] = x_ref[
+                dp, 0, tile * rows : (tile + 1) * rows
+            ].astype(F32)
+
+
+def widen_rows(gathered, first, rows, width):
+    dps, count = gathered.shape[:2]
+    size = rows * (width // LANES)
+    base = first // size
+    return pl.pallas_call(
+        widen_rows_body,
+        name="widen_rows",
+        grid=(count,),
+        out_shape=jax.ShapeDtypeStruct((count * dps * rows, width), F32),
+        in_specs=[pl.BlockSpec((dps, 1, size, LANES), lambda i: (0, i, base, 0))],
+        out_specs=pl.BlockSpec((dps * rows, width), lambda i: (i, 0)),
+    )(gathered)
+
+
+def split_shards(
+    hidden,
+    group_ids,
+    norm1_gain,
+    query_weight,
+    key_weight,
+    value_weight,
+    out_weight,
+    relative_bias,
+    norm2_gain,
+    gate_weight,
+    up_weight,
+    down_projection_weight,
+    out_grad,
+    *,
+    count,
+):
+    tokens, width = hidden.shape[1:]
+    levels, head_count = relative_bias.shape
+    depth = query_weight.shape[1] // head_count
+    heads = head_count // count
+    inner = heads * depth
+    length = group_ids.shape[1]
+    ff = gate_weight.shape[1] // 4
+    me = lax.axis_index("seq")
+    dp = lax.axis_index("dp")
+    gain_one = norm1_gain.astype(F32)
+    gain_two = norm2_gain.astype(F32)
+
+    def over_core(value):
+        return lax.ppermute(value, "dp", [(i, i ^ 1) for i in range(4)])
+
+    def over_x(value):
+        return lax.ppermute(value, "dp", [(i, i ^ 2) for i in range(4)])
+
+    def gather_dp(value):
+        near = over_core(value)
+        far = over_x(value)
+        cross = over_core(far)
+        return jnp.concatenate([value, near, far, cross])
+
+    def sum_dp(value):
+        parts = value.reshape(4, tokens, width)
+        kept = parts[0::2] + over_core(parts[1::2].astype(BF)).astype(F32)
+        return kept[0] + over_x(kept[1].astype(BF)).astype(F32)
+
+    row = ring_gather(hidden[0], count, 0, "gather_row").reshape(length, width)
+    row_f = row.astype(F32)
+    row_scale = lax.rsqrt(jnp.mean(row_f * row_f, axis=-1, keepdims=True) + EPSILON)
+    normed = (row_f * row_scale * gain_one).astype(BF)
+    own_columns = lambda w: lax.dynamic_slice_in_dim(w, me * inner, inner, axis=1)
+    qkv_weight = jnp.concatenate(
+        [own_columns(w) for w in (query_weight, key_weight, value_weight)], axis=1
+    )
+    qkv = dot(normed, qkv_weight).astype(BF)
+    groups = group_ids[0]
+    table = lax.dynamic_slice_in_dim(relative_bias, me * heads, heads, axis=1).T.astype(F32)
+    weights, mixed_heads = attend(qkv, groups, table, heads, depth)
+    mixed = exchange(mixed_heads, count, 1, "mixed_exchange")[0]
+
+    inputs = hidden[0].astype(F32)
+    middle = inputs + dot(mixed, out_weight)
+    scale_two = lax.rsqrt(jnp.mean(middle * middle, axis=-1, keepdims=True) + EPSILON)
+    normed_two = (middle * scale_two * gain_two).astype(BF)
+    cotangents = gather_dp(out_grad[0])
+    tokens_two = gather_dp(normed_two)
+    pair_weight = jnp.concatenate(
+        [
+            lax.dynamic_slice_in_dim(gate_weight, dp * ff, ff, axis=1),
+            lax.dynamic_slice_in_dim(up_weight, dp * ff, ff, axis=1),
+        ],
+        axis=1,
+    )
+    down_weight = lax.dynamic_slice_in_dim(down_projection_weight, dp * ff, ff, axis=0)
+    pair = dot(tokens_two, pair_weight)
+    gate, up = pair[:, :ff], pair[:, ff:]
+    root = 0.7978845608028654
+    squared = gate * gate
+    bend = jnp.tanh(root * (gate + 0.044715 * gate * squared))
+    half = 0.5 * (1.0 + bend)
+    gelu = gate * half
+    slope = half + 0.5 * gate * (1.0 - bend * bend) * root * (1.0 + 3 * 0.044715 * squared)
+    activated = (gelu * up).astype(BF)
+    act_grad = dot_cols(cotangents, down_weight)
+    pair_grad = jnp.concatenate(
+        [(act_grad * up * slope).astype(BF), (act_grad * gelu).astype(BF)], axis=1
+    )
+    normed_two_grad = sum_dp(dot_cols(pair_grad, pair_weight))
+    block_out = (middle + sum_dp(dot(activated, down_weight))).astype(BF)
+    pair_terms = dot_rows(tokens_two, pair_grad).astype(BF).reshape(count, width // count, 2 * ff)
+    down_terms = dot_rows(activated, cotangents).astype(BF)
+    cotangent = out_grad[0].astype(F32)
+    lifted = gain_two * normed_two_grad
+    middle_grad = (
+        cotangent
+        + scale_two * lifted
+        - middle * scale_two**3 * jnp.mean(middle * lifted, axis=-1, keepdims=True)
+    )
+    gain_two_grad = jnp.sum(normed_two_grad * middle * scale_two, axis=0)
+
+    own_out = lax.dynamic_slice_in_dim(out_weight, me * inner, inner, axis=0)
+    feed, proj, own_dqkv, table_part = tail(
+        middle_grad.astype(BF), pair_terms, down_terms, own_out, qkv, weights, normed, mixed_heads,
+        count, heads, depth, levels,
+    )
+    normed_grad = (
+        dot_cols(own_dqkv[0], query_weight)
+        + dot_cols(own_dqkv[1], key_weight)
+        + dot_cols(own_dqkv[2], value_weight)
+    )
+    scale_one = lax.rsqrt(jnp.mean(inputs * inputs, axis=-1, keepdims=True) + EPSILON)
+    raised = gain_one * normed_grad
+    hidden_grad = (
+        middle_grad
+        + scale_one * raised
+        - inputs * scale_one**3 * jnp.mean(inputs * raised, axis=-1, keepdims=True)
+    )
+    gain_one_grad = jnp.sum(normed_grad * inputs * scale_one, axis=0)
+    table_grad = lax.dynamic_update_slice_in_dim(
+        jnp.zeros((levels, head_count), F32), jnp.sum(table_part, axis=-1).T, me * heads, axis=1
+    )
+
+    small = jnp.concatenate([gain_one_grad, gain_two_grad, table_grad.reshape(-1)])
+    small = small.reshape(-1, LANES)
+    small = small + over_core(small)
+    small = small + over_x(small)
+    step = 1
+    while step < count:
+        small = small + lax.ppermute(small, "seq", [(i, i ^ step) for i in range(count)])
+        step *= 2
+    small = small.reshape(-1)
+    quarter, slim = width // 4, inner // 4
+    gate_grad, up_grad = widen_pair(feed, width // count, ff)
+    (down_grad,) = widen_columns(feed, 2 * ff * width // count // LANES, ff, 1, 2)
+    query_grad, key_grad, value_grad = widen_columns(proj, 0, quarter, 3, 1)
+    out_weight_grad = widen_rows(proj, 3 * quarter, slim, width)
+    return (
+        block_out[None],
+        hidden_grad[None],
+        small[:width],
+        query_grad,
+        key_grad,
+        value_grad,
+        out_weight_grad,
+        small[2 * width :].reshape(levels, head_count),
+        small[width : 2 * width],
+        gate_grad,
+        up_grad,
+        down_grad,
+    )
+
+
 def rms_norm(vector, norm_gain):
     return (
         vector * lax.rsqrt(jnp.mean(vector * vector, axis=-1, keepdims=True) + EPSILON) * norm_gain
-    )
-
-
-def dot_rows(left_mat, right_mat):
-    return lax.dot_general(
-        left_mat, right_mat, (((0,), (0,)), ((), ())), preferred_element_type=jnp.float32
-    )
-
-
-def dot_cols(left_mat, right_mat):
-    return lax.dot_general(
-        left_mat, right_mat, (((1,), (1,)), ((), ())), preferred_element_type=jnp.float32
     )
 
 
@@ -327,38 +1281,25 @@
 
 
 def solution(mesh):
-    placed = (
-        P("dp", "seq", None),
-        P("dp", None),
-        P(),
-        P(),
-        P(),
-        P(),
-        P(),
-        P(),
-        P(),
-        P(),
-        P(),
-        P(),
-        P("dp", "seq", None),
-    )
-    return jax.shard_map(
-        shards,
-        mesh=mesh,
-        in_specs=placed,
-        out_specs=(
-            P("dp", "seq", None),
-            P("dp", "seq", None),
-            P(),
-            P(),
-            P(),
-            P(),
-            P(),
-            P(),
-            P(),
-            P(),
-            P(),
-            P(),
-        ),
-        check_vma=False,
-    )
+    placed = (P("dp", "seq", None), P("dp", None)) + (P(),) * 10 + (P("dp", "seq", None),)
+    out_specs = (P("dp", "seq", None),) * 2 + (P(),) * 10
+    count = mesh.shape["seq"]
+
+    def run(*args):
+        hidden, query_weight, relative_bias = args[0], args[3], args[7]
+        head_count = relative_bias.shape[1]
+        inner = query_weight.shape[1] // count
+        fits = (
+            mesh.shape["dp"] == 4
+            and count % 2 == 0
+            and head_count % count == 0
+            and inner == LANES
+            and hidden.shape[2] == count * LANES
+            and hidden.shape[1] == count * LANES
+        )
+        body = functools.partial(split_shards, count=count) if fits else shards
+        return jax.shard_map(
+            body, mesh=mesh, in_specs=placed, out_specs=out_specs, check_vma=False
+        )(*args)
+
+    return run

time: 1870 us -> 366 us (0.20)
  waiting for transfers between devices: 1550 us -> 25.1 us
  Pallas kernels: 0 us -> 273 us
  blocking collectives: 95.8 us -> 0 us
  matrix products: 116 us -> 27 us
  other arithmetic: 62.8 us -> 12.2 us
    reduce_scatter x9 -> x0, waiting for transfers between devices: 1070 us -> none  [the longest x1 195 us: shards(): lax.psum_scatter(local_grads[8], 'seq', scatter_dimension=0, tiled=True)]
    all_gather x9 -> x0, waiting for transfers between devices: 401 us -> none  [the longest x1 89.4 us: shards(): lax.all_gather(shared[9].astype(jnp.bfloat16), 'seq', axis=0, tiled=True)]
    pallas_call x0 -> x8, Pallas kernels: none -> 273 us  [the longest x1 191 us: tail(): pl.pallas_call(functools.partial(tail_body, count, heads, depth, levels),...]
    psum x1 -> x0, waiting for transfers between devices: 70.6 us -> none  [shards(): lax.psum(shared[1].astype(jnp.bfloat16), 'dp').astype(jnp.float32)]
    dot_general x15 -> x4, matrix products: 66 us -> 8.24 us  [dot(): return jnp.dot(left_mat, right_mat, preferred_element_type=F32)]
    unnamed x2 -> x0, blocking collectives: 55.1 us -> none
    convert_element_type x19 -> x6, other arithmetic: 56.6 us -> 7.13 us  [the longest x1 3.46 us: split_shards(): normed = (row_f * row_scale * gain_one).astype(BF)]
    all_gather x2 -> x0, blocking collectives: 34.6 us -> none  [the longest x1 18.4 us: shards(): lax.all_gather(shared[6].astype(jnp.bfloat16), 'seq', axis=0, tiled=True)]
  transfers between devices with their start and end apart: 19 -> 15, of which waited for: 17 -> 8; matrix products, arithmetic and copies ran while one was open for 8% -> 5% of each run, Pallas kernels for 0% -> 10%
where the time goes in v1:
time: 366 us; the launch traced here: 360 us
  Pallas kernels  273 us (75%)
  matrix products  27 us (7%)
  waiting for transfers between devices  25.1 us (7%)
  other arithmetic  12.2 us (3%)
  local copies, waits for them, and re-layouts  11.3 us (3%)
  starting transfers between devices  10.3 us (3%)
    pallas_call x1, Pallas kernels, tail(): pl.pallas_call(functools.partial(tail_body, count, heads, depth, levels),...  191 us
    pallas_call x1, Pallas kernels, ring_gather(): pl.pallas_call(functools.partial(ring_gather_body, count), name=name, out...  27.8 us
    ppermute x5, waiting for transfers between devices, over_x(): return lax.ppermute(value, 'dp', [(i, i ^ 2) for i in range(4)])  18.1 us
    pallas_call x2, Pallas kernels, widen_columns(): pl.pallas_call(widen_columns_body, name='widen_columns', grid=(dps, piece...  16.9 us
    pallas_call x1, Pallas kernels, widen_pair(): pl.pallas_call(functools.partial(widen_pair_body, part), name='widen_pair...  13.5 us
    dot_general x5, matrix products, dot_cols(): lax.dot_general(left_mat, right_mat, (((1,), (1,)), ((), ())), preferred_...  11.2 us
    pallas_call x1, Pallas kernels, attend(): pl.pallas_call(functools.partial(attend_body, heads, depth), name='attend...  9.57 us
    dot_general x4, matrix products, dot(): return jnp.dot(left_mat, right_mat, preferred_element_type=F32)  8.24 us
  transfers between devices with their start and end apart: 15, of which 8 were waited for; matrix products, arithmetic and copies ran while one was open for 5% of the time, Pallas kernels for 10%

profile of v1, /device:TPU:0, one launch (start us, length us, event | category | flops | bytes accessed | tf_op | source)
XLA Modules:
  0.0 360.1 jit_solution(10959764700654142976)
XLA Ops:
  0.7 0.8 convert_element_type.84
  1.5 27.8 %gather_row.1 = bf16[8,128,1024]{2,1,0:T(8,128)(2,1)} custom-call(bf16[128,1024]{1,0:T(8,128)(2,1)} %bitcast.87), custom_call_target="tpu_custom_call" | custom-call | tf_op jit(solution)/shard_map/gather_row/pallas_call | solution.py:326
  29.4 2.1 multiply_reduce_fusion
  31.4 0.2 copy.31.column_ids
  31.7 0.7 convert_bitcast_fusion.table_ref
  32.4 3.5 fusion.1.normed_ref
  35.8 1.0 constant_dynamic-slice_fusion.5
  36.8 1.1 constant_dynamic-slice_fusion.3
  37.9 2.8 convolution_convert_fusion.2.qkv_ref
  40.7 9.6 %attend.1 = (bf16[2,1024,1024]{2,1,0:T(8,128)(2,1)S(1)}, bf16[1024,128]{1,0:T(8,128)(2,1)S(1)}) custom-call(f32[2,32]{1,0:T(2,128)S(1)} %convert_bitcast_fusion.table_ref, bf16[1024,384]{1,0:T(8,128)(2,1)S(1)} %convolution_convert_fusion.2.qkv_ref, s32[1024,1]{1,0:T(8,128)S(1)} %copy.31.column_ids, s32[1,1024]{1,0:T(1,128)S(1)} %copy-done.5), custom_call_target="tpu_custom_call" | custom-call | tf_op jit(solution)/shard_map/attend/pallas_call | solution.py:439
  50.3 2.0 copy-done.2
  52.3 0.7 copy-done.4
  53.0 8.1 %mixed_exchange.1 = bf16[1,128,1024]{2,1,0:T(8,128)(2,1)} custom-call(bf16[1024,128]{1,0:T(8,128)(2,1)} %copy-done.4), custom_call_target="tpu_custom_call" | custom-call | tf_op jit(solution)/shard_map/mixed_exchange/pallas_call | solution.py:372
  61.2 1.6 multiply_reduce_fusion.3
  62.8 0.1 multiply_convert_fusion.3
  62.9 1.6 collective-permute-start.1
  64.4 0.5 collective-permute-start.6
  65.0 0.2 collective-permute-start.5
  65.2 1.1 fusion.14
  66.3 3.7 %constant_dynamic-slice_fusion.1 = (bf16[1024,704]{1,0:T(8,128)(2,1)S(1)}, bf16[1024,704]{1,0:T(8,128)(2,1)S(1)}) fusion(bf16[1024,2816]{1,0:T(8,128)(2,1)} %param.23, s32[]{:T(128)S(6)} %select_n.8, bf16[1024,2816]{1,0:T(8,128)(2,1)} %param.22), kind=kLoop, calls=%fused_computation.76 | loop fusion | bytes 5767172 | tf_op jit(solution)/shard_map/dynamic_slice | solution.py:903
  70.0 0.9 collective-permute-done.1
  70.9 0.7 constant_dynamic-slice_fusion.own_out_ref
  71.6 3.5 collective-permute-done.6
  75.1 2.9 fusion.3
  78.0 2.9 multiply_convert_fusion.1
  80.9 1.9 fusion.2
  82.8 0.2 convert.16
  83.0 0.6 collective-permute-start.8
  83.5 1.0 fusion.7
  84.5 0.2 convert.14
  84.7 0.1 collective-permute-start.3
  84.8 4.4 %convolution_convert_fusion = bf16[1024,1408]{1,0:T(8,128)(2,1)} fusion(bf16[512,704]{1,0:T(8,128)(2,1)S(1)} %get-tuple-element.65, bf16[512,704]{1,0:T(8,128)(2,1)S(1)} %get-tuple-element.64, bf16[128,1024]{1,0:T(8,128)(2,1)S(1)} %collective-permute-done.2, bf16[128,1024]{1,0:T(8,128)(2,1)S(1)} %collective-permute-done.1, ...), kind=kOutput, calls=%fused_computation.4 | convolution fusion | flops 1484914688 | bytes 5373952 | tf_op jit(solution)/shard_map/dot_general | solution.py:36
  89.2 3.1 convolution_convert_fusion.1.tall_ref
  92.3 0.1 convert_add_fusion
  92.5 1.6 collective-permute-start.9
  94.1 0.1 convert_add_fusion.1
  94.3 0.8 collective-permute-start.4
  95.1 6.6 %collective-permute-done.9 = bf16[128,1024]{1,0:T(8,128)(2,1)S(1)} collective-permute-done((bf16[128,1024]{1,0:T(8,128)(2,1)S(1)}, bf16[128,1024]{1,0:T(8,128)(2,1)S(1)}, u32[]{:S(2)}, u32[]{:S(2)}) %collective-permute-start.9) | collective-permute-done | bytes 262176 | tf_op jit(solution)/shard_map/ppermute | solution.py:867
  101.7 0.2 multiply_reduce_fusion.1
  101.9 5.0 %collective-permute-done.4 = bf16[128,1024]{1,0:T(8,128)(2,1)S(1)} collective-permute-done((bf16[128,1024]{1,0:T(8,128)(2,1)S(1)}, bf16[128,1024]{1,0:T(8,128)(2,1)S(1)}, u32[]{:S(2)}, u32[]{:S(2)}) %collective-permute-start.4) | collective-permute-done | bytes 262176 | tf_op jit(solution)/shard_map/ppermute | solution.py:867
  106.9 2.0 fusion.45
  108.9 190.8 %tail.1 = (bf16[4,8,2112,128]{3,2,1,0:T(8,128)(2,1)}, bf16[4,8,1024,128]{3,2,1,0:T(8,128)(2,1)}, bf16[3,128,1024]{2,1,0:T(8,128)(2,1)}, f32[2,32,128]{2,1,0:T(8,128)}) custom-call(bf16[128,1024]{1,0:T(8,128)(2,1)} %get-tuple-element.62.branch_ref, bf16[8,128,1408]{2,1,0:T(8,128)(2,1)} %bitcast.92, bf16[704,1024]{1,0:T(8,128)(2,1)} %convolution_convert_fusion.1.tall_ref, ...), custom_call_target="tpu_custom_call" | custom-call | tf_op jit(solution)/shard_map/tail/pallas_call | solution.py:707
  299.8 1.9 fusion.30
  301.7 1.8 convolution_add_fusion.1
  303.6 0.1 reduce_sum.79
  303.7 0.1 copy.34
  303.8 0.2 dynamic_update_slice.3
  304.1 2.7 fusion.20
  306.7 0.6 collective-permute-start.10
  307.4 0.8 collective-permute-done.10
  308.2 1.5 collective-permute-start.11
  309.7 2.2 collective-permute-done.11
  311.9 0.9 collective-permute-start.12
  312.8 2.8 collective-permute-done.12
  315.6 0.5 collective-permute-start.13
  316.1 3.2 collective-permute-done.13
  319.3 1.6 collective-permute-start.14
  320.9 1.0 fusion.17
  321.9 8.0 %widen_columns.2 = (f32[1024,1024]{1,0:T(8,128)}, f32[1024,1024]{1,0:T(8,128)}, f32[1024,1024]{1,0:T(8,128)}) custom-call(bf16[4,8,1024,128]{3,2,1,0:T(8,128)(2,1)} %get-tuple-element.27.x_ref), custom_call_target="tpu_custom_call" | custom-call | tf_op jit(solution)/shard_map/widen_columns/pallas_call | solution.py:796
  329.8 6.0 %widen_rows.1 = f32[1024,1024]{1,0:T(8,128)} custom-call(bf16[4,8,1024,128]{3,2,1,0:T(8,128)(2,1)} %get-tuple-element.27.x_ref), custom_call_target="tpu_custom_call" | custom-call | tf_op jit(solution)/shard_map/widen_rows/pallas_call | solution.py:824
  335.8 13.5 %widen_pair.1 = (f32[1024,2816]{1,0:T(8,128)}, f32[1024,2816]{1,0:T(8,128)}) custom-call(bf16[4,8,2112,128]{3,2,1,0:T(8,128)(2,1)} %get-tuple-element.31.x_ref), custom_call_target="tpu_custom_call" | custom-call | tf_op jit(solution)/shard_map/widen_pair/pallas_call | solution.py:770
  349.3 8.9 %widen_columns.3 = f32[2816,1024]{1,0:T(8,128)} custom-call(bf16[4,8,2112,128]{3,2,1,0:T(8,128)(2,1)} %get-tuple-element.31.x_ref), custom_call_target="tpu_custom_call" | custom-call | tf_op jit(solution)/shard_map/widen_columns/pallas_call | solution.py:796
  358.3 0.6 slice_bitcast_fusion.2
  358.9 0.7 copy.35
  (55 shorter events, 0.5 us)
Async XLA Ops:
  0.6 60.5 %copy-start = (bf16[1024,1024]{1,0:T(8,128)(2,1)S(1)}, bf16[1024,1024]{1,0:T(8,128)(2,1)}, u32[]{:S(2)}) copy-start(bf16[1024,1024]{1,0:T(8,128)(2,1)} %param.19) | copy-start | bytes 6291460
  1.5 29.9 %copy-start.5 = (s32[1,1024]{1,0:T(1,128)S(1)}, s32[1,1024]{1,0:T(1,128)}, u32[]{:S(2)}) copy-start(s32[1,1024]{1,0:T(1,128)} %row_ids.1) | copy-start | bytes 12292
  40.7 22.0 %copy-start.3 = (bf16[1024,384]{1,0:T(8,128)(2,1)}, bf16[1024,384]{1,0:T(8,128)(2,1)S(1)}, u32[]{:S(2)}) copy-start(bf16[1024,384]{1,0:T(8,128)(2,1)S(1)} %convolution_convert_fusion.2.qkv_ref) | copy-start | bytes 2359300
  50.3 2.0 copy-start.2
  52.3 0.7 copy-start.4
  53.0 9.7 %copy-start.10 = (bf16[1024]{0:T(1024)(128)(2,1)S(1)}, bf16[1024]{0:T(1024)(128)(2,1)}, u32[]{:S(2)}) copy-start(bf16[1024]{0:T(1024)(128)(2,1)} %param.21) | copy-start | bytes 6148
  62.9 8.0 %collective-permute-start.1 = (bf16[128,1024]{1,0:T(8,128)(2,1)S(1)}, bf16[128,1024]{1,0:T(8,128)(2,1)S(1)}, u32[]{:S(2)}, u32[]{:S(2)}) collective-permute-start(bf16[128,1024]{1,0:T(8,128)(2,1)S(1)} %multiply_convert_fusion.3), channel_id=1, source_target_pairs={{0,16},{8,24},{16,0},{24,8},{1,17},{9,25},{17,1},{25,9},{2,18},{10... | collective-permute-start | bytes 786440 | tf_op jit(solution)/shard_map/ppermute | solution.py:867
  64.4 10.6 %collective-permute-start = (bf16[128,1024]{1,0:T(8,128)(2,1)S(1)}, bf16[128,1024]{1,0:T(8,128)(2,1)}, u32[]{:S(2)}, u32[]{:S(2)}) collective-permute-start(bf16[128,1024]{1,0:T(8,128)(2,1)S(1)} %multiply_convert_fusion.3), channel_id=1, source_target_pairs={{0,8},{8,0},{16,24},{24,16},{1,9},{9,1},{17,25},{25,17},{2,10},{10... | collective-permute-start | bytes 786440 | tf_op jit(solution)/shard_map/ppermute | solution.py:864
  64.4 10.6 %collective-permute-start.6 = (bf16[128,1024]{1,0:T(8,128)(2,1)}, bf16[128,1024]{1,0:T(8,128)(2,1)}, u32[]{:S(2)}, u32[]{:S(2)}) collective-permute-start(bf16[128,1024]{1,0:T(8,128)(2,1)} %bitcast.10), channel_id=1, source_target_pairs={{0,16},{8,24},{16,0},{24,8},{1,17},{9,25},{17,1},{25,9},{2,18},{10... | collective-permute-start | bytes 786440 | tf_op jit(solution)/shard_map/ppermute | solution.py:867
  65.0 13.0 %collective-permute-start.5 = (bf16[128,1024]{1,0:T(8,128)(2,1)}, bf16[128,1024]{1,0:T(8,128)(2,1)}, u32[]{:S(2)}, u32[]{:S(2)}) collective-permute-start(bf16[128,1024]{1,0:T(8,128)(2,1)} %bitcast.10), channel_id=1, source_target_pairs={{0,8},{8,0},{16,24},{24,16},{1,9},{9,1},{17,25},{25,17},{2,10},{10... | collective-permute-start | bytes 786440 | tf_op jit(solution)/shard_map/ppermute | solution.py:864
  70.9 4.2 %collective-permute-start.2 = (bf16[128,1024]{1,0:T(8,128)(2,1)S(1)}, bf16[128,1024]{1,0:T(8,128)(2,1)S(1)}, u32[]{:S(2)}, u32[]{:S(2)}) collective-permute-start(bf16[128,1024]{1,0:T(8,128)(2,1)S(1)} %collective-permute-done.1), channel_id=1, source_target_pairs={{0,8},{8,0},{16,24},{24,16},{1,9},{9,1},{17,25},{25,17},{2,10},{10... | collective-permute-start | bytes 786440 | tf_op jit(solution)/shard_map/ppermute | solution.py:864
  70.9 7.1 %slice-start = ((s8[5767168]{0:T(1024)(128)(4,1)}), s8[4194304]{0:T(1024)(128)(4,1)S(1)}, s32[]{:S(2)}) async-start(s8[5767168]{0:T(1024)(128)(4,1)} %bitcast.94), calls=%async_computation | async-start | bytes 8388608
  75.0 2.9 collective-permute-start.7
  75.1 2.9 slice-start.1
  83.0 9.4 %collective-permute-start.8 = (bf16[2,128,1024]{2,1,0:T(8,128)(2,1)S(1)}, bf16[2,128,1024]{2,1,0:T(8,128)(2,1)S(1)}, u32[]{:S(2)}, u32[]{:S(2)}) collective-permute-start(bf16[2,128,1024]{2,1,0:T(8,128)(2,1)S(1)} %slice.66), channel_id=1, source_target_pairs={{0,8},{8,0},{16,24},{24,16},{1,9},{9,1},{17,25},{25,17},{2,10},{10... | collective-permute-start | bytes 1572872 | tf_op jit(solution)/shard_map/ppermute | solution.py:864
  84.7 9.4 %collective-permute-start.3 = (bf16[2,128,1024]{2,1,0:T(8,128)(2,1)S(1)}, bf16[2,128,1024]{2,1,0:T(8,128)(2,1)S(1)}, u32[]{:S(2)}, u32[]{:S(2)}) collective-permute-start(bf16[2,128,1024]{2,1,0:T(8,128)(2,1)S(1)} %slice.62), channel_id=1, source_target_pairs={{0,8},{8,0},{16,24},{24,16},{1,9},{9,1},{17,25},{25,17},{2,10},{10... | collective-permute-start | bytes 1572872 | tf_op jit(solution)/shard_map/ppermute | solution.py:864
  92.5 9.2 %collective-permute-start.9 = (bf16[128,1024]{1,0:T(8,128)(2,1)S(1)}, bf16[128,1024]{1,0:T(8,128)(2,1)S(1)}, u32[]{:S(2)}, u32[]{:S(2)}) collective-permute-start(bf16[128,1024]{1,0:T(8,128)(2,1)S(1)} %fusion.27), channel_id=1, source_target_pairs={{0,16},{8,24},{16,0},{24,8},{1,17},{9,25},{17,1},{25,9},{2,18},{10... | collective-permute-start | bytes 786440 | tf_op jit(solution)/shard_map/ppermute | solution.py:867
  94.3 12.6 %collective-permute-start.4 = (bf16[128,1024]{1,0:T(8,128)(2,1)S(1)}, bf16[128,1024]{1,0:T(8,128)(2,1)S(1)}, u32[]{:S(2)}, u32[]{:S(2)}) collective-permute-start(bf16[128,1024]{1,0:T(8,128)(2,1)S(1)} %fusion.26), channel_id=1, source_target_pairs={{0,16},{8,24},{16,0},{24,8},{1,17},{9,25},{17,1},{25,9},{2,18},{10... | collective-permute-start | bytes 786440 | tf_op jit(solution)/shard_map/ppermute | solution.py:867
  108.9 190.8 %copy-start.7 = (bf16[1024,1024]{1,0:T(8,128)(2,1)S(1)}, bf16[1024,1024]{1,0:T(8,128)(2,1)}, u32[]{:S(2)}) copy-start(bf16[1024,1024]{1,0:T(8,128)(2,1)} %param.16) | copy-start | bytes 6291460
  299.7 2.0 copy-start.8
  301.7 1.9 copy-start.9
  301.7 2.4 copy-start.6
  306.7 1.4 collective-permute-start.10
  308.2 3.7 %collective-permute-start.11 = (f32[20,128]{1,0:T(8,128)S(1)}, f32[20,128]{1,0:T(8,128)S(1)}, u32[]{:S(2)}, u32[]{:S(2)}) collective-permute-start(f32[20,128]{1,0:T(8,128)S(1)} %fusion.44), channel_id=1, source_target_pairs={{0,16},{8,24},{16,0},{24,8},{1,17},{9,25},{17,1},{25,9},{2,18},{10... | collective-permute-start | bytes 30728 | tf_op jit(solution)/shard_map/ppermute | solution.py:867
  311.9 3.7 %collective-permute-start.12 = (f32[20,128]{1,0:T(8,128)S(1)}, f32[20,128]{1,0:T(8,128)S(1)}, u32[]{:S(2)}, u32[]{:S(2)}) collective-permute-start(f32[20,128]{1,0:T(8,128)S(1)} %fusion.53), channel_id=1, source_target_pairs={{0,1},{1,0},{2,3},{3,2},{4,5},{5,4},{6,7},{7,6},{8,9},{9,8},{10,11... | collective-permute-start | bytes 30728 | tf_op jit(solution)/shard_map/ppermute | solution.py:962
  315.6 3.7 %collective-permute-start.13 = (f32[20,128]{1,0:T(8,128)S(1)}, f32[20,128]{1,0:T(8,128)S(1)}, u32[]{:S(2)}, u32[]{:S(2)}) collective-permute-start(f32[20,128]{1,0:T(8,128)S(1)} %add.129), channel_id=1, source_target_pairs={{0,2},{1,3},{2,0},{3,1},{4,6},{5,7},{6,4},{7,5},{8,10},{9,11},{10,... | collective-permute-start | bytes 30728 | tf_op jit(solution)/shard_map/ppermute | solution.py:962
  319.3 38.9 %collective-permute-start.14 = (f32[20,128]{1,0:T(8,128)S(1)}, f32[20,128]{1,0:T(8,128)S(1)}, u32[]{:S(2)}, u32[]{:S(2)}) collective-permute-start(f32[20,128]{1,0:T(8,128)S(1)} %add.130), channel_id=1, source_target_pairs={{0,4},{1,5},{2,6},{3,7},{4,0},{5,1},{6,2},{7,3},{8,12},{9,13},{10,... | collective-permute-start | bytes 30728 | tf_op jit(solution)/shard_map/ppermute | solution.py:962
  349.3 10.3 %copy-start.1 = (bf16[1024,1024]{1,0:T(8,128)(2,1)S(1)}, bf16[1024,1024]{1,0:T(8,128)(2,1)}, u32[]{:S(2)}) copy-start(bf16[1024,1024]{1,0:T(8,128)(2,1)} %param.19) | copy-start | bytes 6291460

commit v2 on v0

--- a/solution.py
+++ b/solution.py
@@ -1,11 +1,23 @@
+import functools
+import types
+
 import jax
 import jax.numpy as jnp
 from jax import lax
+from jax.experimental import pallas as pl
+from jax.experimental.pallas import tpu as pltpu
 from jax.sharding import PartitionSpec as P
 
 EPSILON = 1e-06
 MASKED = -1e30
 THRESHOLDS = (12, 16, 23, 32, 46, 64, 91)
+MESH = pl.DeviceIdType.MESH
+BF = jnp.bfloat16
+F32 = jnp.float32
+LANES = 128
+ANY = pl.BlockSpec(memory_space=pl.ANY)
+VMEM = pl.BlockSpec(memory_space=pltpu.VMEM)
+SMEM = pl.BlockSpec(memory_space=pltpu.SMEM)
 
 
 def bucket_of(relative):
@@ -17,21 +29,1144 @@
     return near_bucket + 16 * (relative > 0).astype(jnp.int32)
 
 
+def dot(left_mat, right_mat):
+    return jnp.dot(left_mat, right_mat, preferred_element_type=F32)
+
+
+def dot_rows(left_mat, right_mat):
+    return lax.dot_general(
+        left_mat, right_mat, (((0,), (0,)), ((), ())), preferred_element_type=F32
+    )
+
+
+def dot_cols(left_mat, right_mat):
+    return lax.dot_general(
+        left_mat, right_mat, (((1,), (1,)), ((), ())), preferred_element_type=F32
+    )
+
+
+def ring_place(index, count):
+    odd = index % 2
+    return (1 - odd) * (index // 2) + odd * ((2 * count - 1 - index) // 2)
+
+
+def ring_index(place, count):
+    late = place // (count // 2)
+    return (1 - late) * 2 * place + late * (2 * count - 1 - 2 * place)
+
+
+def greet(targets):
+    barrier = pltpu.get_barrier_semaphore()
+    for target in targets:
+        pl.semaphore_signal(barrier, inc=1, device_id=target, device_id_type=MESH)
+    pl.semaphore_wait(barrier, len(targets))
+
+
+def comm_params(collective_id, vmem=None):
+    return pltpu.CompilerParams(
+        collective_id=collective_id, has_side_effects=True, vmem_limit_bytes=vmem
+    )
+
+
+class Spot:
+    def __init__(self, count):
+        self.count = count
+        self.half = count // 2
+        self.me = lax.axis_index("seq")
+        self.dp = lax.axis_index("dp")
+        self.place = ring_place(self.me, count)
+        self.nexts = tuple((self.dp, self.at(step)) for step in (1, -1))
+        self.far_dp = (self.dp + 2) % 4
+        self.twin_dp = self.dp + 1 - 2 * (self.dp % 2)
+        self.far = (self.far_dp, self.me)
+        self.twin = (self.twin_dp, self.me)
+        self.others = tuple((self.dp, (self.me + step) % count) for step in range(1, count))
+
+    def at(self, step):
+        return ring_index((self.place + (step + self.count) % self.count) % self.count, self.count)
+
+    def back(self, way, hop):
+        return self.at(-hop if way == 0 else hop)
+
+
+def push(source, target, send_sem, recv_sem, device):
+    copy = pltpu.make_async_remote_copy(
+        src_ref=source,
+        dst_ref=target,
+        send_sem=send_sem,
+        recv_sem=recv_sem,
+        device_id=device,
+        device_id_type=MESH,
+    )
+    copy.start()
+    return copy
+
+
+class RingGather:
+    def __init__(self, spot, own, into, send_sems, recv_sems):
+        self.spot, self.own, self.into = spot, own, into
+        self.send_sems, self.recv_sems = send_sems, recv_sems
+        self.copies = {}
+
+    def pieces(self, way, hop):
+        return (0, 1) if hop < self.spot.half - 1 else (way,)
+
+    def forward(self, hop, way, piece):
+        spot = self.spot
+        if hop >= spot.half or piece not in self.pieces(way, hop):
+            return
+        origin = spot.back(way, hop)
+        target = self.into(origin, piece)
+        self.copies[hop, way, piece] = push(
+            self.own(piece) if hop == 0 else target,
+            target,
+            self.send_sems.at[way, hop, piece],
+            self.recv_sems.at[way, hop, piece],
+            spot.nexts[way],
+        )
+
+    def begin(self):
+        for piece in range(2):
+            for way in range(2):
+                self.forward(0, way, piece)
+
+    def step(self, hop):
+        for piece in range(2):
+            for way in range(2):
+                if (hop, way, piece) in self.copies:
+                    self.copies[hop, way, piece].wait_recv()
+                    self.forward(hop + 1, way, piece)
+
+    def finish(self):
+        for copy in self.copies.values():
+            copy.wait_send()
+
+
+class RingSum:
+    def __init__(self, spot, terms, buf, send_sems, recv_sems):
+        self.spot, self.terms, self.buf = spot, terms, buf
+        self.send_sems, self.recv_sems = send_sems, recv_sems
+        self.rows = terms.shape[1] // 2
+        self.copies = {}
+
+    def term(self, block, piece):
+        return self.terms.at[block, pl.ds(piece * self.rows, self.rows)]
+
+    def send(self, hop, way, piece, source):
+        self.copies[hop, way, piece] = push(
+            source,
+            self.buf.at[way, hop, piece],
+            self.send_sems.at[way, hop, piece],
+            self.recv_sems.at[way, hop, piece],
+            self.spot.nexts[way],
+        )
+
+    def block(self, way, hop):
+        step = self.spot.half - hop
+        return self.spot.at(step if way == 0 else -step)
+
+    def begin(self):
+        for way in range(2):
+            self.send(0, way, way, self.term(self.block(way, 0), way))
+        for way in range(2):
+            self.send(1, way, 1 - way, self.term(self.block(way, 1), 1 - way))
+
+    def step(self, hop):
+        for piece in range(2):
+            for way in range(2):
+                if (hop, way, piece) not in self.copies or hop + 1 >= self.spot.half:
+                    continue
+                self.copies[hop, way, piece].wait_recv()
+                term = self.term(self.block(way, hop + 1), piece)
+                self.buf[way, hop, piece] = (
+                    self.buf[way, hop, piece].astype(F32) + term[...].astype(F32)
+                ).astype(BF)
+                self.send(hop + 1, way, piece, self.buf.at[way, hop, piece])
+
+    def total(self, out):
+        last = self.spot.half - 1
+        for piece in range(2):
+            value = self.term(self.spot.me, piece)[...].astype(F32)
+            for way in range(2):
+                self.copies[last, way, piece].wait_recv()
+                value = value + self.buf[way, last, piece].astype(F32)
+            out[pl.ds(piece * self.rows, self.rows)] = value.astype(BF)
+
+    def finish(self):
+        for copy in self.copies.values():
+            copy.wait_send()
+
+
+class PairGather:
+    def __init__(self, spot, own_ref, buf, send_sems, recv_sems):
+        self.spot, self.buf = spot, buf
+        self.send_sems, self.recv_sems = send_sems, recv_sems
+        rows = own_ref.shape[0]
+        self.low, self.high = pl.ds(0, rows), pl.ds(rows, rows)
+        self.far = self.push(1, own_ref, buf.at[1, self.low], spot.far)
+        self.near = self.push(0, own_ref, buf.at[0, self.high], spot.twin)
+
+    def push(self, index, source, target, device):
+        return push(source, target, self.send_sems.at[index], self.recv_sems.at[index], device)
+
+    def relay(self):
+        self.far.wait_recv()
+        self.cross = self.push(
+            2, self.buf.at[1, self.low], self.buf.at[1, self.high], self.spot.twin
+        )
+
+    def finish(self):
+        for copy in (self.near, self.far, self.cross):
+            copy.wait_send()
+
+
+class PairSum:
+    def __init__(self, spot, kept, outs, ins, far_out, far_in, send_sems, recv_sems):
+        self.spot, self.kept, self.outs, self.ins = spot, kept, outs, ins
+        self.far_out, self.far_in = far_out, far_in
+        self.send_sems, self.recv_sems = send_sems, recv_sems
+        self.copies = []
+
+    def near(self, half):
+        self.copies.append(
+            push(
+                self.outs.at[half], self.ins.at[half],
+                self.send_sems.at[half], self.recv_sems.at[half], self.spot.twin,
+            )
+        )
+
+    def over(self):
+        self.copies[1].wait_recv()
+        self.far_out[...] = (self.kept[1] + self.ins[1].astype(F32)).astype(BF)
+        self.copies.append(
+            push(
+                self.far_out, self.far_in, self.send_sems.at[2], self.recv_sems.at[2], self.spot.far
+            )
+        )
+
+    def total(self):
+        self.copies[0].wait_recv()
+        self.copies[2].wait_recv()
+        return self.kept[0] + self.ins[0].astype(F32) + self.far_in[...].astype(F32)
+
+    def finish(self):
+        for copy in self.copies:
+            copy.wait_send()
+
+
+class MeshGather:
+    def __init__(self, spot, x_ref, o_ref, share, sems):
+        self.spot, self.x_ref, self.o_ref = spot, x_ref, o_ref
+        self.ring_s, self.ring_r, self.x_s, self.x_r, self.core_s, self.core_r = sems
+        rows = x_ref.shape[0]
+        first = rows * share // 100 // 32 * 32
+        cuts = (0, first // 2, first, first + (rows - first) // 2 // 16 * 16, rows)
+        self.windows = [
+            [pl.ds(cuts[2 * part + piece], cuts[2 * part + piece + 1] - cuts[2 * part + piece]) for piece in range(2)]
+            for part in range(2)
+        ]
+        self.ring, self.x, self.core = {}, {}, {}
+
+    def into(self, dp, origin, part, piece):
+        return self.o_ref.at[dp, origin, self.windows[part][piece]]
+
+    def pieces(self, way, hop):
+        return (0, 1) if hop < self.spot.half - 1 else (way,)
+
+    def pass_on(self, part, lane, hop, way, piece, source):
+        spot = self.spot
+        dp = spot.far_dp if lane else spot.dp
+        origin = spot.me if way is None else spot.back(way, hop)
+        target = self.into(dp, origin, part, piece)
+        source = target if source is None else source
+        slot = 0 if way is None else 2 * hop - 1 + way
+        for onward in (0, 1) if way is None else (way,):
+            if hop < spot.half and piece in self.pieces(onward, hop):
+                index = (2 * part if lane == 0 else 4) + onward
+                self.ring[part, lane, hop, onward, piece] = push(
+                    source, target,
+                    self.ring_s.at[index, hop, piece], self.ring_r.at[index, hop, piece],
+                    spot.nexts[onward],
+                )
+        if part == 0 and lane == 0:
+            self.x[part, slot, piece] = push(
+                source, target,
+                self.x_s.at[part, slot, piece], self.x_r.at[part, slot, piece], spot.far,
+            )
+        index = 2 * part + lane
+        self.core[part, lane, slot, piece] = push(
+            source, target,
+            self.core_s.at[index, slot, piece], self.core_r.at[index, slot, piece], spot.twin,
+        )
+
+    def begin(self):
+        spot = self.spot
+        for piece in range(2):
+            self.x[1, 0, piece] = push(
+                self.x_ref.at[self.windows[1][piece]],
+                self.into(spot.dp, spot.me, 1, piece),
+                self.x_s.at[1, 0, piece], self.x_r.at[1, 0, piece], spot.far,
+            )
+        for part in range(2):
+            for piece in range(2):
+                self.pass_on(part, 0, 0, None, piece, self.x_ref.at[self.windows[part][piece]])
+
+    def begin_far(self):
+        for piece in range(2):
+            self.x[1, 0, piece].wait_recv()
+            self.pass_on(1, 1, 0, None, piece, None)
+
+    def step(self, hop):
+        for piece in range(2):
+            for part, lane in ((0, 0), (1, 0), (1, 1)):
+                for way in range(2):
+                    key = (part, lane, hop, way, piece)
+                    if key in self.ring:
+                        self.ring[key].wait_recv()
+                        self.pass_on(part, lane, hop + 1, way, piece, None)
+
+    def step_far(self, hop):
+        spot = self.spot
+        for piece in range(2):
+            for way in (None,) if hop == 0 else range(2):
+                slot = 0 if way is None else 2 * hop - 1 + way
+                if (0, slot, piece) in self.x:
+                    self.x[0, slot, piece].wait_recv()
+                    origin = spot.me if way is None else spot.back(way, hop)
+                    target = self.into(spot.far_dp, origin, 0, piece)
+                    self.core[0, 1, slot, piece] = push(
+                        target, target,
+                        self.core_s.at[1, slot, piece], self.core_r.at[1, slot, piece], spot.twin,
+                    )
+
+    def finish(self):
+        for copy in self.core.values():
+            copy.wait_recv()
+        for copies in (self.ring, self.x, self.core):
+            for copy in copies.values():
+                copy.wait_send()
+
+
+def mesh_sems(count):
+    half = count // 2
+    return [
+        pltpu.SemaphoreType.DMA(shape)
+        for shape in ((6, half, 2), (2, 2 * half + 1, 2), (4, 2 * half + 1, 2))
+        for _ in range(2)
+    ]
+
+
+def near_buckets(rows):
+    shape = (rows, rows + 2 * LANES)
+    column = lax.broadcasted_iota(jnp.int32, shape, 1) - LANES
+    return bucket_of(column - lax.broadcasted_iota(jnp.int32, shape, 0))
+
+
+def strip_window(step, rows, length):
+    return pl.ds(pl.multiple_of(length - rows - step * rows, LANES), length)
+
+
+def scale_of(value):
+    return lax.rsqrt(jnp.mean(value * value, axis=-1, keepdims=True) + EPSILON)
+
+
+def row_block(origin, rows):
+    return pl.ds(pl.multiple_of(origin * rows, rows), rows)
+
+
+def exclusive(index, bit):
+    return index + bit - 2 * bit * ((index // bit) % 2)
+
+
+def layer_body(count, heads, depth, ff, names, *refs):
+    r = types.SimpleNamespace(**dict(zip(names, refs)))
+    spot = Spot(count)
+    hidden_ref, grad_ref = r.hidden, r.out_grad
+    rows, width = hidden_ref.shape
+    length = count * rows
+    inner = heads * depth
+    span = r.gate_w.shape[1]
+    odd = spot.dp % 2
+    ff_start = pl.multiple_of(spot.dp * ff - odd * (span - ff), span - ff)
+    own_columns = pl.ds(pl.multiple_of(spot.me * LANES, LANES), LANES)
+    greet(spot.others + (spot.far, spot.twin))
+
+    loads = {}
+
+    def load(name, source, target):
+        copy = pltpu.make_async_copy(source, target, r.load_sems.at[len(loads)])
+        copy.start()
+        loads[name] = copy
+
+    half_rows = rows // 2
+    ring = RingGather(
+        spot,
+        lambda piece: hidden_ref.at[pl.ds(piece * half_rows, half_rows)],
+        lambda origin, piece: r.row.at[origin, pl.ds(piece * half_rows, half_rows)],
+        r.row_s,
+        r.row_r,
+    )
+    ring.begin()
+    cots = PairGather(spot, grad_ref, r.cot, r.cot_s, r.cot_r)
+    sources = (r.query_weight, r.key_weight, r.value_weight)
+    for part, source in enumerate(sources):
+        load(
+            part,
+            source.at[:, pl.ds(pl.multiple_of(spot.me * inner, inner), inner)],
+            r.qkv_w.at[:, pl.ds(part * inner, inner)],
+        )
+    load("out", r.out_weight, r.out_w)
+    ff_columns = pl.ds(pl.multiple_of(ff_start, LANES), span)
+    load("gate", r.gate_weight.at[:, ff_columns], r.gate_w)
+    load("up", r.up_weight.at[:, ff_columns], r.up_w)
+    load("down", r.down_weight.at[pl.ds(ff_start, span)], r.down_w)
+    for part, source in enumerate(sources):
+        load(3 + part, source, r.full_w.at[part])
+
+    strip, qkv, normed, weights = r.strip, r.qkv, r.normed, r.weights
+    low = length - rows - LANES
+    bucket = near_buckets(rows)
+    near_span = bucket.shape[1]
+    table = r.table
+    for head in range(heads):
+        value = jnp.zeros(bucket.shape, F32)
+        for level in range(table.shape[1]):
+            value = jnp.where(bucket == level, table[head, level], value)
+        strip[head, :, :low] = jnp.full((rows, low), table[head, 15], F32)
+        strip[head, :, low : low + near_span] = value
+        after = strip.shape[2] - low - near_span
+        strip[head, :, low + near_span :] = jnp.full((rows, after), table[head, 31], F32)
+    gain_one, gain_two = r.gain_one[...], r.gain_two[...]
+
+    def project(origin, block):
+        value = block.astype(F32)
+        low_value = (value * scale_of(value) * gain_one).astype(BF)
+        mine = row_block(origin, rows)
+        normed[mine] = low_value
+        qkv[mine] = dot(low_value, r.qkv_w[...]).astype(BF)
+
+    for part in range(3):
+        loads[part].wait()
+    project(spot.me, hidden_ref[...])
+    for hop in range(spot.half):
+        ring.step(hop)
+        if hop < spot.half - 1:
+
+            def both(side, carry, hop=hop):
+                origin = spot.at((1 - 2 * side) * (hop + 1))
+                project(origin, r.row[origin])
+                return carry
+
+            lax.fori_loop(0, 2, both, 0)
+        else:
+            origin = spot.at(spot.half)
+            project(origin, r.row[origin])
+    cots.relay()
+    r.cot[0, :rows] = grad_ref[...]
+    mixed_heads, mixed = r.mixed_heads, r.mixed
+
+    def attend(target):
+        mine = row_block(target, rows)
+        same = r.column_ids[mine] == r.row_ids[...]
+        window = strip_window(target, rows, length)
+        for head in range(heads):
+            columns = slice(head * depth, (head + 1) * depth)
+            key = qkv[:, inner + head * depth : inner + (head + 1) * depth]
+            value = qkv[:, 2 * inner + head * depth : 2 * inner + (head + 1) * depth]
+            scores = dot_cols(qkv[mine, columns], key) + strip[head, :, window]
+            scores = jnp.where(same, scores, MASKED)
+            top = jnp.max(scores, axis=1, keepdims=True)
+            weight = jnp.exp(scores - top)
+            weight = weight * (1.0 / jnp.sum(weight, axis=1, keepdims=True))
+            weight = weight.astype(BF)
+            weights[head, mine] = weight
+            mixed_heads[mine, columns] = dot(weight, value).astype(BF)
+
+    def mixed_copy(step):
+        target = (spot.me + step) % count
+        return pltpu.make_async_remote_copy(
+            src_ref=mixed_heads.at[row_block(target, rows)],
+            dst_ref=mixed.at[:, own_columns],
+            send_sem=r.mixed_s.at[step - 1],
+            recv_sem=r.mixed_r.at[step - 1],
+            device_id=(spot.dp, target),
+            device_id_type=MESH,
+        )
+
+    def attend_and_send(step, carry):
+        attend((spot.me + step) % count)
+        mixed_copy(step).start()
+        return carry
+
+    lax.fori_loop(1, count, attend_and_send, 0)
+    attend(spot.me)
+    mixed[:, own_columns] = mixed_heads[row_block(spot.me, rows)]
+    mixed_copies = [mixed_copy(step) for step in range(1, count)]
+
+    loads["out"].wait()
+    for copy in mixed_copies:
+        copy.wait_recv()
+    inputs = hidden_ref[...].astype(F32)
+    middle_ref = r.middle
+    middle = inputs + dot(mixed[...], r.out_w[...])
+    middle_ref[...] = middle
+    tok, cot = r.tok, r.cot
+    tok[0, :rows] = (middle * scale_of(middle) * gain_two).astype(BF)
+    toks = PairGather(spot, tok.at[0, pl.ds(0, rows)], tok, r.tok_s, r.tok_r)
+    gate_w, up_w, down_w = r.gate_w, r.up_w, r.down_w
+    act, gate_g, up_g = r.act, r.gate_g, r.up_g
+    for name in ("gate", "up", "down"):
+        loads[name].wait()
+    both_rows = 2 * rows
+    chunk = 256
+    grads = PairSum(
+        spot, r.grad_kept, r.grad_outs, r.grad_ins, r.grad_far_out, r.grad_far_in,
+        r.grad_s, r.grad_r,
+    )
+    outs = PairSum(
+        spot, r.out_kept, r.out_outs, r.out_ins, r.out_far_out, r.out_far_in,
+        r.out_s, r.out_r,
+    )
+
+    def activate_half(half):
+        mine = pl.ds(half * both_rows, both_rows)
+
+        def tile(index, carry):
+            columns = row_block(index, chunk)
+            gate = dot(tok[half], gate_w[:, columns])
+            up = dot(tok[half], up_w[:, columns])
+            act_grad = dot_cols(cot[half], down_w[columns])
+            place = index * chunk + lax.broadcasted_iota(jnp.int32, (1, chunk), 1)
+            place = place - odd * (span - ff)
+            inside = (place >= 0) & (place < ff)
+            root = 0.7978845608028654
+            squared = gate * gate
+            bend = jnp.tanh(root * (gate + 0.044715 * gate * squared))
+            share = 0.5 * (1.0 + bend)
+            gelu = gate * share
+            slope = share + 0.5 * gate * (1.0 - bend * bend) * root * (
+                1.0 + 3 * 0.044715 * squared
+            )
+            act[mine, columns] = jnp.where(inside, gelu * up, 0.0).astype(BF)
+            gate_g[mine, columns] = jnp.where(inside, act_grad * up * slope, 0.0).astype(BF)
+            up_g[mine, columns] = jnp.where(inside, act_grad * gelu, 0.0).astype(BF)
+            return carry
+
+        lax.fori_loop(0, span // chunk, tile, 0)
+
+    def spread(pair_sum, half, product):
+        def tile(index, carry):
+            columns = row_block(index, chunk)
+            value = product(columns)
+            pair_sum.kept[half, :, columns] = value[:rows]
+            pair_sum.outs[half, :, columns] = value[rows:].astype(BF)
+            return carry
+
+        lax.fori_loop(0, width // chunk, tile, 0)
+        pair_sum.near(half)
+
+    def back_half(half):
+        mine = pl.ds(half * both_rows, both_rows)
+        spread(
+            grads,
+            half,
+            lambda columns: dot_cols(gate_g[mine], gate_w[columns])
+            + dot_cols(up_g[mine], up_w[columns]),
+        )
+
+    def out_half(half):
+        mine = pl.ds(half * both_rows, both_rows)
+        spread(outs, half, lambda columns: dot(act[mine], down_w[:, columns]))
+
+    cots.near.wait_recv()
+    cots.cross.wait_recv()
+    toks.near.wait_recv()
+    activate_half(0)
+    toks.relay()
+    back_half(0)
+    toks.cross.wait_recv()
+    activate_half(1)
+    back_half(1)
+
+    down_terms, pair_terms = r.down_terms, r.pair_terms
+    spare = span - ff
+
+    def down_tile(index, carry):
+        columns = row_block(index, LANES)
+        value = dot_rows(act[:both_rows], cot[0, :, columns]) + dot_rows(
+            act[both_rows:], cot[1, :, columns]
+        )
+        down_terms[index] = jnp.where(odd == 1, value[spare:], value[:ff]).astype(BF)
+        return carry
+
+    lax.fori_loop(0, count, down_tile, 0)
+    down_sum = RingSum(spot, down_terms, r.down_buf, r.down_s, r.down_r)
+    down_sum.begin()
+    grads.over()
+    full = ff // LANES
+    lane = lax.broadcasted_iota(jnp.int32, (LANES, LANES), 1)
+
+    def pair_tile(index, carry):
+        columns = row_block(index, LANES)
+        parts = []
+        for source in (gate_g, up_g):
+            parts.append(
+                dot_rows(tok[0, :, columns], source[:both_rows])
+                + dot_rows(tok[1, :, columns], source[both_rows:])
+            )
+        cut = lambda value, place: value[:, place * LANES : (place + 1) * LANES]
+        for part, value in enumerate(parts):
+            for place in range(full):
+                start = (part * full + place) * LANES
+                pair_terms[index, start : start + LANES] = jnp.where(
+                    odd == 1, cut(value, place + 1), cut(value, place)
+                ).astype(BF)
+        edges = [jnp.where(odd == 1, cut(value, 0), cut(value, full)) for value in parts]
+        turned = pltpu.roll(edges[1], LANES // 2, 1)
+        lower = (lane < LANES // 2).astype(jnp.int32)
+        pair_terms[index, 2 * full * LANES :] = jnp.where(lower == odd, turned, edges[0]).astype(BF)
+        return carry
+
+    lax.fori_loop(0, count, pair_tile, 0)
+    pair_sum = RingSum(spot, pair_terms, r.pair_buf, r.pair_s, r.pair_r)
+    pair_sum.begin()
+    down_sum.step(0)
+    out_half(0)
+    out_half(1)
+
+    normed_two_grad = grads.total()
+    middle = middle_ref[...]
+    scale_two = scale_of(middle)
+    lifted = gain_two * normed_two_grad
+    middle_grad = (
+        grad_ref[...].astype(F32)
+        + scale_two * lifted
+        - middle * (scale_two * scale_two * scale_two)
+        * jnp.mean(middle * lifted, axis=-1, keepdims=True)
+    )
+    middle_grad_ref = r.middle_grad
+    middle_grad_ref[...] = middle_grad
+    small = r.small
+    small[...] = jnp.zeros_like(small)
+    gain_grad = jnp.sum(normed_two_grad * middle * scale_two, axis=0, keepdims=True)
+    tiles = width // LANES
+    for tile in range(tiles):
+        small[tiles + tile : tiles + tile + 1] = gain_grad[:, tile * LANES : (tile + 1) * LANES]
+    branch, own_branch = r.branch, r.own_branch
+    own_branch[...] = middle_grad.astype(BF)
+    branches = RingGather(
+        spot,
+        lambda piece: own_branch.at[pl.ds(piece * half_rows, half_rows)],
+        lambda origin, piece: branch.at[origin, pl.ds(piece * half_rows, half_rows)],
+        r.branch_s,
+        r.branch_r,
+    )
+    branches.begin()
+    branch[spot.me] = own_branch[...]
+    outs.over()
+
+    keys, values, dqkv = r.keys, r.values, r.dqkv
+    strip[...] = jnp.zeros_like(strip)
+    keys[...] = jnp.zeros_like(keys)
+    values[...] = jnp.zeros_like(values)
+    own_out = r.out_w.at[row_block(spot.me, inner)]
+
+    def attend_back(origin):
+        mine = row_block(origin, rows)
+        window = strip_window(origin, rows, length)
+        mixed_grad = dot_cols(branch[origin], own_out[...]).astype(BF)
+        for head in range(heads):
+            columns = slice(head * depth, (head + 1) * depth)
+            key = qkv[:, inner + head * depth : inner + (head + 1) * depth]
+            value = qkv[:, 2 * inner + head * depth : 2 * inner + (head + 1) * depth]
+            grad = mixed_grad[:, columns]
+            weight_low = weights[head, mine]
+            weight = weight_low.astype(F32)
+            scaled = weight * dot_cols(grad, value)
+            score_grad = scaled - weight * jnp.sum(scaled, axis=1, keepdims=True)
+            strip[head, :, window] += score_grad
+            score_low = score_grad.astype(BF)
+            dqkv[mine, columns] = dot(score_low, key).astype(BF)
+            keys[:, columns] += dot_rows(score_low, qkv[mine, columns])
+            values[:, columns] += dot_rows(weight_low, grad)
+
+    down_sum.step(1)
+    attend_back(spot.me)
+    pair_sum.step(0)
+    block_out = middle + outs.total()
+    r.block_out[...] = block_out.astype(BF)
+    mesh_sets = [r.gather_sems[6 * index : 6 * index + 6] for index in range(3)]
+    for hop in range(spot.half):
+        branches.step(hop)
+        if hop == 0:
+            down_sum.step(2)
+        if hop == 1:
+            down_sum.total(r.down_block)
+            down = MeshGather(spot, r.down_block, r.down_all, SHARES[0], mesh_sets[0])
+            down.begin()
+            load("down_own", r.down_block, r.down_all.at[spot.dp, spot.me])
+        if hop:
+            pair_sum.step(hop)
+        if hop == 2:
+            down.begin_far()
+        if hop < spot.half - 1:
+
+            def both_back(side, carry, hop=hop):
+                attend_back(spot.at((1 - 2 * side) * (hop + 1)))
+                return carry
+
+            lax.fori_loop(0, 2, both_back, 0)
+        else:
+            attend_back(spot.at(spot.half))
+        if hop >= 2:
+            down.step(hop - 2)
+            down.step_far(hop - 2)
+
+    dqkv[:, inner : 2 * inner] = keys[...].astype(BF)
+    dqkv[:, 2 * inner :] = values[...].astype(BF)
+    own_dqkv = r.own_dqkv
+    trades = []
+    for index, device in enumerate(spot.others):
+        for part in range(3):
+            trades.append(
+                push(
+                    dqkv.at[row_block(device[1], rows), pl.ds(part * LANES, LANES)],
+                    own_dqkv.at[part, :, own_columns],
+                    r.trade_s.at[index, part],
+                    r.trade_r.at[index, part],
+                    device,
+                )
+            )
+    for part in range(3):
+        own_dqkv[part, :, own_columns] = dqkv[
+            row_block(spot.me, rows), part * LANES : (part + 1) * LANES
+        ]
+    pair_sum.total(r.pair_block)
+    pair = MeshGather(spot, r.pair_block, r.pair_all, SHARES[1], mesh_sets[1])
+    pair.begin()
+    load("pair_own", r.pair_block, r.pair_all.at[spot.dp, spot.me])
+
+    packed = r.packed
+    quarter, slim = width // 4, inner // 4
+
+    def quarter_block(index, carry):
+        block = dot_rows(normed[:, row_block(index, quarter)], dqkv[...])
+        for part in range(3):
+            packed[index, part * quarter : (part + 1) * quarter] = block[
+                :, part * LANES : (part + 1) * LANES
+            ]
+        return carry
+
+    lax.fori_loop(0, 4, quarter_block, 0)
+    for hop in (2, 3):
+        down.step(hop)
+        down.step_far(hop)
+
+    def out_tile(tile, carry):
+        terms = jnp.zeros((inner, LANES), F32)
+        for source in range(count):
+            terms = terms + dot_rows(
+                mixed_heads[source * rows : (source + 1) * rows],
+                branch[source, :, row_block(tile, LANES)],
+            )
+        for index in range(4):
+            base = pl.multiple_of(3 * quarter + tile * slim, slim)
+            packed[index, pl.ds(base, slim)] = terms[index * slim : (index + 1) * slim]
+        return carry
+
+    lax.fori_loop(0, tiles, out_tile, 0)
+    core, side = odd, spot.dp // 2
+    for index in range(2):
+        r.near_out[index] = packed[2 * index + 1 - core].astype(BF)
+    near = push(r.near_out, r.near_in, r.proj_s.at[0], r.proj_r.at[0], spot.twin)
+    pair.begin_far()
+    down.step_far(spot.half)
+    near.wait_recv()
+    r.far_out[...] = (
+        packed[2 * (1 - side) + core] + r.near_in[1 - side].astype(F32)
+    ).astype(BF)
+    far = push(r.far_out, r.far_in, r.proj_s.at[1], r.proj_r.at[1], spot.far)
+    pair.step(0)
+    pair.step_far(0)
+    far.wait_recv()
+    r.proj_block[...] = (
+        packed[2 * side + core] + r.near_in[side].astype(F32) + r.far_in[...].astype(F32)
+    ).astype(BF)
+    proj = MeshGather(spot, r.proj_block, r.proj_all, SHARES[2], mesh_sets[2])
+    proj.begin()
+    load("proj_own", r.proj_block, r.proj_all.at[spot.dp, spot.me])
+
+    for head in range(heads):
+        middle_part = strip[head, :, low : low + near_span]
+        before = jnp.sum(strip[head, :, :low], axis=0, keepdims=True)
+        after = jnp.sum(strip[head, :, low + near_span :], axis=0, keepdims=True)
+        levels = []
+        for level in range(table.shape[1]):
+            part = jnp.sum(jnp.where(bucket == level, middle_part, 0.0), axis=0, keepdims=True)
+            line = part[:, :LANES]
+            for tile in range(1, near_span // LANES):
+                line = line + part[:, tile * LANES : (tile + 1) * LANES]
+            edge = before if level == 15 else after if level == 31 else None
+            if edge is not None:
+                for tile in range(edge.shape[1] // LANES):
+                    line = line + edge[:, tile * LANES : (tile + 1) * LANES]
+            r.levels[level : level + 1] = line
+        sums = lax.dot_general(
+            jnp.ones((8, LANES), F32),
+            r.levels[...],
+            (((1,), (1,)), ((), ())),
+            precision=lax.Precision.HIGHEST,
+            preferred_element_type=F32,
+        )
+        small[pl.ds(2 * tiles + spot.me * heads + head, 1), : table.shape[1]] = sums[:1]
+
+    pair.step(1)
+    proj.begin_far()
+    pair.step_far(1)
+    for part in range(3):
+        loads[3 + part].wait()
+    for copy in trades:
+        copy.wait_recv()
+    normed_grad = dot_cols(own_dqkv[0], r.full_w[0])
+    for part in range(1, 3):
+        normed_grad = normed_grad + dot_cols(own_dqkv[part], r.full_w[part])
+    inputs = hidden_ref[...].astype(F32)
+    scale_one = scale_of(inputs)
+    raised = gain_one * normed_grad
+    r.hidden_grad[...] = (
+        middle_grad_ref[...]
+        + scale_one * raised
+        - inputs * (scale_one * scale_one * scale_one)
+        * jnp.mean(inputs * raised, axis=-1, keepdims=True)
+    )
+    gain_grad = jnp.sum(normed_grad * inputs * scale_one, axis=0, keepdims=True)
+    for tile in range(tiles):
+        small[tile : tile + 1] = gain_grad[:, tile * LANES : (tile + 1) * LANES]
+
+    partners = [spot.twin, spot.far]
+    bit = 1
+    while bit < count:
+        partners.append((spot.dp, exclusive(spot.me, bit)))
+        bit *= 2
+    small_out, small_in = r.small_out, r.small_in
+    small_copies = []
+
+    def small_send():
+        index = len(small_copies)
+        if index < len(partners):
+            small_out[index] = small[...]
+            small_copies.append(
+                push(
+                    small_out.at[index], small_in.at[index],
+                    r.small_s.at[index], r.small_r.at[index], partners[index],
+                )
+            )
+
+    def small_step():
+        if len(small_copies) <= len(partners) and small_copies:
+            index = len(small_copies) - 1
+            small_copies[index].wait_recv()
+            small[...] += small_in[index]
+            small_send()
+
+    small_send()
+    for hop in range(2, spot.half):
+        pair.step(hop)
+        pair.step_far(hop)
+        small_step()
+        proj.step(hop - 2)
+        proj.step_far(hop - 2)
+    pair.step_far(spot.half)
+    small_step()
+    for hop in range(spot.half - 2, spot.half):
+        proj.step(hop)
+        proj.step_far(hop)
+        small_step()
+    proj.step_far(spot.half)
+    r.small_sum[...] = small[...]
+    for name in ("down_own", "pair_own", "proj_own"):
+        loads[name].wait()
+    for copy in mixed_copies + trades + [near, far] + small_copies:
+        copy.wait_send()
+    for item in (ring, cots, toks, grads, outs, down_sum, pair_sum, branches, down, pair, proj):
+        item.finish()
+
+
+SHARES = (80, 70, 57)
+
+
+def layer(arrays, count, heads, depth, ff):
+    rows, width = arrays["hidden"].shape
+    length = count * rows
+    inner = heads * depth
+    half = count // 2
+    span = (ff + LANES - 1) // LANES * LANES
+    pair_rows = 2 * ff // LANES * rows
+    proj_rows = 3 * (width // 4) + inner // 4 * (width // LANES)
+    small_rows = 2 * (width // LANES) + count * heads
+    steps = 2 + (count - 1).bit_length()
+    dma = pltpu.SemaphoreType.DMA
+    specs = dict(
+        hidden=VMEM,
+        out_grad=VMEM,
+        gain_one=VMEM,
+        gain_two=VMEM,
+        column_ids=VMEM,
+        row_ids=VMEM,
+        table=SMEM,
+    )
+    shape = jax.ShapeDtypeStruct
+    results = dict(
+        block_out=(shape((rows, width), BF), VMEM),
+        hidden_grad=(shape((rows, width), F32), VMEM),
+        small_sum=(shape((small_rows, LANES), F32), VMEM),
+        down_all=(shape((4, count, ff, LANES), BF), ANY),
+        pair_all=(shape((4, count, pair_rows, LANES), BF), ANY),
+        proj_all=(shape((4, count, proj_rows, LANES), BF), ANY),
+    )
+    vm = pltpu.VMEM
+    ring_buf = lambda n: vm((2, half, 2, n // 2, LANES), BF)
+    pairs = {}
+    for name in ("grad", "out"):
+        pairs[name + "_kept"] = vm((2, rows, width), F32)
+        pairs[name + "_outs"] = vm((2, rows, width), BF)
+        pairs[name + "_ins"] = vm((2, rows, width), BF)
+        pairs[name + "_far_out"] = vm((rows, width), BF)
+        pairs[name + "_far_in"] = vm((rows, width), BF)
+        pairs[name + "_s"] = dma((3,))
+        pairs[name + "_r"] = dma((3,))
+    for name in ("cot", "tok"):
+        pairs[name] = vm((2, 2 * rows, width), BF)
+        pairs[name + "_s"] = dma((3,))
+        pairs[name + "_r"] = dma((3,))
+    for name in ("row", "branch"):
+        pairs[name] = vm((count, rows, width), BF)
+        pairs[name + "_s"] = dma((2, half, 2))
+        pairs[name + "_r"] = dma((2, half, 2))
+    for name, size in (("down", ff), ("pair", pair_rows)):
+        pairs[name + "_terms"] = vm((count, size, LANES), BF)
+        pairs[name + "_buf"] = ring_buf(size)
+        pairs[name + "_block"] = vm((size, LANES), BF)
+        pairs[name + "_s"] = dma((2, half, 2))
+        pairs[name + "_r"] = dma((2, half, 2))
+    scratch = dict(
+        **pairs,
+        strip=vm((heads, rows, 2 * length - rows), F32),
+        normed=vm((length, width), BF),
+        qkv=vm((length, 3 * inner), BF),
+        weights=vm((heads, length, length), BF),
+        mixed_heads=vm((length, inner), BF),
+        mixed=vm((rows, width), BF),
+        qkv_w=vm((width, 3 * inner), BF),
+        full_w=vm((3, width, width), BF),
+        out_w=vm((width, width), BF),
+        gate_w=vm((width, span), BF),
+        up_w=vm((width, span), BF),
+        down_w=vm((span, width), BF),
+        middle=vm((rows, width), F32),
+        middle_grad=vm((rows, width), F32),
+        act=vm((4 * rows, span), BF),
+        gate_g=vm((4 * rows, span), BF),
+        up_g=vm((4 * rows, span), BF),
+        own_branch=vm((rows, width), BF),
+        keys=vm((length, inner), F32),
+        values=vm((length, inner), F32),
+        dqkv=vm((length, 3 * inner), BF),
+        own_dqkv=vm((3, rows, width), BF),
+        packed=vm((4, proj_rows, LANES), F32),
+        near_out=vm((2, proj_rows, LANES), BF),
+        near_in=vm((2, proj_rows, LANES), BF),
+        far_out=vm((proj_rows, LANES), BF),
+        far_in=vm((proj_rows, LANES), BF),
+        proj_block=vm((proj_rows, LANES), BF),
+        levels=vm((arrays["table"].shape[1], LANES), F32),
+        small=vm((small_rows, LANES), F32),
+        small_out=vm((steps, small_rows, LANES), F32),
+        small_in=vm((steps, small_rows, LANES), F32),
+        load_sems=dma((16,)),
+        mixed_s=dma((count - 1,)),
+        mixed_r=dma((count - 1,)),
+        trade_s=dma((count - 1, 3)),
+        trade_r=dma((count - 1, 3)),
+        proj_s=dma((2,)),
+        proj_r=dma((2,)),
+        small_s=dma((steps,)),
+        small_r=dma((steps,)),
+    )
+    names = tuple(arrays) + tuple(results) + tuple(scratch)
+
+    def body(*refs):
+        plain = refs[: len(names)]
+        layer_body(
+            count, heads, depth, ff, names + ("gather_sems",), *plain, refs[len(names) :]
+        )
+
+    outs = pl.pallas_call(
+        body,
+        name="layer",
+        out_shape=tuple(value[0] for value in results.values()),
+        in_specs=[specs.get(name, ANY) for name in arrays],
+        out_specs=tuple(value[1] for value in results.values()),
+        scratch_shapes=list(scratch.values()) + mesh_sems(count) * 3,
+        compiler_params=comm_params(0, 60 << 20),
+    )(*arrays.values())
+    return types.SimpleNamespace(**dict(zip(results, outs)))
+
+
+def widen_pair_body(part, x_ref, gate_ref, up_ref):
+    rows = gate_ref.shape[0]
+    full, half = part // LANES, LANES // 2
+    for dp in range(x_ref.shape[0]):
+        base = dp * part
+        shift = half if dp % 2 else 0
+        for which, o_ref in enumerate((gate_ref, up_ref)):
+            for tile in range(full):
+                start = (which * full + tile) * rows
+                column = base + shift + tile * LANES
+                o_ref[:, column : column + LANES] = x_ref[dp, 0, start : start + rows].astype(F32)
+        edge = x_ref[dp, 0, 2 * full * rows :].astype(F32)
+        column = base if dp % 2 else base + full * LANES
+        gate_half = slice(half, LANES) if dp % 2 else slice(0, half)
+        up_half = slice(0, half) if dp % 2 else slice(half, LANES)
+        gate_ref[:, column : column + half] = edge[:, gate_half]
+        up_ref[:, column : column + half] = edge[:, up_half]
+
+
+def widen_pair(gathered, rows, part):
+    dps, count, size = gathered.shape[:3]
+    shape = jax.ShapeDtypeStruct((count * rows, dps * part), F32)
+    spec = pl.BlockSpec((rows, dps * part), lambda i: (i, 0))
+    return pl.pallas_call(
+        functools.partial(widen_pair_body, part),
+        name="widen_pair",
+        grid=(count,),
+        out_shape=(shape, shape),
+        in_specs=[pl.BlockSpec((dps, 1, size, LANES), lambda i: (0, i, 0, 0))],
+        out_specs=(spec, spec),
+        compiler_params=pltpu.CompilerParams(vmem_limit_bytes=48 << 20),
+    )(gathered)
+
+
+def widen_columns_body(x_ref, *o_refs):
+    rows = o_refs[0].shape[0]
+    for index, o_ref in enumerate(o_refs):
+        for source in range(x_ref.shape[1]):
+            o_ref[:, source * LANES : (source + 1) * LANES] = x_ref[
+                0, source, index * rows : (index + 1) * rows
+            ].astype(F32)
+
+
+def widen_columns(gathered, first, rows, outs, pieces):
+    dps, count = gathered.shape[:2]
+    size = rows // pieces
+    shape = jax.ShapeDtypeStruct((dps * rows, count * LANES), F32)
+    spec = pl.BlockSpec((size, count * LANES), lambda i, k: (i * pieces + k, 0))
+    base = first // (size * outs)
+    return pl.pallas_call(
+        widen_columns_body,
+        name="widen_columns",
+        grid=(dps, pieces),
+        out_shape=(shape,) * outs,
+        in_specs=[
+            pl.BlockSpec((1, count, size * outs, LANES), lambda i, k: (i, 0, base + k, 0))
+        ],
+        out_specs=(spec,) * outs,
+        compiler_params=pltpu.CompilerParams(vmem_limit_bytes=48 << 20),
+    )(gathered)
+
+
+def widen_rows_body(x_ref, o_ref):
+    dps, _, size, _ = x_ref.shape
+    tiles = o_ref.shape[1] // LANES
+    rows = size // tiles
+    for dp in range(dps):
+        for tile in range(tiles):
+            o_ref[dp * rows : (dp + 1) * rows, tile * LANES : (tile + 1) * LANES] = x_ref[
+                dp, 0, tile * rows : (tile + 1) * rows
+            ].astype(F32)
+
+
+def widen_rows(gathered, first, rows, width):
+    dps, count = gathered.shape[:2]
+    size = rows * (width // LANES)
+    base = first // size
+    return pl.pallas_call(
+        widen_rows_body,
+        name="widen_rows",
+        grid=(count,),
+        out_shape=jax.ShapeDtypeStruct((count * dps * rows, width), F32),
+        in_specs=[pl.BlockSpec((dps, 1, size, LANES), lambda i: (0, i, base, 0))],
+        out_specs=pl.BlockSpec((dps * rows, width), lambda i: (i, 0)),
+    )(gathered)
+
+
+def split_shards(
+    hidden,
+    group_ids,
+    norm1_gain,
+    query_weight,
+    key_weight,
+    value_weight,
+    out_weight,
+    relative_bias,
+    norm2_gain,
+    gate_weight,
+    up_weight,
+    down_projection_weight,
+    out_grad,
+    *,
+    count,
+):
+    width = hidden.shape[2]
+    levels, head_count = relative_bias.shape
+    depth = query_weight.shape[1] // head_count
+    heads = head_count // count
+    ff = gate_weight.shape[1] // 4
+    me = lax.axis_index("seq")
+    table = lax.dynamic_slice_in_dim(relative_bias, me * heads, heads, axis=1).T.astype(F32)
+    arrays = dict(
+        hidden=hidden[0],
+        out_grad=out_grad[0],
+        gain_one=norm1_gain.astype(F32)[None],
+        gain_two=norm2_gain.astype(F32)[None],
+        column_ids=group_ids[0][:, None],
+        row_ids=group_ids,
+        table=table,
+        query_weight=query_weight,
+        key_weight=key_weight,
+        value_weight=value_weight,
+        out_weight=out_weight,
+        gate_weight=gate_weight,
+        up_weight=up_weight,
+        down_weight=down_projection_weight,
+    )
+    out = layer(arrays, count, heads, depth, ff)
+    quarter, slim = width // 4, heads * depth // 4
+    gate_grad, up_grad = widen_pair(out.pair_all, width // count, ff)
+    (down_grad,) = widen_columns(out.down_all, 0, ff, 1, 2)
+    query_grad, key_grad, value_grad = widen_columns(out.proj_all, 0, quarter, 3, 1)
+    out_weight_grad = widen_rows(out.proj_all, 3 * quarter, slim, width)
+    small = out.small_sum
+    tiles = width // LANES
+    return (
+        out.block_out[None],
+        out.hidden_grad[None],
+        small[:tiles].reshape(-1),
+        query_grad,
+        key_grad,
+        value_grad,
+        out_weight_grad,
+        small[2 * tiles :, :levels].T,
+        small[tiles : 2 * tiles].reshape(-1),
+        gate_grad,
+        up_grad,
+        down_grad,
+    )
+
+
 def rms_norm(vector, norm_gain):
     return (
         vector * lax.rsqrt(jnp.mean(vector * vector, axis=-1, keepdims=True) + EPSILON) * norm_gain
-    )
-
-
-def dot_rows(left_mat, right_mat):
-    return lax.dot_general(
-        left_mat, right_mat, (((0,), (0,)), ((), ())), preferred_element_type=jnp.float32
-    )
-
-
-def dot_cols(left_mat, right_mat):
-    return lax.dot_general(
-        left_mat, right_mat, (((1,), (1,)), ((), ())), preferred_element_type=jnp.float32
     )
 
 
@@ -327,38 +1462,26 @@
 
 
 def solution(mesh):
-    placed = (
-        P("dp", "seq", None),
-        P("dp", None),
-        P(),
-        P(),
-        P(),
-        P(),
-        P(),
-        P(),
-        P(),
-        P(),
-        P(),
-        P(),
-        P("dp", "seq", None),
-    )
-    return jax.shard_map(
-        shards,
-        mesh=mesh,
-        in_specs=placed,
-        out_specs=(
-            P("dp", "seq", None),
-            P("dp", "seq", None),
-            P(),
-            P(),
-            P(),
-            P(),
-            P(),
-            P(),
-            P(),
-            P(),
-            P(),
-            P(),
-        ),
-        check_vma=False,
-    )
+    placed = (P("dp", "seq", None), P("dp", None)) + (P(),) * 10 + (P("dp", "seq", None),)
+    out_specs = (P("dp", "seq", None),) * 2 + (P(),) * 10
+    count = mesh.shape["seq"]
+
+    def run(*args):
+        hidden, query_weight, relative_bias = args[0], args[3], args[7]
+        head_count = relative_bias.shape[1]
+        inner = query_weight.shape[1] // count
+        fits = (
+            mesh.shape["dp"] == 4
+            and count % 2 == 0
+            and head_count % count == 0
+            and inner == LANES
+            and hidden.shape[2] == count * LANES
+            and hidden.shape[1] == count * LANES
+            and args[9].shape[1] % (4 * LANES) == 2 * LANES
+        )
+        body = functools.partial(split_shards, count=count) if fits else shards
+        return jax.shard_map(
+            body, mesh=mesh, in_specs=placed, out_specs=out_specs, check_vma=False
+        )(*args)
+
+    return run

time: 1870 us -> 294 us (0.16)
  waiting for transfers between devices: 1550 us -> 0 us
  Pallas kernels: 0 us -> 279 us
  matrix products: 116 us -> 0 us
  blocking collectives: 95.8 us -> 0 us
  other arithmetic: 62.8 us -> 3.8 us
    reduce_scatter x9 -> x0, waiting for transfers between devices: 1070 us -> none  [the longest x1 195 us: shards(): lax.psum_scatter(local_grads[8], 'seq', scatter_dimension=0, tiled=True)]
    all_gather x9 -> x0, waiting for transfers between devices: 401 us -> none  [the longest x1 89.4 us: shards(): lax.all_gather(shared[9].astype(jnp.bfloat16), 'seq', axis=0, tiled=True)]
    pallas_call x0 -> x5, Pallas kernels: none -> 279 us  [the longest x1 245 us: layer(): pl.pallas_call(body, name='layer', out_shape=tuple((value[0] for value in...]
    dot_general x29 -> x0, matrix products: 116 us -> none  [the longest x7 35.9 us: dot_rows(): lax.dot_general(left_mat, right_mat, (((0,), (0,)), ((), ())), preferred_...]
    psum x1 -> x0, waiting for transfers between devices: 70.6 us -> none  [shards(): lax.psum(shared[1].astype(jnp.bfloat16), 'dp').astype(jnp.float32)]
    convert_element_type x19 -> x1, other arithmetic: 56.6 us -> 1.25 us  [split_shards(): lax.dynamic_slice_in_dim(relative_bias, me * heads, heads, axis=1)]
    unnamed x2 -> x0, blocking collectives: 55.1 us -> none
    all_gather x2 -> x0, blocking collectives: 34.6 us -> none  [the longest x1 18.4 us: shards(): lax.all_gather(shared[6].astype(jnp.bfloat16), 'seq', axis=0, tiled=True)]
  transfers between devices with their start and end apart: 19 -> 0, of which waited for: 17 -> 0; matrix products, arithmetic and copies ran while one was open for 8% -> 0% of each run, Pallas kernels for 0% -> 0%
where the time goes in v2:
time: 294 us; the launch traced here: 289 us
  Pallas kernels  279 us (95%)
  local copies, waits for them, and re-layouts  5.09 us (2%)
  other arithmetic  3.8 us (1%)
    pallas_call x1, Pallas kernels, layer(): pl.pallas_call(body, name='layer', out_shape=tuple((value[0] for value in...  245 us
    pallas_call x1, Pallas kernels, widen_pair(): pl.pallas_call(functools.partial(widen_pair_body, part), name='widen_pair...  14.6 us
    pallas_call x2, Pallas kernels, widen_columns(): pl.pallas_call(widen_columns_body, name='widen_columns', grid=(dps, piece...  13.8 us
    pallas_call x1, Pallas kernels, widen_rows(): pl.pallas_call(widen_rows_body, name='widen_rows', grid=(count,), out_sha...  5.99 us

profile of v2, /device:TPU:0, one launch (start us, length us, event | category | flops | bytes accessed | tf_op | source)
XLA Modules:
  0.0 288.9 jit_solution(18414579929167164004)
XLA Ops:
  0.6 1.3 broadcast_in_dim.22
  1.9 1.3 broadcast_in_dim.23
  3.2 1.7 copy.25.refs_4_
  4.9 1.2 convert_bitcast_fusion.refs_6_
  6.1 245.0 %layer.1 = (bf16[128,1024]{1,0:T(8,128)(2,1)}, f32[128,1024]{1,0:T(8,128)}, f32[32,128]{1,0:T(8,128)}, bf16[4,8,704,128]{3,2,1,0:T(8,128)(2,1)}, bf16[4,8,1408,1...) custom-call(bf16[128,1024]{1,0:T(8,128)(2,1)} %bitcast.16, bf16[128,1024]{1,0:T(8,128)(2,1)} %bitcast.17, ...), custom_call_target="tpu_custom_call" | custom-call | tf_op jit(solution)/shard_map/layer/pallas_call | solution.py:1004
  251.1 1.3 slice_bitcast_fusion.1
  252.4 8.0 %widen_columns.2 = (f32[1024,1024]{1,0:T(8,128)}, f32[1024,1024]{1,0:T(8,128)}, f32[1024,1024]{1,0:T(8,128)}) custom-call(bf16[4,8,1024,128]{3,2,1,0:T(8,128)(2,1)} %get-tuple-element.26.x_ref), custom_call_target="tpu_custom_call" | custom-call | tf_op jit(solution)/shard_map/widen_columns/pallas_call | solution.py:1065
  260.4 0.0 copy-start.3
  260.4 6.0 %widen_rows.1 = f32[1024,1024]{1,0:T(8,128)} custom-call(bf16[4,8,1024,128]{3,2,1,0:T(8,128)(2,1)} %get-tuple-element.26.x_ref), custom_call_target="tpu_custom_call" | custom-call | tf_op jit(solution)/shard_map/widen_rows/pallas_call | solution.py:1093
  266.4 0.0 copy-done.3
  266.4 0.6 slice_bitcast_fusion
  267.0 0.0 copy-start
  267.0 14.6 %widen_pair.1 = (f32[1024,2816]{1,0:T(8,128)}, f32[1024,2816]{1,0:T(8,128)}) custom-call(bf16[4,8,1408,128]{3,2,1,0:T(8,128)(2,1)} %get-tuple-element.30.x_ref), custom_call_target="tpu_custom_call" | custom-call | tf_op jit(solution)/shard_map/widen_pair/pallas_call | solution.py:1039
  281.6 0.0 copy-done
  281.6 0.0 copy-start.2
  281.6 0.0 copy-start.1
  281.6 5.8 %widen_columns.3 = f32[2816,1024]{1,0:T(8,128)} custom-call(bf16[4,8,704,128]{3,2,1,0:T(8,128)(2,1)S(1)} %copy-done), custom_call_target="tpu_custom_call" | custom-call | tf_op jit(solution)/shard_map/widen_columns/pallas_call | solution.py:1065
  287.4 0.0 copy-done.2
  287.4 0.7 copy.28
  288.1 0.0 copy-done.1
  288.1 0.8 copy.29
Async XLA Ops:
  260.4 6.0 %copy-start.3 = (f32[32,128]{1,0:T(8,128)S(1)}, f32[32,128]{1,0:T(8,128)}, u32[]{:S(2)}) copy-start(f32[32,128]{1,0:T(8,128)} %get-tuple-element.25) | copy-start | bytes 49156
  267.0 14.6 %copy-start = (bf16[4,8,704,128]{3,2,1,0:T(8,128)(2,1)S(1)}, bf16[4,8,704,128]{3,2,1,0:T(8,128)(2,1)}, u32[]{:S(2)}) copy-start(bf16[4,8,704,128]{3,2,1,0:T(8,128)(2,1)} %get-tuple-element.33.x_ref) | copy-start | bytes 17301508
  281.6 5.8 %copy-start.2 = (bf16[128,1024]{1,0:T(8,128)(2,1)S(1)}, bf16[128,1024]{1,0:T(8,128)(2,1)}, u32[]{:S(2)}) copy-start(bf16[128,1024]{1,0:T(8,128)(2,1)} %get-tuple-element.23) | copy-start | bytes 786436
  281.6 6.5 %copy-start.1 = (f32[128,1024]{1,0:T(8,128)S(1)}, f32[128,1024]{1,0:T(8,128)}, u32[]{:S(2)}) copy-start(f32[128,1024]{1,0:T(8,128)} %get-tuple-element.24) | copy-start | bytes 1572868

commit v3 on v2

--- a/solution.py
+++ b/solution.py
@@ -17,7 +17,6 @@
 LANES = 128
 ANY = pl.BlockSpec(memory_space=pl.ANY)
 VMEM = pl.BlockSpec(memory_space=pltpu.VMEM)
-SMEM = pl.BlockSpec(memory_space=pltpu.SMEM)
 
 
 def bucket_of(relative):
@@ -102,11 +101,19 @@
     return copy
 
 
+def wait_all(like, sem):
+    pltpu.make_async_copy(like, like, sem).wait()
+
+
 class RingGather:
-    def __init__(self, spot, own, into, send_sems, recv_sems):
-        self.spot, self.own, self.into = spot, own, into
-        self.send_sems, self.recv_sems = send_sems, recv_sems
+    def __init__(self, spot, own, blocks, send_sem, recv_sems):
+        self.spot, self.own, self.blocks = spot, own, blocks
+        self.send_sem, self.recv_sems = send_sem, recv_sems
+        self.rows = blocks.shape[1] // 2
         self.copies = {}
+
+    def into(self, origin, piece):
+        return self.blocks.at[origin, pl.ds(piece * self.rows, self.rows)]
 
     def pieces(self, way, hop):
         return (0, 1) if hop < self.spot.half - 1 else (way,)
@@ -118,17 +125,16 @@
         origin = spot.back(way, hop)
         target = self.into(origin, piece)
         self.copies[hop, way, piece] = push(
-            self.own(piece) if hop == 0 else target,
+            self.own.at[pl.ds(piece * self.rows, self.rows)] if hop == 0 else target,
             target,
-            self.send_sems.at[way, hop, piece],
+            self.send_sem,
             self.recv_sems.at[way, hop, piece],
             spot.nexts[way],
         )
 
-    def begin(self):
-        for piece in range(2):
-            for way in range(2):
-                self.forward(0, way, piece)
+    def begin(self, piece):
+        for way in range(2):
+            self.forward(0, way, piece)
 
     def step(self, hop):
         for piece in range(2):
@@ -138,14 +144,13 @@
                     self.forward(hop + 1, way, piece)
 
     def finish(self):
-        for copy in self.copies.values():
-            copy.wait_send()
+        wait_all(self.blocks.at[pl.ds(0, self.spot.count - 1)], self.send_sem)
 
 
 class RingSum:
-    def __init__(self, spot, terms, buf, send_sems, recv_sems):
+    def __init__(self, spot, terms, buf, send_sem, recv_sems):
         self.spot, self.terms, self.buf = spot, terms, buf
-        self.send_sems, self.recv_sems = send_sems, recv_sems
+        self.send_sem, self.recv_sems = send_sem, recv_sems
         self.rows = terms.shape[1] // 2
         self.copies = {}
 
@@ -156,7 +161,7 @@
         self.copies[hop, way, piece] = push(
             source,
             self.buf.at[way, hop, piece],
-            self.send_sems.at[way, hop, piece],
+            self.send_sem,
             self.recv_sems.at[way, hop, piece],
             self.spot.nexts[way],
         )
@@ -193,8 +198,7 @@
             out[pl.ds(piece * self.rows, self.rows)] = value.astype(BF)
 
     def finish(self):
-        for copy in self.copies.values():
-            copy.wait_send()
+        wait_all(self.terms.at[pl.ds(0, self.spot.count - 1)], self.send_sem)
 
 
 class PairGather:
@@ -257,21 +261,25 @@
 class MeshGather:
     def __init__(self, spot, x_ref, o_ref, share, sems):
         self.spot, self.x_ref, self.o_ref = spot, x_ref, o_ref
-        self.ring_s, self.ring_r, self.x_s, self.x_r, self.core_s, self.core_r = sems
+        self.ring_s, self.ring_r, self.x_s, self.far_r, self.own_r, self.core_s, self.core_r = sems
         rows = x_ref.shape[0]
         first = rows * share // 100 // 32 * 32
         cuts = (0, first // 2, first, first + (rows - first) // 2 // 16 * 16, rows)
+        self.parts = (pl.ds(0, first), pl.ds(first, rows - first))
         self.windows = [
             [pl.ds(cuts[2 * part + piece], cuts[2 * part + piece + 1] - cuts[2 * part + piece]) for piece in range(2)]
             for part in range(2)
         ]
-        self.ring, self.x, self.core = {}, {}, {}
+        self.ring, self.x = {}, {}
 
     def into(self, dp, origin, part, piece):
         return self.o_ref.at[dp, origin, self.windows[part][piece]]
 
     def pieces(self, way, hop):
         return (0, 1) if hop < self.spot.half - 1 else (way,)
+
+    def to_core(self, source, target):
+        push(source, target, self.core_s, self.core_r, self.spot.twin)
 
     def pass_on(self, part, lane, hop, way, piece, source):
         spot = self.spot
@@ -282,22 +290,17 @@
         slot = 0 if way is None else 2 * hop - 1 + way
         for onward in (0, 1) if way is None else (way,):
             if hop < spot.half and piece in self.pieces(onward, hop):
-                index = (2 * part if lane == 0 else 4) + onward
                 self.ring[part, lane, hop, onward, piece] = push(
                     source, target,
-                    self.ring_s.at[index, hop, piece], self.ring_r.at[index, hop, piece],
+                    self.ring_s.at[part + lane],
+                    self.ring_r.at[2 * (part + lane) + onward, hop, piece],
                     spot.nexts[onward],
                 )
-        if part == 0 and lane == 0:
+        if part == 0:
             self.x[part, slot, piece] = push(
-                source, target,
-                self.x_s.at[part, slot, piece], self.x_r.at[part, slot, piece], spot.far,
+                source, target, self.x_s.at[0], self.far_r.at[slot, piece], spot.far
             )
-        index = 2 * part + lane
-        self.core[part, lane, slot, piece] = push(
-            source, target,
-            self.core_s.at[index, slot, piece], self.core_r.at[index, slot, piece], spot.twin,
-        )
+        self.to_core(source, target)
 
     def begin(self):
         spot = self.spot
@@ -305,7 +308,7 @@
             self.x[1, 0, piece] = push(
                 self.x_ref.at[self.windows[1][piece]],
                 self.into(spot.dp, spot.me, 1, piece),
-                self.x_s.at[1, 0, piece], self.x_r.at[1, 0, piece], spot.far,
+                self.x_s.at[1], self.own_r.at[piece], spot.far,
             )
         for part in range(2):
             for piece in range(2):
@@ -334,25 +337,23 @@
                     self.x[0, slot, piece].wait_recv()
                     origin = spot.me if way is None else spot.back(way, hop)
                     target = self.into(spot.far_dp, origin, 0, piece)
-                    self.core[0, 1, slot, piece] = push(
-                        target, target,
-                        self.core_s.at[1, slot, piece], self.core_r.at[1, slot, piece], spot.twin,
-                    )
+                    self.to_core(target, target)
 
     def finish(self):
-        for copy in self.core.values():
-            copy.wait_recv()
-        for copies in (self.ring, self.x, self.core):
-            for copy in copies.values():
-                copy.wait_send()
+        o_ref, count = self.o_ref, self.spot.count
+        wait_all(o_ref.at[pl.ds(0, 2)], self.core_r)
+        wait_all(o_ref.at[pl.ds(0, 2)], self.core_s)
+        for index in range(3):
+            wait_all(o_ref.at[0, pl.ds(0, count - 1), self.parts[min(index, 1)]], self.ring_s.at[index])
+        wait_all(o_ref.at[0, :, self.parts[0]], self.x_s.at[0])
+        wait_all(self.x_ref.at[self.parts[1]], self.x_s.at[1])
 
 
 def mesh_sems(count):
     half = count // 2
+    dma = pltpu.SemaphoreType.DMA
     return [
-        pltpu.SemaphoreType.DMA(shape)
-        for shape in ((6, half, 2), (2, 2 * half + 1, 2), (4, 2 * half + 1, 2))
-        for _ in range(2)
+        dma((3,)), dma((6, half, 2)), dma((2,)), dma((2 * half + 1, 2)), dma((2,)), dma(()), dma(())
     ]
 
 
@@ -389,7 +390,7 @@
     odd = spot.dp % 2
     ff_start = pl.multiple_of(spot.dp * ff - odd * (span - ff), span - ff)
     own_columns = pl.ds(pl.multiple_of(spot.me * LANES, LANES), LANES)
-    greet(spot.others + (spot.far, spot.twin))
+    greet(spot.nexts + (spot.far, spot.twin))
 
     loads = {}
 
@@ -398,16 +399,14 @@
         copy.start()
         loads[name] = copy
 
-    half_rows = rows // 2
     ring = RingGather(
         spot,
-        lambda piece: hidden_ref.at[pl.ds(piece * half_rows, half_rows)],
-        lambda origin, piece: r.row.at[origin, pl.ds(piece * half_rows, half_rows)],
+        hidden_ref,
+        r.row,
         r.row_s,
         r.row_r,
     )
-    ring.begin()
-    cots = PairGather(spot, grad_ref, r.cot, r.cot_s, r.cot_r)
+    ring.begin(0)
     sources = (r.query_weight, r.key_weight, r.value_weight)
     for part, source in enumerate(sources):
         load(
@@ -427,16 +426,24 @@
     low = length - rows - LANES
     bucket = near_buckets(rows)
     near_span = bucket.shape[1]
-    table = r.table
+    level_count, head_count = r.table.shape
+    chosen = lax.broadcasted_iota(jnp.int32, (head_count, LANES), 0) == (
+        spot.me * heads + lax.broadcasted_iota(jnp.int32, (head_count, LANES), 1)
+    )
+    table = dot(r.table[...], chosen.astype(BF))
     for head in range(heads):
+        entry = lambda level: table[level : level + 1, head : head + 1]
         value = jnp.zeros(bucket.shape, F32)
-        for level in range(table.shape[1]):
-            value = jnp.where(bucket == level, table[head, level], value)
-        strip[head, :, :low] = jnp.full((rows, low), table[head, 15], F32)
+        for level in range(level_count):
+            value = jnp.where(bucket == level, entry(level), value)
+        strip[head, :, :low] = jnp.broadcast_to(entry(15), (rows, low))
         strip[head, :, low : low + near_span] = value
         after = strip.shape[2] - low - near_span
-        strip[head, :, low + near_span :] = jnp.full((rows, after), table[head, 31], F32)
-    gain_one, gain_two = r.gain_one[...], r.gain_two[...]
+        strip[head, :, low + near_span :] = jnp.broadcast_to(entry(31), (rows, after))
+    ring.begin(1)
+    cots = PairGather(spot, grad_ref, r.cot, r.cot_s, r.cot_r)
+    gain_one = r.gain_one[...].astype(F32)
+    gain_two = r.gain_two[...].astype(F32)
 
     def project(origin, block):
         value = block.astype(F32)
@@ -467,7 +474,8 @@
 
     def attend(target):
         mine = row_block(target, rows)
-        same = r.column_ids[mine] == r.row_ids[...]
+        turned_ids = jnp.broadcast_to(r.row_ids[:, mine], (LANES, rows)).T
+        same = turned_ids[:, :1] == r.row_ids[...]
         window = strip_window(target, rows, length)
         for head in range(heads):
             columns = slice(head * depth, (head + 1) * depth)
@@ -487,8 +495,8 @@
         return pltpu.make_async_remote_copy(
             src_ref=mixed_heads.at[row_block(target, rows)],
             dst_ref=mixed.at[:, own_columns],
-            send_sem=r.mixed_s.at[step - 1],
-            recv_sem=r.mixed_r.at[step - 1],
+            send_sem=r.mixed_s,
+            recv_sem=r.mixed_r,
             device_id=(spot.dp, target),
             device_id_type=MESH,
         )
@@ -501,11 +509,9 @@
     lax.fori_loop(1, count, attend_and_send, 0)
     attend(spot.me)
     mixed[:, own_columns] = mixed_heads[row_block(spot.me, rows)]
-    mixed_copies = [mixed_copy(step) for step in range(1, count)]
 
     loads["out"].wait()
-    for copy in mixed_copies:
-        copy.wait_recv()
+    wait_all(mixed.at[:, pl.ds(0, width - LANES)], r.mixed_r)
     inputs = hidden_ref[...].astype(F32)
     middle_ref = r.middle
     middle = inputs + dot(mixed[...], r.out_w[...])
@@ -629,7 +635,6 @@
 
     lax.fori_loop(0, count, pair_tile, 0)
     pair_sum = RingSum(spot, pair_terms, r.pair_buf, r.pair_s, r.pair_r)
-    pair_sum.begin()
     down_sum.step(0)
     out_half(0)
     out_half(1)
@@ -656,20 +661,23 @@
     own_branch[...] = middle_grad.astype(BF)
     branches = RingGather(
         spot,
-        lambda piece: own_branch.at[pl.ds(piece * half_rows, half_rows)],
-        lambda origin, piece: branch.at[origin, pl.ds(piece * half_rows, half_rows)],
+        own_branch,
+        branch,
         r.branch_s,
         r.branch_r,
     )
-    branches.begin()
+    branches.begin(0)
     branch[spot.me] = own_branch[...]
     outs.over()
-
-    keys, values, dqkv = r.keys, r.values, r.dqkv
+    keys, values, dqkv, packed = r.keys, r.values, r.dqkv, r.packed
     strip[...] = jnp.zeros_like(strip)
     keys[...] = jnp.zeros_like(keys)
     values[...] = jnp.zeros_like(values)
+    branches.begin(1)
+    packed[...] = jnp.zeros_like(packed)
+
     own_out = r.out_w.at[row_block(spot.me, inner)]
+    quarter, slim = width // 4, inner // 4
 
     def attend_back(origin):
         mine = row_block(origin, rows)
@@ -689,26 +697,31 @@
             dqkv[mine, columns] = dot(score_low, key).astype(BF)
             keys[:, columns] += dot_rows(score_low, qkv[mine, columns])
             values[:, columns] += dot_rows(weight_low, grad)
-
+        terms = dot_rows(mixed_heads[mine], branch[origin])
+        for tile in range(tiles):
+            for index in range(4):
+                base = 3 * quarter + tile * slim
+                packed[index, base : base + slim] += terms[
+                    index * slim : (index + 1) * slim, tile * LANES : (tile + 1) * LANES
+                ]
+        terms = dot_rows(normed[mine], dqkv[mine, :inner])
+        for index in range(4):
+            packed[index, :quarter] += terms[index * quarter : (index + 1) * quarter]
+
+    mesh_sets = [r.gather_sems[7 * index : 7 * index + 7] for index in range(3)]
+    attend_back(spot.me)
     down_sum.step(1)
-    attend_back(spot.me)
-    pair_sum.step(0)
-    block_out = middle + outs.total()
-    r.block_out[...] = block_out.astype(BF)
-    mesh_sets = [r.gather_sems[6 * index : 6 * index + 6] for index in range(3)]
+    r.block_out[...] = (middle + outs.total()).astype(BF)
     for hop in range(spot.half):
         branches.step(hop)
         if hop == 0:
             down_sum.step(2)
-        if hop == 1:
+        if hop == spot.half - 2:
+            pair_sum.begin()
             down_sum.total(r.down_block)
             down = MeshGather(spot, r.down_block, r.down_all, SHARES[0], mesh_sets[0])
             down.begin()
             load("down_own", r.down_block, r.down_all.at[spot.dp, spot.me])
-        if hop:
-            pair_sum.step(hop)
-        if hop == 2:
-            down.begin_far()
         if hop < spot.half - 1:
 
             def both_back(side, carry, hop=hop):
@@ -718,76 +731,48 @@
             lax.fori_loop(0, 2, both_back, 0)
         else:
             attend_back(spot.at(spot.half))
-        if hop >= 2:
-            down.step(hop - 2)
-            down.step_far(hop - 2)
 
     dqkv[:, inner : 2 * inner] = keys[...].astype(BF)
     dqkv[:, 2 * inner :] = values[...].astype(BF)
+
+    def quarter_block(index, carry):
+        block = dot_rows(normed[:, row_block(index, quarter)], dqkv[:, inner:])
+        for part in range(2):
+            packed[index, (part + 1) * quarter : (part + 2) * quarter] = block[
+                :, part * LANES : (part + 1) * LANES
+            ]
+        return carry
+
+    lax.fori_loop(0, 4, quarter_block, 0)
+    core, side = odd, spot.dp // 2
+    for index in range(2):
+        r.near_out[index] = packed[2 * index + 1 - core].astype(BF)
+    near = push(r.near_out, r.near_in, r.proj_s.at[0], r.proj_r.at[0], spot.twin)
+    pair_sum.step(0)
+    near.wait_recv()
+    r.far_out[...] = (
+        packed[2 * (1 - side) + core] + r.near_in[1 - side].astype(F32)
+    ).astype(BF)
+    far = push(r.far_out, r.far_in, r.proj_s.at[1], r.proj_r.at[1], spot.far)
+
     own_dqkv = r.own_dqkv
-    trades = []
-    for index, device in enumerate(spot.others):
+    for device in spot.others:
         for part in range(3):
-            trades.append(
-                push(
-                    dqkv.at[row_block(device[1], rows), pl.ds(part * LANES, LANES)],
-                    own_dqkv.at[part, :, own_columns],
-                    r.trade_s.at[index, part],
-                    r.trade_r.at[index, part],
-                    device,
-                )
+            push(
+                dqkv.at[row_block(device[1], rows), pl.ds(part * LANES, LANES)],
+                own_dqkv.at[part, :, own_columns],
+                r.trade_s,
+                r.trade_r,
+                device,
             )
     for part in range(3):
         own_dqkv[part, :, own_columns] = dqkv[
             row_block(spot.me, rows), part * LANES : (part + 1) * LANES
         ]
-    pair_sum.total(r.pair_block)
-    pair = MeshGather(spot, r.pair_block, r.pair_all, SHARES[1], mesh_sets[1])
-    pair.begin()
-    load("pair_own", r.pair_block, r.pair_all.at[spot.dp, spot.me])
-
-    packed = r.packed
-    quarter, slim = width // 4, inner // 4
-
-    def quarter_block(index, carry):
-        block = dot_rows(normed[:, row_block(index, quarter)], dqkv[...])
-        for part in range(3):
-            packed[index, part * quarter : (part + 1) * quarter] = block[
-                :, part * LANES : (part + 1) * LANES
-            ]
-        return carry
-
-    lax.fori_loop(0, 4, quarter_block, 0)
-    for hop in (2, 3):
-        down.step(hop)
-        down.step_far(hop)
-
-    def out_tile(tile, carry):
-        terms = jnp.zeros((inner, LANES), F32)
-        for source in range(count):
-            terms = terms + dot_rows(
-                mixed_heads[source * rows : (source + 1) * rows],
-                branch[source, :, row_block(tile, LANES)],
-            )
-        for index in range(4):
-            base = pl.multiple_of(3 * quarter + tile * slim, slim)
-            packed[index, pl.ds(base, slim)] = terms[index * slim : (index + 1) * slim]
-        return carry
-
-    lax.fori_loop(0, tiles, out_tile, 0)
-    core, side = odd, spot.dp // 2
-    for index in range(2):
-        r.near_out[index] = packed[2 * index + 1 - core].astype(BF)
-    near = push(r.near_out, r.near_in, r.proj_s.at[0], r.proj_r.at[0], spot.twin)
-    pair.begin_far()
-    down.step_far(spot.half)
-    near.wait_recv()
-    r.far_out[...] = (
-        packed[2 * (1 - side) + core] + r.near_in[1 - side].astype(F32)
-    ).astype(BF)
-    far = push(r.far_out, r.far_in, r.proj_s.at[1], r.proj_r.at[1], spot.far)
-    pair.step(0)
-    pair.step_far(0)
+    down.begin_far()
+    down.step(0)
+    down.step_far(0)
+    pair_sum.step(1)
     far.wait_recv()
     r.proj_block[...] = (
         packed[2 * side + core] + r.near_in[side].astype(F32) + r.far_in[...].astype(F32)
@@ -795,13 +780,16 @@
     proj = MeshGather(spot, r.proj_block, r.proj_all, SHARES[2], mesh_sets[2])
     proj.begin()
     load("proj_own", r.proj_block, r.proj_all.at[spot.dp, spot.me])
+    down.step(1)
+    down.step_far(1)
+    pair_sum.step(2)
 
     for head in range(heads):
         middle_part = strip[head, :, low : low + near_span]
         before = jnp.sum(strip[head, :, :low], axis=0, keepdims=True)
         after = jnp.sum(strip[head, :, low + near_span :], axis=0, keepdims=True)
         levels = []
-        for level in range(table.shape[1]):
+        for level in range(level_count):
             part = jnp.sum(jnp.where(bucket == level, middle_part, 0.0), axis=0, keepdims=True)
             line = part[:, :LANES]
             for tile in range(1, near_span // LANES):
@@ -818,15 +806,24 @@
             precision=lax.Precision.HIGHEST,
             preferred_element_type=F32,
         )
-        small[pl.ds(2 * tiles + spot.me * heads + head, 1), : table.shape[1]] = sums[:1]
-
-    pair.step(1)
+        small[pl.ds(2 * tiles + spot.me * heads + head, 1), : level_count] = sums[:1]
+
+    pair_sum.total(r.pair_block)
+    pair = MeshGather(spot, r.pair_block, r.pair_all, SHARES[1], mesh_sets[1])
+    pair.begin()
+    load("pair_own", r.pair_block, r.pair_all.at[spot.dp, spot.me])
     proj.begin_far()
-    pair.step_far(1)
+    for hop in (2, 3):
+        down.step(hop)
+        down.step_far(hop)
+    down.step_far(spot.half)
+    proj.step(0)
+    proj.step_far(0)
+    pair.begin_far()
+
     for part in range(3):
         loads[3 + part].wait()
-    for copy in trades:
-        copy.wait_recv()
+    wait_all(own_dqkv.at[:, :, pl.ds(0, width - LANES)], r.trade_r)
     normed_grad = dot_cols(own_dqkv[0], r.full_w[0])
     for part in range(1, 3):
         normed_grad = normed_grad + dot_cols(own_dqkv[part], r.full_w[part])
@@ -870,29 +867,29 @@
             small_send()
 
     small_send()
-    for hop in range(2, spot.half):
+    for hop in range(spot.half):
         pair.step(hop)
         pair.step_far(hop)
         small_step()
-        proj.step(hop - 2)
-        proj.step_far(hop - 2)
+        if hop < spot.half - 1:
+            proj.step(hop + 1)
+            proj.step_far(hop + 1)
+        else:
+            proj.step_far(spot.half)
     pair.step_far(spot.half)
     small_step()
-    for hop in range(spot.half - 2, spot.half):
-        proj.step(hop)
-        proj.step_far(hop)
-        small_step()
-    proj.step_far(spot.half)
     r.small_sum[...] = small[...]
     for name in ("down_own", "pair_own", "proj_own"):
         loads[name].wait()
-    for copy in mixed_copies + trades + [near, far] + small_copies:
+    wait_all(mixed_heads.at[pl.ds(0, length - rows)], r.mixed_s)
+    wait_all(dqkv.at[pl.ds(0, length - rows)], r.trade_s)
+    for copy in [near, far] + small_copies:
         copy.wait_send()
     for item in (ring, cots, toks, grads, outs, down_sum, pair_sum, branches, down, pair, proj):
         item.finish()
 
 
-SHARES = (80, 70, 57)
+SHARES = (70, 57, 57)
 
 
 def layer(arrays, count, heads, depth, ff):
@@ -911,9 +908,8 @@
         out_grad=VMEM,
         gain_one=VMEM,
         gain_two=VMEM,
-        column_ids=VMEM,
         row_ids=VMEM,
-        table=SMEM,
+        table=VMEM,
     )
     shape = jax.ShapeDtypeStruct
     results = dict(
@@ -941,13 +937,13 @@
         pairs[name + "_r"] = dma((3,))
     for name in ("row", "branch"):
         pairs[name] = vm((count, rows, width), BF)
-        pairs[name + "_s"] = dma((2, half, 2))
+        pairs[name + "_s"] = dma(())
         pairs[name + "_r"] = dma((2, half, 2))
     for name, size in (("down", ff), ("pair", pair_rows)):
         pairs[name + "_terms"] = vm((count, size, LANES), BF)
         pairs[name + "_buf"] = ring_buf(size)
         pairs[name + "_block"] = vm((size, LANES), BF)
-        pairs[name + "_s"] = dma((2, half, 2))
+        pairs[name + "_s"] = dma(())
         pairs[name + "_r"] = dma((2, half, 2))
     scratch = dict(
         **pairs,
@@ -979,15 +975,15 @@
         far_out=vm((proj_rows, LANES), BF),
         far_in=vm((proj_rows, LANES), BF),
         proj_block=vm((proj_rows, LANES), BF),
-        levels=vm((arrays["table"].shape[1], LANES), F32),
+        levels=vm((arrays["table"].shape[0], LANES), F32),
         small=vm((small_rows, LANES), F32),
         small_out=vm((steps, small_rows, LANES), F32),
         small_in=vm((steps, small_rows, LANES), F32),
         load_sems=dma((16,)),
-        mixed_s=dma((count - 1,)),
-        mixed_r=dma((count - 1,)),
-        trade_s=dma((count - 1, 3)),
-        trade_r=dma((count - 1, 3)),
+        mixed_s=dma(()),
+        mixed_r=dma(()),
+        trade_s=dma(()),
+        trade_r=dma(()),
         proj_s=dma((2,)),
         proj_r=dma((2,)),
         small_s=dma((steps,)),
@@ -1013,91 +1009,91 @@
     return types.SimpleNamespace(**dict(zip(results, outs)))
 
 
-def widen_pair_body(part, x_ref, gate_ref, up_ref):
-    rows = gate_ref.shape[0]
+def widen_body(
+    part, down_ref, pair_ref, proj_ref, block_ref, hidden_ref, small_ref,
+    down_out, gate_out, up_out, query_out, key_out, value_out, out_out,
+    block_out, hidden_out, one_out, two_out, bias_out,
+):
     full, half = part // LANES, LANES // 2
-    for dp in range(x_ref.shape[0]):
+    down_out[...] = down_ref[:, 0].astype(F32)
+    for dp in range(pair_ref.shape[0]):
         base = dp * part
         shift = half if dp % 2 else 0
-        for which, o_ref in enumerate((gate_ref, up_ref)):
+        for which, o_ref in enumerate((gate_out, up_out)):
             for tile in range(full):
-                start = (which * full + tile) * rows
                 column = base + shift + tile * LANES
-                o_ref[:, column : column + LANES] = x_ref[dp, 0, start : start + rows].astype(F32)
-        edge = x_ref[dp, 0, 2 * full * rows :].astype(F32)
+                o_ref[:, column : column + LANES] = pair_ref[dp, 0, which * full + tile].astype(F32)
+        edge = pair_ref[dp, 0, 2 * full].astype(F32)
         column = base if dp % 2 else base + full * LANES
         gate_half = slice(half, LANES) if dp % 2 else slice(0, half)
         up_half = slice(0, half) if dp % 2 else slice(half, LANES)
-        gate_ref[:, column : column + half] = edge[:, gate_half]
-        up_ref[:, column : column + half] = edge[:, up_half]
-
-
-def widen_pair(gathered, rows, part):
-    dps, count, size = gathered.shape[:3]
-    shape = jax.ShapeDtypeStruct((count * rows, dps * part), F32)
-    spec = pl.BlockSpec((rows, dps * part), lambda i: (i, 0))
-    return pl.pallas_call(
-        functools.partial(widen_pair_body, part),
-        name="widen_pair",
-        grid=(count,),
-        out_shape=(shape, shape),
-        in_specs=[pl.BlockSpec((dps, 1, size, LANES), lambda i: (0, i, 0, 0))],
-        out_specs=(spec, spec),
+        gate_out[:, column : column + half] = edge[:, gate_half]
+        up_out[:, column : column + half] = edge[:, up_half]
+        slim = out_out.shape[0] // pair_ref.shape[0]
+        for tile in range(out_out.shape[1] // LANES):
+            out_out[dp * slim : (dp + 1) * slim, tile * LANES : (tile + 1) * LANES] = proj_ref[
+                dp, 0, 3, tile * slim : (tile + 1) * slim
+            ].astype(F32)
+    for index, o_ref in enumerate((query_out, key_out, value_out)):
+        o_ref[...] = proj_ref[:, 0, index].astype(F32)
+
+    @pl.when((pl.program_id(0) == 0) & (pl.program_id(1) == 0))
+    def _():
+        block_out[...] = block_ref[...]
+        hidden_out[...] = hidden_ref[...]
+        tiles = one_out.shape[0]
+        one_out[...] = small_ref[:tiles]
+        two_out[...] = small_ref[tiles : 2 * tiles]
+        bias_out[...] = small_ref[2 * tiles :].T[: bias_out.shape[0]]
+
+
+def widen(out, levels, ff):
+    rows, width = out.hidden_grad.shape
+    dps, count = out.down_all.shape[:2]
+    quarter = width // dps
+    small_rows = out.small_sum.shape[0]
+    tiles = width // LANES
+    heads = small_rows - 2 * tiles
+    pair = out.pair_all.reshape(dps, count, -1, rows, LANES)
+    proj = out.proj_all.reshape(dps, count, 4, quarter, LANES)
+    shape = lambda *dims: jax.ShapeDtypeStruct(dims, F32)
+    spec = pl.BlockSpec
+    whole = lambda *dims: spec(dims, lambda i, h: (0,) * len(dims))
+    wide = spec((rows // 2, dps * ff), lambda i, h: (2 * i + h, 0))
+    tall = lambda size: spec((dps, size // 2, LANES), lambda i, h: (0, h, i))
+    results = pl.pallas_call(
+        functools.partial(widen_body, ff),
+        name="widen",
+        grid=(count, 2),
+        out_shape=(
+            shape(dps, ff, width),
+            shape(width, dps * ff),
+            shape(width, dps * ff),
+            *[shape(dps, quarter, width)] * 3,
+            shape(width, width),
+            jax.ShapeDtypeStruct((rows, width), BF),
+            shape(rows, width),
+            shape(tiles, LANES),
+            shape(tiles, LANES),
+            shape(levels, heads),
+        ),
+        in_specs=[
+            spec((dps, 1, ff // 2, LANES), lambda i, h: (0, i, h, 0)),
+            spec((dps, 1, pair.shape[2], rows // 2, LANES), lambda i, h: (0, i, 0, h, 0)),
+            spec((dps, 1, 4, quarter // 2, LANES), lambda i, h: (0, i, 0, h, 0)),
+            whole(rows, width),
+            whole(rows, width),
+            whole(small_rows, LANES),
+        ],
+        out_specs=(
+            tall(ff), wide, wide, tall(quarter), tall(quarter), tall(quarter),
+            spec((width // count, width // 2), lambda i, h: (i, h)),
+            whole(rows, width), whole(rows, width), whole(tiles, LANES), whole(tiles, LANES),
+            whole(levels, heads),
+        ),
         compiler_params=pltpu.CompilerParams(vmem_limit_bytes=48 << 20),
-    )(gathered)
-
-
-def widen_columns_body(x_ref, *o_refs):
-    rows = o_refs[0].shape[0]
-    for index, o_ref in enumerate(o_refs):
-        for source in range(x_ref.shape[1]):
-            o_ref[:, source * LANES : (source + 1) * LANES] = x_ref[
-                0, source, index * rows : (index + 1) * rows
-            ].astype(F32)
-
-
-def widen_columns(gathered, first, rows, outs, pieces):
-    dps, count = gathered.shape[:2]
-    size = rows // pieces
-    shape = jax.ShapeDtypeStruct((dps * rows, count * LANES), F32)
-    spec = pl.BlockSpec((size, count * LANES), lambda i, k: (i * pieces + k, 0))
-    base = first // (size * outs)
-    return pl.pallas_call(
-        widen_columns_body,
-        name="widen_columns",
-        grid=(dps, pieces),
-        out_shape=(shape,) * outs,
-        in_specs=[
-            pl.BlockSpec((1, count, size * outs, LANES), lambda i, k: (i, 0, base + k, 0))
-        ],
-        out_specs=(spec,) * outs,
-        compiler_params=pltpu.CompilerParams(vmem_limit_bytes=48 << 20),
-    )(gathered)
-
-
-def widen_rows_body(x_ref, o_ref):
-    dps, _, size, _ = x_ref.shape
-    tiles = o_ref.shape[1] // LANES
-    rows = size // tiles
-    for dp in range(dps):
-        for tile in range(tiles):
-            o_ref[dp * rows : (dp + 1) * rows, tile * LANES : (tile + 1) * LANES] = x_ref[
-                dp, 0, tile * rows : (tile + 1) * rows
-            ].astype(F32)
-
-
-def widen_rows(gathered, first, rows, width):
-    dps, count = gathered.shape[:2]
-    size = rows * (width // LANES)
-    base = first // size
-    return pl.pallas_call(
-        widen_rows_body,
-        name="widen_rows",
-        grid=(count,),
-        out_shape=jax.ShapeDtypeStruct((count * dps * rows, width), F32),
-        in_specs=[pl.BlockSpec((dps, 1, size, LANES), lambda i: (0, i, base, 0))],
-        out_specs=pl.BlockSpec((dps * rows, width), lambda i: (i, 0)),
-    )(gathered)
+    )(out.down_all, pair, proj, out.block_out, out.hidden_grad, out.small_sum)
+    return results
 
 
 def split_shards(
@@ -1122,16 +1118,13 @@
     depth = query_weight.shape[1] // head_count
     heads = head_count // count
     ff = gate_weight.shape[1] // 4
-    me = lax.axis_index("seq")
-    table = lax.dynamic_slice_in_dim(relative_bias, me * heads, heads, axis=1).T.astype(F32)
     arrays = dict(
         hidden=hidden[0],
         out_grad=out_grad[0],
-        gain_one=norm1_gain.astype(F32)[None],
-        gain_two=norm2_gain.astype(F32)[None],
-        column_ids=group_ids[0][:, None],
+        gain_one=norm1_gain[None],
+        gain_two=norm2_gain[None],
         row_ids=group_ids,
-        table=table,
+        table=relative_bias,
         query_weight=query_weight,
         key_weight=key_weight,
         value_weight=value_weight,
@@ -1141,26 +1134,13 @@
         down_weight=down_projection_weight,
     )
     out = layer(arrays, count, heads, depth, ff)
-    quarter, slim = width // 4, heads * depth // 4
-    gate_grad, up_grad = widen_pair(out.pair_all, width // count, ff)
-    (down_grad,) = widen_columns(out.down_all, 0, ff, 1, 2)
-    query_grad, key_grad, value_grad = widen_columns(out.proj_all, 0, quarter, 3, 1)
-    out_weight_grad = widen_rows(out.proj_all, 3 * quarter, slim, width)
-    small = out.small_sum
-    tiles = width // LANES
+    down, gate, up, query, key, value, projected, block, grad, one, two, bias = widen(
+        out, levels, ff
+    )
+    square = lambda v: v.reshape(-1, width)
     return (
-        out.block_out[None],
-        out.hidden_grad[None],
-        small[:tiles].reshape(-1),
-        query_grad,
-        key_grad,
-        value_grad,
-        out_weight_grad,
-        small[2 * tiles :, :levels].T,
-        small[tiles : 2 * tiles].reshape(-1),
-        gate_grad,
-        up_grad,
-        down_grad,
+        block[None], grad[None], one.reshape(-1), square(query), square(key), square(value),
+        projected, bias, two.reshape(-1), gate, up, square(down),
     )
 
 

time: 294 us -> 271 us (0.922); the launches traced: 289 us -> 270 us
  Pallas kernels: 279 us -> 262 us
  other arithmetic: 3.8 us -> 0 us
    pallas_call x1, Pallas kernels: 245 us -> 234 us  [layer(): pl.pallas_call(body, name='layer', out_shape=tuple((value[0] for value in...]
    pallas_call x4 -> x1, Pallas kernels: 34.4 us -> 27.9 us  [widen(): pl.pallas_call(functools.partial(widen_body, ff), name='widen', grid=(cou...]
    unnamed x10 -> x8, local copies, waits for them, and re-layouts: 1.51 us -> 4.73 us
where the time goes in v3:
time: 271 us; the launch traced here: 270 us
  Pallas kernels  262 us (97%)
  local copies, waits for them, and re-layouts  7.29 us (3%)
    pallas_call x1, Pallas kernels, layer(): pl.pallas_call(body, name='layer', out_shape=tuple((value[0] for value in...  234 us
    pallas_call x1, Pallas kernels, widen(): pl.pallas_call(functools.partial(widen_body, ff), name='widen', grid=(cou...  27.9 us

profile of v3, /device:TPU:0, one launch (start us, length us, event | category | flops | bytes accessed | tf_op | source)
XLA Modules:
  0.0 270.2 jit_solution(3370437382045261872)
XLA Ops:
  0.6 1.3 broadcast_in_dim.12.refs_2_
  1.9 1.3 broadcast_in_dim.13.refs_3_
  3.2 1.4 copy.25.refs_5_
  4.6 234.3 %layer.1 = (bf16[128,1024]{1,0:T(8,128)(2,1)}, f32[128,1024]{1,0:T(8,128)}, f32[32,128]{1,0:T(8,128)}, bf16[4,8,704,128]{3,2,1,0:T(8,128)(2,1)}, bf16[4,8,1408,1...) custom-call(bf16[128,1024]{1,0:T(8,128)(2,1)} %bitcast.14, bf16[128,1024]{1,0:T(8,128)(2,1)} %bitcast.15, ...), custom_call_target="tpu_custom_call" | custom-call | tf_op jit(solution)/shard_map/layer/pallas_call | solution.py:1000
  238.9 0.0 copy-start
  238.9 1.0 copy-done
  239.9 0.0 copy-start.1
  239.9 0.9 copy-done.1
  240.9 0.0 copy-start.2
  240.9 0.7 copy-done.2
  241.6 27.9 %widen.1 = (f32[4,704,1024]{2,1,0:T(8,128)}, f32[1024,2816]{1,0:T(8,128)}, f32[1024,2816]{1,0:T(8,128)}, f32[4,256,1024]{2,1,0:T(8,128)}, f32[4,256,1024]{2,1,0:...) custom-call(bf16[4,8,704,128]{3,2,1,0:T(8,128)(2,1)} %get-tuple-elem, ...), custom_call_target="tpu_custom_call" | custom-call | tf_op jit(solution)/shard_map/widen/pallas_call | solution.py:1064
  269.5 0.7 copy.26
Async XLA Ops:
  238.9 1.0 copy-start
  239.9 0.9 copy-start.1
  240.9 0.7 copy-start.2

commit v4 on v3

--- a/solution.py
+++ b/solution.py
@@ -88,17 +88,26 @@
         return self.at(-hop if way == 0 else hop)
 
 
-def push(source, target, send_sem, recv_sem, device):
-    copy = pltpu.make_async_remote_copy(
-        src_ref=source,
-        dst_ref=target,
-        send_sem=send_sem,
-        recv_sem=recv_sem,
-        device_id=device,
-        device_id_type=MESH,
-    )
-    copy.start()
-    return copy
+def push(source, target, send_sem, recv_sem, device, split=1):
+    def copy_of(source, target):
+        return pltpu.make_async_remote_copy(
+            src_ref=source,
+            dst_ref=target,
+            send_sem=send_sem,
+            recv_sem=recv_sem,
+            device_id=device,
+            device_id_type=MESH,
+        )
+
+    whole = copy_of(source, target)
+    if split == 1:
+        whole.start()
+        return whole
+    rows = source.shape[0] // split
+    for index in range(split):
+        window = pl.ds(index * rows, rows)
+        copy_of(source.at[window], target.at[window]).start()
+    return whole
 
 
 def wait_all(like, sem):
@@ -106,8 +115,8 @@
 
 
 class RingGather:
-    def __init__(self, spot, own, blocks, send_sem, recv_sems):
-        self.spot, self.own, self.blocks = spot, own, blocks
+    def __init__(self, spot, own, blocks, send_sem, recv_sems, split=1):
+        self.spot, self.own, self.blocks, self.split = spot, own, blocks, split
         self.send_sem, self.recv_sems = send_sem, recv_sems
         self.rows = blocks.shape[1] // 2
         self.copies = {}
@@ -130,6 +139,7 @@
             self.send_sem,
             self.recv_sems.at[way, hop, piece],
             spot.nexts[way],
+            self.split,
         )
 
     def begin(self, piece):
@@ -422,28 +432,36 @@
     for part, source in enumerate(sources):
         load(3 + part, source, r.full_w.at[part])
 
-    strip, qkv, normed, weights = r.strip, r.qkv, r.normed, r.weights
+    qkv, normed, weights = r.qkv, r.normed, r.weights
+    both_rows = 2 * rows
     low = length - rows - LANES
     bucket = near_buckets(rows)
     near_span = bucket.shape[1]
-    level_count, head_count = r.table.shape
-    chosen = lax.broadcasted_iota(jnp.int32, (head_count, LANES), 0) == (
-        spot.me * heads + lax.broadcasted_iota(jnp.int32, (head_count, LANES), 1)
-    )
-    table = dot(r.table[...], chosen.astype(BF))
+    score_strip = r.score_strip
+    strip = score_strip.at[:, pl.ds(0, rows)]
+    score_low = length - both_rows - LANES
+    score_bucket = near_buckets(both_rows)
+    score_span = score_bucket.shape[1]
+    head_count, level_count = r.table.shape
+    chosen = lax.broadcasted_iota(jnp.int32, (8, head_count), 1) == (
+        spot.me * heads + lax.broadcasted_iota(jnp.int32, (8, head_count), 0)
+    )
+    table = dot(chosen.astype(BF), r.table[...])
     for head in range(heads):
-        entry = lambda level: table[level : level + 1, head : head + 1]
-        value = jnp.zeros(bucket.shape, F32)
+        entry = lambda level: table[head : head + 1, level : level + 1]
+        value = jnp.zeros(score_bucket.shape, F32)
         for level in range(level_count):
-            value = jnp.where(bucket == level, entry(level), value)
-        strip[head, :, :low] = jnp.broadcast_to(entry(15), (rows, low))
-        strip[head, :, low : low + near_span] = value
-        after = strip.shape[2] - low - near_span
-        strip[head, :, low + near_span :] = jnp.broadcast_to(entry(31), (rows, after))
+            value = jnp.where(score_bucket == level, entry(level), value)
+        after = score_strip.shape[2] - score_low - score_span
+        score_strip[head, :, :score_low] = jnp.broadcast_to(entry(15), (both_rows, score_low))
+        score_strip[head, :, score_low : score_low + score_span] = value
+        score_strip[head, :, score_low + score_span :] = jnp.broadcast_to(
+            entry(31), (both_rows, after)
+        )
     ring.begin(1)
     cots = PairGather(spot, grad_ref, r.cot, r.cot_s, r.cot_r)
-    gain_one = r.gain_one[...].astype(F32)
-    gain_two = r.gain_two[...].astype(F32)
+    gain_one = r.gain_one[...].astype(F32).reshape(1, width)
+    gain_two = r.gain_two[...].astype(F32).reshape(1, width)
 
     def project(origin, block):
         value = block.astype(F32)
@@ -468,20 +486,21 @@
         else:
             origin = spot.at(spot.half)
             project(origin, r.row[origin])
+    ring.finish()
     cots.relay()
     r.cot[0, :rows] = grad_ref[...]
     mixed_heads, mixed = r.mixed_heads, r.mixed
 
-    def attend(target):
-        mine = row_block(target, rows)
-        turned_ids = jnp.broadcast_to(r.row_ids[:, mine], (LANES, rows)).T
+    def attend(block):
+        mine = row_block(block, both_rows)
+        turned_ids = jnp.broadcast_to(r.row_ids[:, mine], (LANES, both_rows)).T
         same = turned_ids[:, :1] == r.row_ids[...]
-        window = strip_window(target, rows, length)
+        window = strip_window(block, both_rows, length)
         for head in range(heads):
             columns = slice(head * depth, (head + 1) * depth)
             key = qkv[:, inner + head * depth : inner + (head + 1) * depth]
             value = qkv[:, 2 * inner + head * depth : 2 * inner + (head + 1) * depth]
-            scores = dot_cols(qkv[mine, columns], key) + strip[head, :, window]
+            scores = dot_cols(qkv[mine, columns], key) + score_strip[head, :, window]
             scores = jnp.where(same, scores, MASKED)
             top = jnp.max(scores, axis=1, keepdims=True)
             weight = jnp.exp(scores - top)
@@ -490,24 +509,25 @@
             weights[head, mine] = weight
             mixed_heads[mine, columns] = dot(weight, value).astype(BF)
 
-    def mixed_copy(step):
-        target = (spot.me + step) % count
-        return pltpu.make_async_remote_copy(
-            src_ref=mixed_heads.at[row_block(target, rows)],
-            dst_ref=mixed.at[:, own_columns],
-            send_sem=r.mixed_s,
-            recv_sem=r.mixed_r,
-            device_id=(spot.dp, target),
-            device_id_type=MESH,
+    def mixed_send(target):
+        push(
+            mixed_heads.at[row_block(target, rows)],
+            mixed.at[:, own_columns],
+            r.mixed_s,
+            r.mixed_r,
+            (spot.dp, target),
         )
 
     def attend_and_send(step, carry):
-        attend((spot.me + step) % count)
-        mixed_copy(step).start()
+        block = (spot.me // 2 + step) % (count // 2)
+        attend(block)
+        for index in range(2):
+            mixed_send(2 * block + index)
         return carry
 
-    lax.fori_loop(1, count, attend_and_send, 0)
-    attend(spot.me)
+    lax.fori_loop(1, count // 2, attend_and_send, 0)
+    attend(spot.me // 2)
+    mixed_send(exclusive(spot.me, 1))
     mixed[:, own_columns] = mixed_heads[row_block(spot.me, rows)]
 
     loads["out"].wait()
@@ -523,7 +543,6 @@
     act, gate_g, up_g = r.act, r.gate_g, r.up_g
     for name in ("gate", "up", "down"):
         loads[name].wait()
-    both_rows = 2 * rows
     chunk = 256
     grads = PairSum(
         spot, r.grad_kept, r.grad_outs, r.grad_ins, r.grad_far_out, r.grad_far_in,
@@ -635,6 +654,7 @@
 
     lax.fori_loop(0, count, pair_tile, 0)
     pair_sum = RingSum(spot, pair_terms, r.pair_buf, r.pair_s, r.pair_r)
+    pair_sum.begin()
     down_sum.step(0)
     out_half(0)
     out_half(1)
@@ -657,7 +677,7 @@
     tiles = width // LANES
     for tile in range(tiles):
         small[tiles + tile : tiles + tile + 1] = gain_grad[:, tile * LANES : (tile + 1) * LANES]
-    branch, own_branch = r.branch, r.own_branch
+    branch, own_branch = r.row, r.own_branch
     own_branch[...] = middle_grad.astype(BF)
     branches = RingGather(
         spot,
@@ -665,16 +685,9 @@
         branch,
         r.branch_s,
         r.branch_r,
-    )
-    branches.begin(0)
-    branch[spot.me] = own_branch[...]
-    outs.over()
+        SPLITS[0],
+    )
     keys, values, dqkv, packed = r.keys, r.values, r.dqkv, r.packed
-    strip[...] = jnp.zeros_like(strip)
-    keys[...] = jnp.zeros_like(keys)
-    values[...] = jnp.zeros_like(values)
-    branches.begin(1)
-    packed[...] = jnp.zeros_like(packed)
 
     own_out = r.out_w.at[row_block(spot.me, inner)]
     quarter, slim = width // 4, inner // 4
@@ -709,136 +722,130 @@
             packed[index, :quarter] += terms[index * quarter : (index + 1) * quarter]
 
     mesh_sets = [r.gather_sems[7 * index : 7 * index + 7] for index in range(3)]
-    attend_back(spot.me)
-    down_sum.step(1)
-    r.block_out[...] = (middle + outs.total()).astype(BF)
-    for hop in range(spot.half):
-        branches.step(hop)
-        if hop == 0:
-            down_sum.step(2)
-        if hop == spot.half - 2:
-            pair_sum.begin()
-            down_sum.total(r.down_block)
-            down = MeshGather(spot, r.down_block, r.down_all, SHARES[0], mesh_sets[0])
-            down.begin()
-            load("down_own", r.down_block, r.down_all.at[spot.dp, spot.me])
-        if hop < spot.half - 1:
-
-            def both_back(side, carry, hop=hop):
-                attend_back(spot.at((1 - 2 * side) * (hop + 1)))
-                return carry
-
-            lax.fori_loop(0, 2, both_back, 0)
-        else:
-            attend_back(spot.at(spot.half))
-
-    dqkv[:, inner : 2 * inner] = keys[...].astype(BF)
-    dqkv[:, 2 * inner :] = values[...].astype(BF)
-
-    def quarter_block(index, carry):
-        block = dot_rows(normed[:, row_block(index, quarter)], dqkv[:, inner:])
-        for part in range(2):
-            packed[index, (part + 1) * quarter : (part + 2) * quarter] = block[
-                :, part * LANES : (part + 1) * LANES
+    down = MeshGather(spot, r.down_block, r.down_all, SHARES[0], mesh_sets[0])
+    pair = MeshGather(spot, r.pair_block, r.pair_all, SHARES[1], mesh_sets[1])
+    proj = MeshGather(spot, r.proj_block, r.proj_all, SHARES[2], mesh_sets[2])
+    core, side = odd, spot.dp // 2
+    own_dqkv = r.own_dqkv
+
+    def branch_start():
+        branches.begin(0)
+        branch[spot.me] = own_branch[...]
+        strip[...] = jnp.zeros_like(strip)
+        keys[...] = jnp.zeros_like(keys)
+        values[...] = jnp.zeros_like(values)
+        branches.begin(1)
+        packed[...] = jnp.zeros_like(packed)
+        attend_back(spot.me)
+
+    def finish_down():
+        down_sum.total(r.down_block)
+        down.begin()
+        load("down_own", r.down_block, r.down_all.at[spot.dp, spot.me])
+
+    def finish_pair():
+        pair_sum.total(r.pair_block)
+        pair.begin()
+        load("pair_own", r.pair_block, r.pair_all.at[spot.dp, spot.me])
+
+    def attend_pair(hop):
+        def both_back(index, carry):
+            attend_back(spot.at((1 - 2 * index) * (hop + 1)))
+            return carry
+
+        lax.fori_loop(0, 2, both_back, 0)
+
+    def finish_heads():
+        dqkv[:, inner : 2 * inner] = keys[...].astype(BF)
+        dqkv[:, 2 * inner :] = values[...].astype(BF)
+
+        def quarter_block(index, carry):
+            block = dot_rows(normed[:, row_block(index, quarter)], dqkv[:, inner:])
+            for part in range(2):
+                packed[index, (part + 1) * quarter : (part + 2) * quarter] = block[
+                    :, part * LANES : (part + 1) * LANES
+                ]
+            return carry
+
+        lax.fori_loop(0, 4, quarter_block, 0)
+        for index in range(2):
+            r.near_out[index] = packed[2 * index + 1 - core].astype(BF)
+        return push(r.near_out, r.near_in, r.proj_s.at[0], r.proj_r.at[0], spot.twin)
+
+    def heads_over():
+        near.wait_recv()
+        r.far_out[...] = (
+            packed[2 * (1 - side) + core] + r.near_in[1 - side].astype(F32)
+        ).astype(BF)
+        return push(r.far_out, r.far_in, r.proj_s.at[1], r.proj_r.at[1], spot.far, SPLITS[1])
+
+    def finish_proj():
+        far.wait_recv()
+        r.proj_block[...] = (
+            packed[2 * side + core] + r.near_in[side].astype(F32) + r.far_in[...].astype(F32)
+        ).astype(BF)
+        proj.begin()
+        load("proj_own", r.proj_block, r.proj_all.at[spot.dp, spot.me])
+
+    def trade():
+        for device in spot.others:
+            for part in range(3):
+                push(
+                    dqkv.at[row_block(device[1], rows), pl.ds(part * LANES, LANES)],
+                    own_dqkv.at[part, :, own_columns],
+                    r.trade_s,
+                    r.trade_r,
+                    device,
+                )
+        for part in range(3):
+            own_dqkv[part, :, own_columns] = dqkv[
+                row_block(spot.me, rows), part * LANES : (part + 1) * LANES
             ]
-        return carry
-
-    lax.fori_loop(0, 4, quarter_block, 0)
-    core, side = odd, spot.dp // 2
-    for index in range(2):
-        r.near_out[index] = packed[2 * index + 1 - core].astype(BF)
-    near = push(r.near_out, r.near_in, r.proj_s.at[0], r.proj_r.at[0], spot.twin)
-    pair_sum.step(0)
-    near.wait_recv()
-    r.far_out[...] = (
-        packed[2 * (1 - side) + core] + r.near_in[1 - side].astype(F32)
-    ).astype(BF)
-    far = push(r.far_out, r.far_in, r.proj_s.at[1], r.proj_r.at[1], spot.far)
-
-    own_dqkv = r.own_dqkv
-    for device in spot.others:
+
+    def finish_table():
+        for head in range(heads):
+            middle_part = strip[head, :, low : low + near_span]
+            before = jnp.sum(strip[head, :, :low], axis=0, keepdims=True)
+            after = jnp.sum(strip[head, :, low + near_span :], axis=0, keepdims=True)
+            levels = []
+            for level in range(level_count):
+                part = jnp.sum(jnp.where(bucket == level, middle_part, 0.0), axis=0, keepdims=True)
+                line = part[:, :LANES]
+                for tile in range(1, near_span // LANES):
+                    line = line + part[:, tile * LANES : (tile + 1) * LANES]
+                edge = before if level == 15 else after if level == 31 else None
+                if edge is not None:
+                    for tile in range(edge.shape[1] // LANES):
+                        line = line + edge[:, tile * LANES : (tile + 1) * LANES]
+                r.levels[level : level + 1] = line
+            sums = lax.dot_general(
+                jnp.ones((8, LANES), F32),
+                r.levels[...],
+                (((1,), (1,)), ((), ())),
+                precision=lax.Precision.HIGHEST,
+                preferred_element_type=F32,
+            )
+            small[pl.ds(2 * tiles + spot.me * heads + head, 1), : level_count] = sums[:1]
+
+    def finish_input():
         for part in range(3):
-            push(
-                dqkv.at[row_block(device[1], rows), pl.ds(part * LANES, LANES)],
-                own_dqkv.at[part, :, own_columns],
-                r.trade_s,
-                r.trade_r,
-                device,
-            )
-    for part in range(3):
-        own_dqkv[part, :, own_columns] = dqkv[
-            row_block(spot.me, rows), part * LANES : (part + 1) * LANES
-        ]
-    down.begin_far()
-    down.step(0)
-    down.step_far(0)
-    pair_sum.step(1)
-    far.wait_recv()
-    r.proj_block[...] = (
-        packed[2 * side + core] + r.near_in[side].astype(F32) + r.far_in[...].astype(F32)
-    ).astype(BF)
-    proj = MeshGather(spot, r.proj_block, r.proj_all, SHARES[2], mesh_sets[2])
-    proj.begin()
-    load("proj_own", r.proj_block, r.proj_all.at[spot.dp, spot.me])
-    down.step(1)
-    down.step_far(1)
-    pair_sum.step(2)
-
-    for head in range(heads):
-        middle_part = strip[head, :, low : low + near_span]
-        before = jnp.sum(strip[head, :, :low], axis=0, keepdims=True)
-        after = jnp.sum(strip[head, :, low + near_span :], axis=0, keepdims=True)
-        levels = []
-        for level in range(level_count):
-            part = jnp.sum(jnp.where(bucket == level, middle_part, 0.0), axis=0, keepdims=True)
-            line = part[:, :LANES]
-            for tile in range(1, near_span // LANES):
-                line = line + part[:, tile * LANES : (tile + 1) * LANES]
-            edge = before if level == 15 else after if level == 31 else None
-            if edge is not None:
-                for tile in range(edge.shape[1] // LANES):
-                    line = line + edge[:, tile * LANES : (tile + 1) * LANES]
-            r.levels[level : level + 1] = line
-        sums = lax.dot_general(
-            jnp.ones((8, LANES), F32),
-            r.levels[...],
-            (((1,), (1,)), ((), ())),
-            precision=lax.Precision.HIGHEST,
-            preferred_element_type=F32,
-        )
-        small[pl.ds(2 * tiles + spot.me * heads + head, 1), : level_count] = sums[:1]
-
-    pair_sum.total(r.pair_block)
-    pair = MeshGather(spot, r.pair_block, r.pair_all, SHARES[1], mesh_sets[1])
-    pair.begin()
-    load("pair_own", r.pair_block, r.pair_all.at[spot.dp, spot.me])
-    proj.begin_far()
-    for hop in (2, 3):
-        down.step(hop)
-        down.step_far(hop)
-    down.step_far(spot.half)
-    proj.step(0)
-    proj.step_far(0)
-    pair.begin_far()
-
-    for part in range(3):
-        loads[3 + part].wait()
-    wait_all(own_dqkv.at[:, :, pl.ds(0, width - LANES)], r.trade_r)
-    normed_grad = dot_cols(own_dqkv[0], r.full_w[0])
-    for part in range(1, 3):
-        normed_grad = normed_grad + dot_cols(own_dqkv[part], r.full_w[part])
-    inputs = hidden_ref[...].astype(F32)
-    scale_one = scale_of(inputs)
-    raised = gain_one * normed_grad
-    r.hidden_grad[...] = (
-        middle_grad_ref[...]
-        + scale_one * raised
-        - inputs * (scale_one * scale_one * scale_one)
-        * jnp.mean(inputs * raised, axis=-1, keepdims=True)
-    )
-    gain_grad = jnp.sum(normed_grad * inputs * scale_one, axis=0, keepdims=True)
-    for tile in range(tiles):
-        small[tile : tile + 1] = gain_grad[:, tile * LANES : (tile + 1) * LANES]
+            loads[3 + part].wait()
+        wait_all(own_dqkv.at[:, :, pl.ds(0, width - LANES)], r.trade_r)
+        normed_grad = dot_cols(own_dqkv[0], r.full_w[0])
+        for part in range(1, 3):
+            normed_grad = normed_grad + dot_cols(own_dqkv[part], r.full_w[part])
+        inputs = hidden_ref[...].astype(F32)
+        scale_one = scale_of(inputs)
+        raised = gain_one * normed_grad
+        r.hidden_grad[...] = (
+            middle_grad_ref[...]
+            + scale_one * raised
+            - inputs * (scale_one * scale_one * scale_one)
+            * jnp.mean(inputs * raised, axis=-1, keepdims=True)
+        )
+        gain_grad = jnp.sum(normed_grad * inputs * scale_one, axis=0, keepdims=True)
+        for tile in range(tiles):
+            small[tile : tile + 1] = gain_grad[:, tile * LANES : (tile + 1) * LANES]
 
     partners = [spot.twin, spot.far]
     bit = 1
@@ -866,17 +873,57 @@
             small[...] += small_in[index]
             small_send()
 
+    def pass_round(gather, hop):
+        gather.step(hop)
+        gather.step_far(hop)
+
+    outs.over()
+    down_sum.step(1)
+    pair_sum.step(0)
+    down_sum.step(2)
+    pair_sum.step(1)
+    finish_down()
+    pair_sum.step(2)
+    branch_start()
+    r.block_out[...] = (middle + outs.total()).astype(BF)
+    finish_pair()
+    branches.step(0)
+    down.begin_far()
+    attend_pair(0)
+    branches.step(1)
+    pair.begin_far()
+    attend_pair(1)
+    branches.step(2)
+    pass_round(down, 0)
+    attend_pair(2)
+    branches.step(3)
+    attend_back(spot.at(spot.half))
+    near = finish_heads()
+    pass_round(pair, 0)
+    far = heads_over()
+    pass_round(down, 1)
+    trade()
+    pass_round(pair, 1)
+    finish_proj()
+    pass_round(down, 2)
+    finish_table()
+    pass_round(pair, 2)
+    proj.begin_far()
+    pass_round(down, 3)
+    down.step_far(4)
+    pass_round(proj, 0)
+    pass_round(pair, 3)
+    finish_input()
     small_send()
-    for hop in range(spot.half):
-        pair.step(hop)
-        pair.step_far(hop)
-        small_step()
-        if hop < spot.half - 1:
-            proj.step(hop + 1)
-            proj.step_far(hop + 1)
-        else:
-            proj.step_far(spot.half)
-    pair.step_far(spot.half)
+    pair.step_far(4)
+    pass_round(proj, 1)
+    small_step()
+    pass_round(proj, 2)
+    small_step()
+    pass_round(proj, 3)
+    small_step()
+    proj.step_far(4)
+    small_step()
     small_step()
     r.small_sum[...] = small[...]
     for name in ("down_own", "pair_own", "proj_own"):
@@ -885,11 +932,12 @@
     wait_all(dqkv.at[pl.ds(0, length - rows)], r.trade_s)
     for copy in [near, far] + small_copies:
         copy.wait_send()
-    for item in (ring, cots, toks, grads, outs, down_sum, pair_sum, branches, down, pair, proj):
+    for item in (cots, toks, grads, outs, down_sum, pair_sum, branches, down, pair, proj):
         item.finish()
 
 
-SHARES = (70, 57, 57)
+SHARES = (80, 70, 57)
+SPLITS = (1, 1)
 
 
 def layer(arrays, count, heads, depth, ff):
@@ -935,8 +983,8 @@
         pairs[name] = vm((2, 2 * rows, width), BF)
         pairs[name + "_s"] = dma((3,))
         pairs[name + "_r"] = dma((3,))
+    pairs["row"] = vm((count, rows, width), BF)
     for name in ("row", "branch"):
-        pairs[name] = vm((count, rows, width), BF)
         pairs[name + "_s"] = dma(())
         pairs[name + "_r"] = dma((2, half, 2))
     for name, size in (("down", ff), ("pair", pair_rows)):
@@ -947,7 +995,7 @@
         pairs[name + "_r"] = dma((2, half, 2))
     scratch = dict(
         **pairs,
-        strip=vm((heads, rows, 2 * length - rows), F32),
+        score_strip=vm((heads, 2 * rows, 2 * length - rows), F32),
         normed=vm((length, width), BF),
         qkv=vm((length, 3 * inner), BF),
         weights=vm((heads, length, length), BF),
@@ -975,7 +1023,7 @@
         far_out=vm((proj_rows, LANES), BF),
         far_in=vm((proj_rows, LANES), BF),
         proj_block=vm((proj_rows, LANES), BF),
-        levels=vm((arrays["table"].shape[0], LANES), F32),
+        levels=vm((arrays["table"].shape[1], LANES), F32),
         small=vm((small_rows, LANES), F32),
         small_out=vm((steps, small_rows, LANES), F32),
         small_in=vm((steps, small_rows, LANES), F32),
@@ -1010,13 +1058,32 @@
 
 
 def widen_body(
-    part, down_ref, pair_ref, proj_ref, block_ref, hidden_ref, small_ref,
+    part, down_ref, pair_ref, proj_ref, slim_ref, block_ref, hidden_ref, small_ref,
     down_out, gate_out, up_out, query_out, key_out, value_out, out_out,
-    block_out, hidden_out, one_out, two_out, bias_out,
+    block_out, hidden_out, one_out, two_out, bias_out, small, sems,
 ):
+    copies = [
+        pltpu.make_async_copy(source, target, sems.at[index])
+        for index, (source, target) in enumerate(
+            ((small_ref, small), (block_ref, block_out), (hidden_ref, hidden_out))
+        )
+    ]
+    step = pl.program_id(0)
+
+    @pl.when(step == 0)
+    def _():
+        for copy in copies:
+            copy.start()
+
     full, half = part // LANES, LANES // 2
-    down_out[...] = down_ref[:, 0].astype(F32)
-    for dp in range(pair_ref.shape[0]):
+    for source in range(down_ref.shape[1]):
+        columns = slice(source * LANES, (source + 1) * LANES)
+        down_out[:, columns] = down_ref[0, source].astype(F32)
+        for index, o_ref in enumerate((query_out, key_out, value_out)):
+            o_ref[:, columns] = proj_ref[0, source, index].astype(F32)
+    dps = pair_ref.shape[0]
+    slim = out_out.shape[0] // dps
+    for dp in range(dps):
         base = dp * part
         shift = half if dp % 2 else 0
         for which, o_ref in enumerate((gate_out, up_out)):
@@ -1029,22 +1096,19 @@
         up_half = slice(0, half) if dp % 2 else slice(half, LANES)
         gate_out[:, column : column + half] = edge[:, gate_half]
         up_out[:, column : column + half] = edge[:, up_half]
-        slim = out_out.shape[0] // pair_ref.shape[0]
         for tile in range(out_out.shape[1] // LANES):
-            out_out[dp * slim : (dp + 1) * slim, tile * LANES : (tile + 1) * LANES] = proj_ref[
-                dp, 0, 3, tile * slim : (tile + 1) * slim
+            out_out[dp * slim : (dp + 1) * slim, tile * LANES : (tile + 1) * LANES] = slim_ref[
+                dp, 0, 0, tile * slim : (tile + 1) * slim
             ].astype(F32)
-    for index, o_ref in enumerate((query_out, key_out, value_out)):
-        o_ref[...] = proj_ref[:, 0, index].astype(F32)
-
-    @pl.when((pl.program_id(0) == 0) & (pl.program_id(1) == 0))
+
+    @pl.when(step == pl.num_programs(0) - 1)
     def _():
-        block_out[...] = block_ref[...]
-        hidden_out[...] = hidden_ref[...]
+        for copy in copies:
+            copy.wait()
         tiles = one_out.shape[0]
-        one_out[...] = small_ref[:tiles]
-        two_out[...] = small_ref[tiles : 2 * tiles]
-        bias_out[...] = small_ref[2 * tiles :].T[: bias_out.shape[0]]
+        one_out[...] = small[:tiles]
+        two_out[...] = small[tiles : 2 * tiles]
+        bias_out[...] = small[2 * tiles :, : bias_out.shape[1]]
 
 
 def widen(out, levels, ff):
@@ -1054,46 +1118,52 @@
     small_rows = out.small_sum.shape[0]
     tiles = width // LANES
     heads = small_rows - 2 * tiles
+    pieces = count // dps
     pair = out.pair_all.reshape(dps, count, -1, rows, LANES)
     proj = out.proj_all.reshape(dps, count, 4, quarter, LANES)
     shape = lambda *dims: jax.ShapeDtypeStruct(dims, F32)
     spec = pl.BlockSpec
-    whole = lambda *dims: spec(dims, lambda i, h: (0,) * len(dims))
-    wide = spec((rows // 2, dps * ff), lambda i, h: (2 * i + h, 0))
-    tall = lambda size: spec((dps, size // 2, LANES), lambda i, h: (0, h, i))
-    results = pl.pallas_call(
+    whole = lambda *dims: spec(dims, lambda i: (0,) * len(dims))
+    row = lambda size, span: spec((size, span), lambda i: (i, 0))
+    return pl.pallas_call(
         functools.partial(widen_body, ff),
         name="widen",
-        grid=(count, 2),
+        grid=(count,),
         out_shape=(
-            shape(dps, ff, width),
+            shape(dps * ff, width),
             shape(width, dps * ff),
             shape(width, dps * ff),
-            *[shape(dps, quarter, width)] * 3,
-            shape(width, width),
+            *[shape(width, width)] * 4,
             jax.ShapeDtypeStruct((rows, width), BF),
             shape(rows, width),
             shape(tiles, LANES),
             shape(tiles, LANES),
-            shape(levels, heads),
+            shape(heads, levels),
         ),
         in_specs=[
-            spec((dps, 1, ff // 2, LANES), lambda i, h: (0, i, h, 0)),
-            spec((dps, 1, pair.shape[2], rows // 2, LANES), lambda i, h: (0, i, 0, h, 0)),
-            spec((dps, 1, 4, quarter // 2, LANES), lambda i, h: (0, i, 0, h, 0)),
-            whole(rows, width),
-            whole(rows, width),
-            whole(small_rows, LANES),
+            spec((1, count, ff // pieces, LANES), lambda i: (i // pieces, 0, i % pieces, 0)),
+            spec((dps, 1, pair.shape[2], rows, LANES), lambda i: (0, i, 0, 0, 0)),
+            spec((1, count, 3, quarter // pieces, LANES), lambda i: (i // pieces, 0, 0, i % pieces, 0)),
+            spec((dps, 1, 1, quarter, LANES), lambda i: (0, i, 3, 0, 0)),
+            ANY,
+            ANY,
+            ANY,
         ],
         out_specs=(
-            tall(ff), wide, wide, tall(quarter), tall(quarter), tall(quarter),
-            spec((width // count, width // 2), lambda i, h: (i, h)),
-            whole(rows, width), whole(rows, width), whole(tiles, LANES), whole(tiles, LANES),
-            whole(levels, heads),
+            row(ff // pieces, width),
+            row(rows, dps * ff),
+            row(rows, dps * ff),
+            *[row(quarter // pieces, width)] * 3,
+            row(width // count, width),
+            ANY,
+            ANY,
+            whole(tiles, LANES),
+            whole(tiles, LANES),
+            whole(heads, levels),
         ),
-        compiler_params=pltpu.CompilerParams(vmem_limit_bytes=48 << 20),
-    )(out.down_all, pair, proj, out.block_out, out.hidden_grad, out.small_sum)
-    return results
+        scratch_shapes=[pltpu.VMEM((small_rows, LANES), F32), pltpu.SemaphoreType.DMA((3,))],
+        compiler_params=pltpu.CompilerParams(vmem_limit_bytes=56 << 20),
+    )(out.down_all, pair, proj, proj, out.block_out, out.hidden_grad, out.small_sum)
 
 
 def split_shards(
@@ -1121,10 +1191,10 @@
     arrays = dict(
         hidden=hidden[0],
         out_grad=out_grad[0],
-        gain_one=norm1_gain[None],
-        gain_two=norm2_gain[None],
+        gain_one=norm1_gain,
+        gain_two=norm2_gain,
         row_ids=group_ids,
-        table=relative_bias,
+        table=relative_bias.T,
         query_weight=query_weight,
         key_weight=key_weight,
         value_weight=value_weight,
@@ -1137,10 +1207,9 @@
     down, gate, up, query, key, value, projected, block, grad, one, two, bias = widen(
         out, levels, ff
     )
-    square = lambda v: v.reshape(-1, width)
     return (
-        block[None], grad[None], one.reshape(-1), square(query), square(key), square(value),
-        projected, bias, two.reshape(-1), gate, up, square(down),
+        block[None], grad[None], one.reshape(-1), query, key, value, projected, bias.T,
+        two.reshape(-1), gate, up, down,
     )
 
 

time: 271 us -> 261 us (0.963)
  local copies, waits for them, and re-layouts: 7.29 us -> 0 us
    unnamed x8 -> x0, local copies, waits for them, and re-layouts: 4.73 us -> none
    pallas_call x1, Pallas kernels: 234 us -> 230 us  [layer(): pl.pallas_call(body, name='layer', out_shape=tuple((value[0] for value in...]
where the time goes in v4:
time: 261 us
  Pallas kernels  260 us (100%)
    pallas_call x1, Pallas kernels, layer(): pl.pallas_call(body, name='layer', out_shape=tuple((value[0] for value in...  230 us
    pallas_call x1, Pallas kernels, widen(): pl.pallas_call(functools.partial(widen_body, ff), name='widen', grid=(cou...  29.6 us

profile of v4, /device:TPU:0, one launch (start us, length us, event | category | flops | bytes accessed | tf_op | source)
XLA Modules:
  0.0 260.8 jit_solution(16519440094120596696)
XLA Ops:
  0.6 230.4 %layer.1 = (bf16[128,1024]{1,0:T(8,128)(2,1)}, f32[128,1024]{1,0:T(8,128)}, f32[32,128]{1,0:T(8,128)}, bf16[4,8,704,128]{3,2,1,0:T(8,128)(2,1)}, bf16[4,8,1408,1...) custom-call(bf16[128,1024]{1,0:T(8,128)(2,1)} %bitcast.13, bf16[128,1024]{1,0:T(8,128)(2,1)} %bitcast.14, ...), custom_call_target="tpu_custom_call" | custom-call | tf_op jit(solution)/shard_map/layer/pallas_call | solution.py:1048
  231.0 29.6 %widen.1 = (f32[2816,1024]{1,0:T(8,128)}, f32[1024,2816]{1,0:T(8,128)}, f32[1024,2816]{1,0:T(8,128)}, f32[1024,1024]{1,0:T(8,128)}, f32[1024,1024]{1,0:T(8,128)}...) custom-call(bf16[4,8,704,128]{3,2,1,0:T(8,128)(2,1)} %get-tuple-elem, ...), custom_call_target="tpu_custom_call" | custom-call | tf_op jit(solution)/shard_map/widen/pallas_call | solution.py:1128

commit v5 on v4

--- a/solution.py
+++ b/solution.py
@@ -877,54 +877,54 @@
         gather.step(hop)
         gather.step_far(hop)
 
+    branch_start()
+    branches.step(0)
+    attend_pair(0)
+    down_sum.step(1)
+    branches.step(1)
+    attend_pair(1)
+    down_sum.step(2)
+    branches.step(2)
+    finish_down()
+    down.begin_far()
+    pair_sum.step(0)
+    attend_pair(2)
+    pass_round(down, 0)
+    pair_sum.step(1)
+    pass_round(down, 1)
+    branches.step(3)
     outs.over()
-    down_sum.step(1)
-    pair_sum.step(0)
-    down_sum.step(2)
-    pair_sum.step(1)
-    finish_down()
-    pair_sum.step(2)
-    branch_start()
-    r.block_out[...] = (middle + outs.total()).astype(BF)
-    finish_pair()
-    branches.step(0)
-    down.begin_far()
-    attend_pair(0)
-    branches.step(1)
-    pair.begin_far()
-    attend_pair(1)
-    branches.step(2)
-    pass_round(down, 0)
-    attend_pair(2)
-    branches.step(3)
     attend_back(spot.at(spot.half))
     near = finish_heads()
-    pass_round(pair, 0)
+    finish_table()
+    trade()
+    pass_round(down, 2)
     far = heads_over()
-    pass_round(down, 1)
-    trade()
-    pass_round(pair, 1)
+    pair_sum.step(2)
+    pass_round(down, 3)
+    finish_input()
     finish_proj()
-    pass_round(down, 2)
-    finish_table()
-    pass_round(pair, 2)
+    small_send()
     proj.begin_far()
-    pass_round(down, 3)
-    down.step_far(4)
+    small_step()
+    finish_pair()
     pass_round(proj, 0)
-    pass_round(pair, 3)
-    finish_input()
-    small_send()
-    pair.step_far(4)
+    pair.begin_far()
     pass_round(proj, 1)
     small_step()
+    pass_round(pair, 0)
+    r.block_out[...] = (middle + outs.total()).astype(BF)
+    down.step_far(4)
     pass_round(proj, 2)
     small_step()
+    pass_round(pair, 1)
+    small_step()
     pass_round(proj, 3)
+    pass_round(pair, 2)
+    pass_round(pair, 3)
     small_step()
     proj.step_far(4)
-    small_step()
-    small_step()
+    pair.step_far(4)
     r.small_sum[...] = small[...]
     for name in ("down_own", "pair_own", "proj_own"):
         loads[name].wait()
@@ -936,7 +936,7 @@
         item.finish()
 
 
-SHARES = (80, 70, 57)
+SHARES = (95, 35, 95)
 SPLITS = (1, 1)
 
 
@@ -1155,8 +1155,8 @@
             row(rows, dps * ff),
             *[row(quarter // pieces, width)] * 3,
             row(width // count, width),
-            ANY,
-            ANY,
+            whole(rows, width),
+            whole(rows, width),
             whole(tiles, LANES),
             whole(tiles, LANES),
             whole(heads, levels),

time: 261 us -> 248 us (0.950)
  Pallas kernels: 260 us -> 246 us
    pallas_call x1, Pallas kernels: 230 us -> 219 us  [layer(): pl.pallas_call(body, name='layer', out_shape=tuple((value[0] for value in...]
where the time goes in v5:
time: 248 us; the launch traced here: 247 us
  Pallas kernels  246 us (99%)
    pallas_call x1, Pallas kernels, layer(): pl.pallas_call(body, name='layer', out_shape=tuple((value[0] for value in...  219 us
    pallas_call x1, Pallas kernels, widen(): pl.pallas_call(functools.partial(widen_body, ff), name='widen', grid=(cou...  27 us

profile of v5, /device:TPU:0, one launch (start us, length us, event | category | flops | bytes accessed | tf_op | source)
XLA Modules:
  0.0 246.6 jit_solution(13850193046975511229)
XLA Ops:
  0.6 218.7 %layer.1 = (bf16[128,1024]{1,0:T(8,128)(2,1)}, f32[128,1024]{1,0:T(8,128)}, f32[32,128]{1,0:T(8,128)}, bf16[4,8,704,128]{3,2,1,0:T(8,128)(2,1)}, bf16[4,8,1408,1...) custom-call(bf16[128,1024]{1,0:T(8,128)(2,1)} %bitcast.13, bf16[128,1024]{1,0:T(8,128)(2,1)} %bitcast.14, ...), custom_call_target="tpu_custom_call" | custom-call | tf_op jit(solution)/shard_map/layer/pallas_call | solution.py:1048
  219.4 27.0 %widen.1 = (f32[2816,1024]{1,0:T(8,128)}, f32[1024,2816]{1,0:T(8,128)}, f32[1024,2816]{1,0:T(8,128)}, f32[1024,1024]{1,0:T(8,128)}, f32[1024,1024]{1,0:T(8,128)}...) custom-call(bf16[4,8,704,128]{3,2,1,0:T(8,128)(2,1)} %get-tuple-elem, ...), custom_call_target="tpu_custom_call" | custom-call | tf_op jit(solution)/shard_map/widen/pallas_call | solution.py:1128

commit v6 on v5

--- a/solution.py
+++ b/solution.py
@@ -58,7 +58,7 @@
     barrier = pltpu.get_barrier_semaphore()
     for target in targets:
         pl.semaphore_signal(barrier, inc=1, device_id=target, device_id_type=MESH)
-    pl.semaphore_wait(barrier, len(targets))
+    return lambda: pl.semaphore_wait(barrier, len(targets))
 
 
 def comm_params(collective_id, vmem=None):
@@ -400,7 +400,7 @@
     odd = spot.dp % 2
     ff_start = pl.multiple_of(spot.dp * ff - odd * (span - ff), span - ff)
     own_columns = pl.ds(pl.multiple_of(spot.me * LANES, LANES), LANES)
-    greet(spot.nexts + (spot.far, spot.twin))
+    all_in = greet(spot.nexts + (spot.far, spot.twin))
 
     loads = {}
 
@@ -416,7 +416,6 @@
         r.row_s,
         r.row_r,
     )
-    ring.begin(0)
     sources = (r.query_weight, r.key_weight, r.value_weight)
     for part, source in enumerate(sources):
         load(
@@ -458,6 +457,9 @@
         score_strip[head, :, score_low + score_span :] = jnp.broadcast_to(
             entry(31), (both_rows, after)
         )
+        if head == 0:
+            all_in()
+            ring.begin(0)
     ring.begin(1)
     cots = PairGather(spot, grad_ref, r.cot, r.cot_s, r.cot_r)
     gain_one = r.gain_one[...].astype(F32).reshape(1, width)
@@ -504,10 +506,11 @@
             scores = jnp.where(same, scores, MASKED)
             top = jnp.max(scores, axis=1, keepdims=True)
             weight = jnp.exp(scores - top)
-            weight = weight * (1.0 / jnp.sum(weight, axis=1, keepdims=True))
+            share = 1.0 / jnp.sum(weight, axis=1, keepdims=True)
+            r.shares[head, mine] = share
             weight = weight.astype(BF)
             weights[head, mine] = weight
-            mixed_heads[mine, columns] = dot(weight, value).astype(BF)
+            mixed_heads[mine, columns] = (dot(weight, value) * share).astype(BF)
 
     def mixed_send(target):
         push(
@@ -611,7 +614,6 @@
     back_half(0)
     toks.cross.wait_recv()
     activate_half(1)
-    back_half(1)
 
     down_terms, pair_terms = r.down_terms, r.pair_terms
     spare = span - ff
@@ -624,10 +626,12 @@
         down_terms[index] = jnp.where(odd == 1, value[spare:], value[:ff]).astype(BF)
         return carry
 
-    lax.fori_loop(0, count, down_tile, 0)
     down_sum = RingSum(spot, down_terms, r.down_buf, r.down_s, r.down_r)
-    down_sum.begin()
-    grads.over()
+
+    def down_ready():
+        lax.fori_loop(0, count, down_tile, 0)
+        down_sum.begin()
+
     full = ff // LANES
     lane = lax.broadcasted_iota(jnp.int32, (LANES, LANES), 1)
 
@@ -652,33 +656,37 @@
         pair_terms[index, 2 * full * LANES :] = jnp.where(lower == odd, turned, edges[0]).astype(BF)
         return carry
 
-    lax.fori_loop(0, count, pair_tile, 0)
     pair_sum = RingSum(spot, pair_terms, r.pair_buf, r.pair_s, r.pair_r)
-    pair_sum.begin()
-    down_sum.step(0)
-    out_half(0)
-    out_half(1)
-
-    normed_two_grad = grads.total()
-    middle = middle_ref[...]
-    scale_two = scale_of(middle)
-    lifted = gain_two * normed_two_grad
-    middle_grad = (
-        grad_ref[...].astype(F32)
-        + scale_two * lifted
-        - middle * (scale_two * scale_two * scale_two)
-        * jnp.mean(middle * lifted, axis=-1, keepdims=True)
-    )
-    middle_grad_ref = r.middle_grad
-    middle_grad_ref[...] = middle_grad
-    small = r.small
-    small[...] = jnp.zeros_like(small)
-    gain_grad = jnp.sum(normed_two_grad * middle * scale_two, axis=0, keepdims=True)
+
+    def pair_ready():
+        lax.fori_loop(0, count, pair_tile, 0)
+        pair_sum.begin()
+
+    small, middle_grad_ref, own_branch = r.small, r.middle_grad, r.own_branch
     tiles = width // LANES
-    for tile in range(tiles):
-        small[tiles + tile : tiles + tile + 1] = gain_grad[:, tile * LANES : (tile + 1) * LANES]
-    branch, own_branch = r.row, r.own_branch
-    own_branch[...] = middle_grad.astype(BF)
+
+    def finish_middle():
+        normed_two_grad = grads.total()
+        middle = middle_ref[...]
+        scale_two = scale_of(middle)
+        lifted = gain_two * normed_two_grad
+        middle_grad = (
+            grad_ref[...].astype(F32)
+            + scale_two * lifted
+            - middle * (scale_two * scale_two * scale_two)
+            * jnp.mean(middle * lifted, axis=-1, keepdims=True)
+        )
+        middle_grad_ref[...] = middle_grad
+        own_branch[...] = middle_grad.astype(BF)
+        small[...] = jnp.zeros_like(small)
+        gain_grad = jnp.sum(normed_two_grad * middle * scale_two, axis=0, keepdims=True)
+        for tile in range(tiles):
+            small[tiles + tile : tiles + tile + 1] = gain_grad[:, tile * LANES : (tile + 1) * LANES]
+
+    def finish_out():
+        r.block_out[...] = (middle_ref[...] + outs.total()).astype(BF)
+
+    branch = r.row
     branches = RingGather(
         spot,
         own_branch,
@@ -695,16 +703,17 @@
     def attend_back(origin):
         mine = row_block(origin, rows)
         window = strip_window(origin, rows, length)
-        mixed_grad = dot_cols(branch[origin], own_out[...]).astype(BF)
+        mixed_grad = dot_cols(branch[origin], own_out[...])
         for head in range(heads):
             columns = slice(head * depth, (head + 1) * depth)
             key = qkv[:, inner + head * depth : inner + (head + 1) * depth]
             value = qkv[:, 2 * inner + head * depth : 2 * inner + (head + 1) * depth]
-            grad = mixed_grad[:, columns]
+            share = r.shares[head, mine]
+            grad = (mixed_grad[:, columns] * share).astype(BF)
             weight_low = weights[head, mine]
             weight = weight_low.astype(F32)
             scaled = weight * dot_cols(grad, value)
-            score_grad = scaled - weight * jnp.sum(scaled, axis=1, keepdims=True)
+            score_grad = scaled - weight * (share * jnp.sum(scaled, axis=1, keepdims=True))
             strip[head, :, window] += score_grad
             score_low = score_grad.astype(BF)
             dqkv[mine, columns] = dot(score_low, key).astype(BF)
@@ -877,54 +886,74 @@
         gather.step(hop)
         gather.step_far(hop)
 
+    down_ready()
+    pair_ready()
+    back_half(1)
+    down_sum.step(0)
+    grads.over()
+    out_half(0)
+    down_sum.step(1)
+    finish_middle()
     branch_start()
+    down_sum.step(2)
     branches.step(0)
     attend_pair(0)
-    down_sum.step(1)
     branches.step(1)
     attend_pair(1)
-    down_sum.step(2)
-    branches.step(2)
+    pair_sum.step(0)
     finish_down()
     down.begin_far()
-    pair_sum.step(0)
+    down.step(0)
+    branches.step(2)
     attend_pair(2)
-    pass_round(down, 0)
+    down.step(1)
     pair_sum.step(1)
-    pass_round(down, 1)
+    down.step_far(0)
+    out_half(1)
     branches.step(3)
-    outs.over()
     attend_back(spot.at(spot.half))
     near = finish_heads()
+    far = heads_over()
+    outs.over()
+    down.step(2)
+    trade()
     finish_table()
-    trade()
-    pass_round(down, 2)
-    far = heads_over()
     pair_sum.step(2)
-    pass_round(down, 3)
+    finish_proj()
+    down.step_far(1)
+    down.step_far(2)
+    finish_pair()
+    down.step_far(3)
     finish_input()
-    finish_proj()
+    down.step(3)
+    proj.begin_far()
     small_send()
-    proj.begin_far()
     small_step()
-    finish_pair()
-    pass_round(proj, 0)
+    proj.step(0)
     pair.begin_far()
-    pass_round(proj, 1)
+    proj.step(1)
     small_step()
-    pass_round(pair, 0)
-    r.block_out[...] = (middle + outs.total()).astype(BF)
+    pair.step(0)
+    proj.step_far(0)
     down.step_far(4)
-    pass_round(proj, 2)
+    proj.step(2)
+    pair.step(1)
     small_step()
-    pass_round(pair, 1)
+    pair.step_far(0)
+    proj.step(3)
+    pair.step(2)
     small_step()
-    pass_round(proj, 3)
-    pass_round(pair, 2)
-    pass_round(pair, 3)
+    proj.step_far(1)
+    proj.step_far(2)
+    pair.step(3)
+    pair.step_far(1)
+    pair.step_far(2)
+    proj.step_far(3)
+    finish_out()
+    proj.step_far(4)
+    pair.step_far(3)
+    pair.step_far(4)
     small_step()
-    proj.step_far(4)
-    pair.step_far(4)
     r.small_sum[...] = small[...]
     for name in ("down_own", "pair_own", "proj_own"):
         loads[name].wait()
@@ -936,7 +965,7 @@
         item.finish()
 
 
-SHARES = (95, 35, 95)
+SHARES = (95, 40, 90)
 SPLITS = (1, 1)
 
 
@@ -999,6 +1028,7 @@
         normed=vm((length, width), BF),
         qkv=vm((length, 3 * inner), BF),
         weights=vm((heads, length, length), BF),
+        shares=vm((heads, length, 1), F32),
         mixed_heads=vm((length, inner), BF),
         mixed=vm((rows, width), BF),
         qkv_w=vm((width, 3 * inner), BF),

time: 248 us -> 248 us (level)
  no operation moved by 1% of the time
where the time goes in v6:
time: 248 us; the launch traced here: 247 us
  Pallas kernels  246 us (99%)
    pallas_call x1, Pallas kernels, layer(): pl.pallas_call(body, name='layer', out_shape=tuple((value[0] for value in...  219 us
    pallas_call x1, Pallas kernels, widen(): pl.pallas_call(functools.partial(widen_body, ff), name='widen', grid=(cou...  27 us

profile of v6, /device:TPU:0, one launch (start us, length us, event | category | flops | bytes accessed | tf_op | source)
XLA Modules:
  0.0 247.0 jit_solution(2275109925018723945)
XLA Ops:
  0.6 219.1 %layer.1 = (bf16[128,1024]{1,0:T(8,128)(2,1)}, f32[128,1024]{1,0:T(8,128)}, f32[32,128]{1,0:T(8,128)}, bf16[4,8,704,128]{3,2,1,0:T(8,128)(2,1)}, bf16[4,8,1408,1...) custom-call(bf16[128,1024]{1,0:T(8,128)(2,1)} %bitcast.13, bf16[128,1024]{1,0:T(8,128)(2,1)} %bitcast.14, ...), custom_call_target="tpu_custom_call" | custom-call | tf_op jit(solution)/shard_map/layer/pallas_call | solution.py:1078
  219.8 27.0 %widen.1 = (f32[2816,1024]{1,0:T(8,128)}, f32[1024,2816]{1,0:T(8,128)}, f32[1024,2816]{1,0:T(8,128)}, f32[1024,1024]{1,0:T(8,128)}, f32[1024,1024]{1,0:T(8,128)}...) custom-call(bf16[4,8,704,128]{3,2,1,0:T(8,128)(2,1)} %get-tuple-elem, ...), custom_call_target="tpu_custom_call" | custom-call | tf_op jit(solution)/shard_map/widen/pallas_call | solution.py:1158
